TPU v7x, 32 devices: a whole 2x2x4 slice. The times are simulated.
32 devices in a mesh: shard: 4 (over x, core), rep: 8 (over z, y).
Axes of the slice: x: 2, y: 2, z: 4, core: 2. Of those that a mesh axis runs over, the one named last changes fastest.
Arguments:
- tokens: bfloat16 [32, 1024, 1536], P(('shard', 'rep')), may hold values from -6 to 6
- norm_gain: bfloat16 [1536], P('shard'), may hold values from 0.5 to 1.5
- in_weight: bfloat16 [1536, 6448], P('shard'), may hold values from -0.15625 to 0.15625
- conv_weight: bfloat16 [4, 3328], P(None, 'shard'), may hold values from -0.5 to 0.5
- conv_bias: bfloat16 [3328], P('shard'), may hold values from -0.5 to 0.5
- dt_bias: bfloat16 [48], P('shard'), may hold values from -4 to -1
- a_log: bfloat16 [48], P('shard'), may hold values from -4 to 1.5
- skip: bfloat16 [48], P('shard'), may hold values from 0.5 to 1.5
- gate_gain: bfloat16 [3072], P('shard'), may hold values from 0.5 to 1.5
- out_weight: bfloat16 [3072, 1536], P('shard'), may hold values from -0.109375 to 0.109375
- cotangent: bfloat16 [32, 1024, 1536], P(('shard', 'rep')), may hold values from -6 to 6
Outputs:
- output: bfloat16 [32, 1024, 1536], P(('shard', 'rep'))
- input_grad: float32 [32, 1024, 1536], P(('shard', 'rep'))
- norm_gain_grad: float32 [1536], P('shard')
- in_weight_grad: float32 [1536, 6448], P('shard')
- conv_weight_grad: float32 [4, 3328], P(None, 'shard')
- conv_bias_grad: float32 [3328], P('shard')
- dt_bias_grad: float32 [48], P('shard')
- a_log_grad: float32 [48], P('shard')
- skip_grad: float32 [48], P('shard')
- gate_gain_grad: float32 [3072], P('shard')
- out_weight_grad: float32 [3072, 1536], P('shard')
All inputs are finite; a program needn't handle non-finite values.
Results may differ from a plain program's by a relative error of at most 0.0077.
Values may be sent and summed in bfloat16 or wider, within the bound.
No kernel may reach another device: no remote copies, remote signals or barrier semaphores. Data moves between devices by JAX's collectives and lax.ppermute only.
A program may use at most 448 MiB of HBM per device.

v0:
```python
import jax
import jax.numpy as jnp
from jax import lax
from jax.sharding import PartitionSpec as P

STRETCH = 256


epsilon = 1e-05


def rms_scale(values, gain):
    return values * lax.rsqrt(jnp.mean(values * values, axis=-1, keepdims=True) + epsilon) * gain


def stretch_step(state, values, keys_b, keys_c, steps, decay_rate):
    logs = jnp.cumsum(steps * decay_rate, axis=0)
    span = logs.shape[0]
    rows = lax.broadcasted_iota(jnp.int32, (span, span), 0)
    cols = lax.broadcasted_iota(jnp.int32, (span, span), 1)
    causal = (rows >= cols)[None, :, :]
    logs_heads = logs.T
    gaps = logs_heads[:, :, None] - logs_heads[:, None, :]
    weights = jnp.where(causal, jnp.exp(jnp.where(causal, gaps, 0.0)), 0.0)
    inner = jnp.dot(keys_c, keys_b.T, precision=lax.Precision.HIGHEST)
    mixing = inner[None, :, :] * weights * steps.T[:, None, :]
    local = jnp.einsum("hts,shp->thp", mixing, values, precision=lax.Precision.HIGHEST)
    carried = (
        jnp.einsum("hpn,tn->thp", state, keys_c, precision=lax.Precision.HIGHEST)
        * jnp.exp(logs)[:, :, None]
    )
    last = logs[-1]
    tails = jnp.exp(last[None, :] - logs) * steps
    scaled = values * tails[:, :, None]
    fresh = jnp.einsum("shp,sn->hpn", scaled, keys_b, precision=lax.Precision.HIGHEST)
    new_state = jnp.exp(last)[:, None, None] * state + fresh
    return (new_state, (local + carried).reshape(span, -1))


def mixer(proj, conv_weight, conv_bias, dt_bias, a_log, skip, gate_gain):
    length = proj.shape[0]
    inner_width = gate_gain.shape[0]
    state_size = (conv_bias.shape[0] - inner_width) // 2
    heads = dt_bias.shape[0]
    head_width = inner_width // heads
    taps = conv_weight.shape[0]
    gate = proj[:, :inner_width]
    conv_in = proj[:, inner_width : 2 * inner_width + 2 * state_size]
    raw_steps = proj[:, 2 * inner_width + 2 * state_size :]
    padded = jnp.pad(conv_in, ((taps - 1, 0), (0, 0)))
    conv_sum = jnp.zeros_like(conv_in) + conv_bias
    for offset in range(taps):
        conv_sum = conv_sum + conv_weight[offset] * padded[offset : offset + length]
    act = jax.nn.silu(conv_sum)
    values = act[:, :inner_width]
    keys_b = act[:, inner_width : inner_width + state_size]
    keys_c = act[:, inner_width + state_size :]
    steps = jax.nn.softplus(raw_steps + dt_bias)
    decay_rate = -jnp.exp(a_log)
    blocks = length // STRETCH

    def advance(state, block_values, block_b, block_c, block_steps):
        return stretch_step(
            state,
            block_values.reshape(STRETCH, heads, head_width),
            block_b,
            block_c,
            block_steps,
            decay_rate,
        )

    stepper = jax.checkpoint(advance)
    state = jnp.zeros((heads, head_width, state_size), jnp.float32)
    outputs = []
    for index in range(blocks):
        lower = index * STRETCH
        state, piece = stepper(
            state,
            values[lower : lower + STRETCH],
            keys_b[lower : lower + STRETCH],
            keys_c[lower : lower + STRETCH],
            steps[lower : lower + STRETCH],
        )
        outputs.append(piece)
    scan_flat = jnp.concatenate(outputs, axis=0)
    skip_cols = jnp.repeat(skip, head_width)
    scan_out = scan_flat + skip_cols[None, :] * values
    gated = scan_out * jax.nn.silu(gate)
    return rms_scale(gated, gate_gain)


def on_device(
    tokens,
    norm_gain,
    in_weight,
    conv_weight,
    conv_bias,
    dt_bias,
    a_log,
    skip,
    gate_gain,
    out_weight,
    cotangent,
):
    whole = (
        lax.all_gather(norm_gain, "shard", axis=0, tiled=True),
        lax.all_gather(in_weight, "shard", axis=0, tiled=True),
        lax.all_gather(conv_weight, "shard", axis=1, tiled=True),
        lax.all_gather(conv_bias, "shard", axis=0, tiled=True),
        lax.all_gather(dt_bias, "shard", axis=0, tiled=True),
        lax.all_gather(a_log, "shard", axis=0, tiled=True),
        lax.all_gather(skip, "shard", axis=0, tiled=True),
        lax.all_gather(gate_gain, "shard", axis=0, tiled=True),
        lax.all_gather(out_weight, "shard", axis=0, tiled=True),
    )
    (
        gain_full,
        in_full,
        conv_w_full,
        conv_b_full,
        dt_full,
        alog_full,
        skip_full,
        gate_full,
        out_full,
    ) = whole
    small = tuple(
        (
            item.astype(jnp.float32)
            for item in (conv_w_full, conv_b_full, dt_full, alog_full, skip_full, gate_full)
        )
    )
    seqs, length, width = tokens.shape
    total_rows = seqs * length
    flat = tokens.reshape(total_rows, width).astype(jnp.float32)
    normed_f, norm_pull = jax.vjp(rms_scale, flat, gain_full.astype(jnp.float32))
    normed = normed_f.astype(jnp.bfloat16)
    proj = jnp.dot(normed, in_full, preferred_element_type=jnp.float32)

    def mix_all(proj_rows, conv_w, conv_b, dt_b, alog_v, skip_v, gate_g):
        shaped = proj_rows.reshape(seqs, length, proj_rows.shape[1])
        mixed_rows = jax.vmap(mixer, in_axes=(0, None, None, None, None, None, None))(
            shaped, conv_w, conv_b, dt_b, alog_v, skip_v, gate_g
        )
        return mixed_rows.reshape(total_rows, mixed_rows.shape[2])

    mixed_f, mix_pull = jax.vjp(mix_all, proj, *small)
    mixed = mixed_f.astype(jnp.bfloat16)
    branch_out = jnp.dot(mixed, out_full, preferred_element_type=jnp.float32)
    output = (flat + branch_out).astype(jnp.bfloat16).reshape(seqs, length, width)
    in_back, out_back = (
        lax.all_gather(in_weight, "shard", axis=0, tiled=True),
        lax.all_gather(out_weight, "shard", axis=0, tiled=True),
    )
    cot_rows = cotangent.reshape(total_rows, width)
    mixed_grad = lax.dot_general(
        cot_rows, out_back, (((1,), (1,)), ((), ())), preferred_element_type=jnp.float32
    )
    mix_grads = mix_pull(mixed_grad)
    proj_grad = mix_grads[0].astype(jnp.bfloat16)
    normed_grad = lax.dot_general(
        proj_grad, in_back, (((1,), (1,)), ((), ())), preferred_element_type=jnp.float32
    )
    flat_grad, gain_grad = norm_pull(normed_grad)
    input_grad = (cot_rows.astype(jnp.float32) + flat_grad).reshape(seqs, length, width)
    out_grad = lax.dot_general(
        mixed, cot_rows, (((0,), (0,)), ((), ())), preferred_element_type=jnp.float32
    )
    in_grad = lax.dot_general(
        normed, proj_grad, (((0,), (0,)), ((), ())), preferred_element_type=jnp.float32
    )
    owned = (
        lax.psum_scatter(gain_grad, "shard", scatter_dimension=0, tiled=True),
        lax.psum_scatter(in_grad, "shard", scatter_dimension=0, tiled=True),
        lax.psum_scatter(mix_grads[1], "shard", scatter_dimension=1, tiled=True),
        lax.psum_scatter(mix_grads[2], "shard", scatter_dimension=0, tiled=True),
        lax.psum_scatter(mix_grads[3], "shard", scatter_dimension=0, tiled=True),
        lax.psum_scatter(mix_grads[4], "shard", scatter_dimension=0, tiled=True),
        lax.psum_scatter(mix_grads[5], "shard", scatter_dimension=0, tiled=True),
        lax.psum_scatter(mix_grads[6], "shard", scatter_dimension=0, tiled=True),
        lax.psum_scatter(out_grad, "shard", scatter_dimension=0, tiled=True),
    )
    summed = lax.psum(
        (owned[0], owned[1], owned[2], owned[3], owned[4], owned[5], owned[6], owned[7], owned[8]),
        "rep",
    )
    return (
        output,
        input_grad,
        summed[0],
        summed[1],
        summed[2],
        summed[3],
        summed[4],
        summed[5],
        summed[6],
        summed[7],
        summed[8],
    )


def solution(mesh):
    placed = (
        P(("shard", "rep"), None, None),
        P("shard"),
        P("shard", None),
        P(None, "shard"),
        P("shard"),
        P("shard"),
        P("shard"),
        P("shard"),
        P("shard"),
        P("shard", None),
        P(("shard", "rep"), None, None),
    )
    return jax.shard_map(
        on_device,
        mesh=mesh,
        in_specs=placed,
        out_specs=(
            P(("shard", "rep"), None, None),
            P(("shard", "rep"), None, None),
            P("shard"),
            P("shard", None),
            P(None, "shard"),
            P("shard"),
            P("shard"),
            P("shard"),
            P("shard"),
            P("shard"),
            P("shard", None),
        ),
        check_vma=False,
    )
```

profile of v0, /device:TPU:0, one launch (start us, length us, event | category | flops | bytes accessed | tf_op | source)
XLA Modules:
  0.0 1887.0 jit_solution(5279300305673587679)
XLA Ops:
  43.6 94.0 %all-gather.6.cloned.1.call-done = bf16[1536,6448]{0,1:T(8,128)(2,1)} async-done(((bf16[384,6448]{0,1:T(8,128)(2,1)}), bf16[1536,6448]{0,1:T(8,128)(2,1)}) %all-gather.6.cloned.1.call-update) | async-done | bytes 19808272 | tf_op jit(solution)/shard_map/all_gather | solution.py:107
  137.6 29.3 %convolution_bitcast_fusion = f32[1,1024,6448]{2,1,0:T(8,128)} fusion(bf16[1536,6448]{0,1:T(8,128)(2,1)} %all-gather.6.cloned.1.call-done, bf16[1,1024,1536]{2,1,0:T(8,128)(2,1)S(1)} %copy-done.29, f32[1536]{0:T(1024)S(1)} %reshape.1986, f32[1024]{0:T(1024)S(1)} %fusion.294), kind=kOutput, calls=%fused_computation.4 | convolution fusion | flops 20289945600 | bytes 49375232 | tf_op jit(solution)/shard_map/dot_general | solution.py:138
  200.3 24.7 %fusion.2 = (f32[1,1024,3328]{2,1,0:T(8,128)S(1)}, f32[1,1024,3328]{2,1,0:T(8,128)}) fusion(f32[1,1024,3328]{2,1,0:T(8,128)} %slice.245, f32[3328]{0:T(1024)} %get-tuple-element.111, f32[3328]{0:T(1024)} %get-tuple-element.112, f32[3328]{0:T(1024)} %get-tuple-element.113, f32[3328]{0:T(1024)} %get-tuple-element.110, f32[3328]{0:T(1024)} %convert_element_type.62), kind=kLoop, calls=%fused_computation.15 | loop fusion | flops 40894464 | bytes 40961024 | tf_op jit(solution)/shard_map/jvp(vmap(jit(silu)))/mul | solution.py:54
  231.8 15.5 fusion.336
  280.0 17.2 bitcast_add_fusion.6
  324.5 16.2 bitcast_add_fusion.3
  352.8 17.0 bitcast_add_fusion.4
  382.3 17.1 bitcast_add_fusion.5
  403.0 18.6 multiply_reduce_fusion.13
  423.9 17.4 fusion.139
  441.2 19.8 %fusion.6 = (f32[3072]{0:T(1024)}, f32[1024]{0:T(1024)S(1)}, f32[1024,3072]{1,0:T(8,128)}) fusion(f32[1,1024,3072]{2,1,0:T(8,128)} %get-tuple-element.145, f32[1024]{0:T(1024)S(1)} %fusion.295, f32[3072]{0:T(1024)S(1)} %bitcast.1060, bf16[3072,1536]{1,0:T(8,128)(2,1)} %all-gather.8.cloned.1.call-done, bf16[1,1024,1536]{2,1,0:T(8,128)(2,1)} %param.21), kind=kOutput, calls=%fused_computation.24 | convolution fusion | flops 9682546688 | bytes 37781504 | tf_op jit(solution)/shard_map/dot_general | solution.py:156
  461.1 32.2 %multiply_reduce_fusion.4 = (f32[3072]{0:T(1024)}, f32[1,1024,3072]{2,1,0:T(8,128)}, f32[1,1024,3072]{2,1,0:T(8,128)}) fusion(f32[1,1024,3328]{2,1,0:T(8,128)} %copy-done, f32[1,1024,6448]{2,1,0:T(8,128)} %convolution_bitcast_fusion, f32[1,1024,3072]{2,1,0:T(8,128)} %get-tuple-element.145, f32[1024]{0:T(1024)S(1)} %multiply_multiply_fusion.1, ...), kind=kLoop, calls=%fused_computation.27 | loop fusion | flops 75494400 | bytes 88125440 | tf_op jit(solution)/shard_map/transpose(jvp(vmap()))/reduce_sum | solution.py:87
  735.0 46.2 %fusion.65 = (f32[48,256]{1,0:T(8,128)S(1)}, f32[48,256]{1,0:T(8,128)S(1)}, f32[48,256]{1,0:T(8,128)}, f32[256,256]{1,0:T(8,128)}, f32[256,256]{1,0:T(8,128)}, /...) fusion(f32[48,256]{1,0:T(8,128)S(1)} %copy-done.105, ...), kind=kOutput, calls=%fused_computation.108 | convolution fusion | flops 2604253184 | bytes 47185920 | tf_op jit(solution)/shard_map/transpose(jvp(vmap(jvp(vmap()))))/checkpoint/hts,shp->thp/dot_general | solution.py:27
  801.8 14.1 bitcast_add_fusion.2
  835.4 14.0 bitcast_add_fusion.1
  1003.3 36.0 %multiply_reduce_fusion.2 = (f32[3328]{0:T(1024)S(1)}, f32[3328]{0:T(1024)S(1)}, f32[3328]{0:T(1024)S(1)}, f32[3328]{0:T(1024)}, f32[3328]{0:T(1024)S(1)}, /*index=5*/f32[1,1024,3328]{2,1,0:T(8,128)}) fusion(f32[1,1024,3328]{2,1,0:T(8,128)} %slice.245, f32[1,1024,6448]{2,1,0:T(8,128)} %convolution_bitcast_fusion, f32[1,1024,3328]{2,1,0:T(8,128)} %get-tuple-element.153, ...), kind=kLoop, calls=%fused_computation.12 | loop fusion | flops 68140800 | bytes 68224000 | tf_op jit(solution)/shard_map/transpose(jvp(vmap()))/reduce_sum | solution.py:53
  1039.3 17.1 broadcast_multiply_fusion
  1056.4 19.7 %pad_add_fusion = f32[1,1024,3328]{2,1,0:T(8,128)} fusion(f32[1,1024,3328]{2,1,0:T(8,128)} %get-tuple-element.156, f32[1,1024,3328]{2,1,0:T(8,128)} %get-tuple-element.157, f32[1,1024,3328]{2,1,0:T(8,128)} %get-tuple-element.158, f32[1,1024,3328]{2,1,0:T(8,128)S(1)} %get-tuple-element.155), kind=kLoop, calls=%fused_computation.7 | loop fusion | flops 10223616 | bytes 68157440 | tf_op jit(solution)/shard_map/transpose(jvp(vmap()))/add_any | solution.py:53
  1076.1 33.3 %fusion.133 = f32[1536,6448]{0,1:T(8,128)} fusion(bf16[1,1024,1536]{2,1,0:T(8,128)(2,1)S(1)} %copy-done.30, f32[1536]{0:T(1024)S(1)} %copy-done.125, f32[1024]{0:T(1024)S(1)} %copy-done.129, f32[1,1024,3072]{2,1,0:T(8,128)} %get-tuple-element.154, f32[1,1024,3328]{2,1,0:T(8,128)} %pad_add_fusion, f32[1,1024,48]{2,1,0:T(8,128)} %get-tuple-element.136), kind=kOutput, calls=%fused_computation.176 | convolution fusion | flops 20309753856 | bytes 69183488 | tf_op jit(solution)/shard_map/dot_general | solution.py:169
  1111.4 267.3 %reduce-scatter.6.cloned.1.call-done = f32[384,6448]{0,1:T(8,128)} async-done(((f32[1536,6448]{0,1:T(8,128)}), f32[384,6448]{0,1:T(8,128)}) %reduce-scatter.6.cloned.1.call-update) | async-done | bytes 9904144 | tf_op jit(solution)/shard_map/reduce_scatter | solution.py:174
  1381.7 33.0 %fusion.73 = (f32[1536]{0:T(1024)S(1)}, f32[1024]{0:T(1024)S(1)}, f32[1024,1536]{1,0:T(8,128)}) fusion(bf16[1,1024,1536]{2,1,0:T(8,128)(2,1)S(1)} %copy-done.30, f32[1024]{0:T(1024)S(1)} %copy-done.129, f32[1536]{0:T(1024)S(1)} %copy-done.125, bf16[1536,6448]{0,1:T(8,128)(2,1)} %all-gather.6.cloned.1.call-done, f32[1,1024,3072]{2,1,0:T(8,128)} %get-tuple-element.154, ...), kind=kOutput, calls=%fused_computation.116 | convolution fusion | flops 20314468352 | bytes 55676928 | tf_op jit(solution)/shard_map/dot_general | solution.py:161
  1432.7 17.1 fusion.131
  1451.0 40.0 %all-reduce.44 = (f32[384]{0:T(512)}, f32[4,832]{1,0:T(4,128)}, f32[832]{0:T(1024)}, f32[12]{0:T(128)}, f32[12]{0:T(128)}, /*index=5*/f32[12]{0:T(128)}, f32[768]{0:T(1024)}) all-reduce(f32[384]{0:T(512)S(1)} %dynamic-slice.5, f32[4,832]{1,0:T(4,128)S(1)} %copy.695, ...), channel_id=1, replica_groups=mesh['shard'=4,'rep'=8] {'rep'}, use_global_device_ids=true, to_apply=%region_59.60 | all-reduce | flops 5348 | bytes 42784 | tf_op jit(solution)/shard_map/psum | solution.py:183
  1491.1 378.1 %all-reduce.50.cloned.1.call-done = (f32[384,6448]{0,1:T(8,128)}, f32[768,1536]{1,0:T(8,128)}) async-done(((f32[384,6448]{0,1:T(8,128)}, f32[768,1536]{1,0:T(8,128)}), (f32[384,6448]{0,1:T(8,128)}, f32[768,1536]{1,0:T(8,128)})) %all-reduce.50.cloned.1.call-update) | async-done | bytes 14622736 | tf_op jit(solution)/shard_map/psum | solution.py:183
  (655 shorter events, 631.5 us)
Async XLA Ops:
  7.2 130.3 %all-gather.6.cloned.1.call-start = ((), (), s32[]{:S(2)}) async-start(), calls=%async_computation.3 | async-start | bytes 24760320 | tf_op jit(solution)/shard_map/all_gather | solution.py:107
  8.0 433.3 %all-gather.8.cloned.1.call-start = ((), (), s32[]{:S(2)}) async-start(), calls=%async_computation.4 | async-start | bytes 11796480 | tf_op jit(solution)/shard_map/all_gather | solution.py:114
  8.7 1102.7 %reduce-scatter.8.cloned.1.call-start = ((), (), s32[]{:S(2)}) async-start(), calls=%async_computation.6 | async-start | bytes 23592960 | tf_op jit(solution)/shard_map/reduce_scatter | solution.py:181
  14.7 152.2 %copy-start.128 = (f32[1024]{0:T(1024)}, f32[1024]{0:T(1024)S(1)}, u32[]{:S(2)}) copy-start(f32[1024]{0:T(1024)S(1)} %fusion.294) | copy-start | bytes 12292
  20.9 146.1 %copy-start.124 = (f32[1536]{0:T(1024)}, f32[1536]{0:T(1024)S(1)}, u32[]{:S(2)}) copy-start(f32[1536]{0:T(1024)S(1)} %reshape.1986) | copy-start | bytes 18436
  29.9 138.4 %copy-start.119 = (f32[48]{0:T(128)}, f32[48]{0:T(128)S(1)}, u32[]{:S(2)}) copy-start(f32[48]{0:T(128)S(1)} %fusion.296) | copy-start | bytes 580
  29.9 137.0 %copy-start.134 = (f32[48]{0:T(128)}, f32[48]{0:T(128)S(1)}, u32[]{:S(2)}) copy-start(f32[48]{0:T(128)S(1)} %convert_element_type.66) | copy-start | bytes 580
  310.8 321.0 %copy-start.1 = (f32[48,64,128]{2,1,0:T(8,128)}, f32[48,64,128]{2,1,0:T(8,128)S(1)}, u32[]{:S(2)}) copy-start(f32[48,64,128]{2,1,0:T(8,128)S(1)} %convolution_add_fusion) | copy-start | bytes 4718596
  316.0 296.6 %copy-start.3 = (f32[48,64,128]{2,1,0:T(8,128)}, f32[48,64,128]{2,1,0:T(8,128)S(1)}, u32[]{:S(2)}) copy-start(f32[48,64,128]{2,1,0:T(8,128)S(1)} %multiply_add_fusion.2) | copy-start | bytes 4718596
  423.8 100.8 %copy-start.44 = (f32[1,256,128]{2,1,0:T(8,128)}, f32[1,256,128]{2,1,0:T(8,128)S(1)}, u32[]{:S(2)}) copy-start(f32[1,256,128]{2,1,0:T(8,128)S(1)} %get-tuple-element.42) | copy-start | bytes 393220
  423.8 131.6 %copy-start.41 = (f32[1,256,128]{2,1,0:T(8,128)}, f32[1,256,128]{2,1,0:T(8,128)S(1)}, u32[]{:S(2)}) copy-start(f32[1,256,128]{2,1,0:T(8,128)S(1)} %get-tuple-element.54) | copy-start | bytes 393220
  601.5 777.3 %reduce-scatter.6.cloned.1.call-start = ((), (), s32[]{:S(2)}) async-start(), calls=%async_computation.5 | async-start | bytes 49520640 | tf_op jit(solution)/shard_map/reduce_scatter | solution.py:174
  734.9 46.3 %copy-start.20 = (f32[48,64,128]{2,1,0:T(8,128)S(1)}, f32[48,64,128]{2,1,0:T(8,128)}, u32[]{:S(2)}) copy-start(f32[48,64,128]{2,1,0:T(8,128)} %copy-done.19) | copy-start | bytes 4718596
  734.9 46.3 %copy-start.45 = (f32[1,256,128]{2,1,0:T(8,128)S(1)}, f32[1,256,128]{2,1,0:T(8,128)}, u32[]{:S(2)}) copy-start(f32[1,256,128]{2,1,0:T(8,128)} %copy-done.44) | copy-start | bytes 393220
  734.9 49.0 %copy-start.71 = (f32[1,256,48]{1,0,2:T(1,128)S(1)}, f32[1,256,48]{1,0,2:T(1,128)}, u32[]{:S(2)}) copy-start(f32[1,256,48]{1,0,2:T(1,128)} %copy-done.70) | copy-start | bytes 147460
  734.9 59.5 %copy-start.51 = (f32[1,48,256]{1,2,0:T(8,128)S(1)}, f32[1,48,256]{1,2,0:T(8,128)}, u32[]{:S(2)}) copy-start(f32[1,48,256]{1,2,0:T(8,128)} %copy-done.50) | copy-start | bytes 147460
  734.9 59.5 %copy-start.37 = (f32[1,256,48]{2,1,0:T(8,128)S(1)}, f32[1,256,48]{2,1,0:T(8,128)}, u32[]{:S(2)}) copy-start(f32[1,256,48]{2,1,0:T(8,128)} %get-tuple-element.49) | copy-start | bytes 147460
  734.9 60.5 %copy-start.4 = (f32[48,64,128]{2,1,0:T(8,128)S(1)}, f32[48,64,128]{2,1,0:T(8,128)}, u32[]{:S(2)}) copy-start(f32[48,64,128]{2,1,0:T(8,128)} %copy-done.3) | copy-start | bytes 4718596
  1109.4 272.0 %copy-start.118 = (f32[3072]{0:T(1024)S(1)}, f32[3072]{0:T(1024)}, u32[]{:S(2)}) copy-start(f32[3072]{0:T(1024)} %get-tuple-element.133) | copy-start | bytes 36868
  1109.4 272.2 %copy-start.138 = (f32[48]{0:T(128)S(1)}, f32[48]{0:T(128)}, u32[]{:S(2)}) copy-start(f32[48]{0:T(128)} %get-tuple-element.201) | copy-start | bytes 580
  1109.4 272.2 %copy-start.139 = (f32[48]{0:T(128)S(1)}, f32[48]{0:T(128)}, u32[]{:S(2)}) copy-start(f32[48]{0:T(128)} %get-tuple-element.199) | copy-start | bytes 580
  1109.4 272.2 %copy-start.141 = (bf16[48]{0:T(256)(128)(2,1)S(1)}, bf16[48]{0:T(256)(128)(2,1)}, u32[]{:S(2)}) copy-start(bf16[48]{0:T(256)(128)(2,1)} %copy-done.140) | copy-start | bytes 292
  1109.4 340.4 %reduce-scatter.10.cloned.1.call-start = ((), (), s32[]{:S(2)}) async-start(), calls=%async_computation.7 | async-start | bytes 2129920
  1111.4 757.8 %all-reduce.50.cloned.1.call-start = ((), (), s32[]{:S(2)}) async-start(), calls=%async_computation.8 | async-start | bytes 29245440 | tf_op jit(solution)/shard_map/psum | solution.py:183
  (130 other events, 2238.1 us)
Sparse Core Ops, SparseCore 0:
  9.6 127.9 all-gather.5
  139.1 64.2 all-gather.7
  601.6 137.8 reduce-scatter.7
  1109.5 269.2 reduce-scatter.5
  1381.8 28.7 reduce-scatter.9
  1414.8 454.3 all-reduce.49
where the time goes:
time: 1890 us
  waiting for transfers between devices  741 us (39%)
  matrix products  494 us (26%)
  local copies, waits for them, and re-layouts  285 us (15%)
  other arithmetic  271 us (14%)
  blocking collectives  76.2 us (4%)
  between operations  20.4 us (1%)
    psum x1, waiting for transfers between devices, on_device(): lax.psum((owned[0], owned[1], owned[2], owned[3], owned[4], owned[5], own...  378 us
    reduce_scatter x1, waiting for transfers between devices, on_device(): lax.psum_scatter(in_grad, 'shard', scatter_dimension=0, tiled=True)  267 us
    dot_general x12, matrix products, stretch_step(): jnp.einsum('hts,shp->thp', mixing, values, precision=lax.Precision.HIGHEST)  210 us
    all_gather x1, waiting for transfers between devices, on_device(): lax.all_gather(in_weight, 'shard', axis=0, tiled=True)  94 us
    dot_general x15, matrix products, stretch_step(): jnp.einsum('hpn,tn->thp', state, keys_c, precision=lax.Precision.HIGHEST)  71.9 us
    mul x24, local copies, waits for them, and re-layouts, stretch_step(): scaled = values * tails[:, :, None]  56.3 us
    dot_general x9, matrix products, stretch_step(): jnp.einsum('shp,sn->hpn', scaled, keys_b, precision=lax.Precision.HIGHEST)  48.5 us
    psum x1, blocking collectives, on_device(): lax.psum((owned[0], owned[1], owned[2], owned[3], owned[4], owned[5], own...  40 us
  transfers between devices with their start and end apart: 6, of which 3 were waited for; matrix products, arithmetic and copies ran while one was open for 46% of the time, Pallas kernels for 0%

commit v1 on v0

v1 whole, which is shorter than its diff:
```python
import functools

import jax
import jax.numpy as jnp
from jax import lax
from jax.experimental import pallas as pl
from jax.experimental.pallas import tpu as pltpu
from jax.sharding import PartitionSpec as P

Q = 128
LANES = 128
HEAD = 64
EPS = 1e-05
F32 = jnp.float32
BF16 = jnp.bfloat16
HI = lax.Precision.HIGHEST
NEG = -1e30


def mm(a, b):
    return jnp.dot(a, b, preferred_element_type=F32)


def mm_t(a, b):
    return lax.dot_general(a, b, (((1,), (1,)), ((), ())), preferred_element_type=F32)


def softplus(v):
    return jnp.maximum(v, 0.0) + jnp.log1p(jnp.exp(-jnp.abs(v)))


def sigmoid(v):
    return 1.0 / (1.0 + jnp.exp(-v))


def tri_lower():
    rows = lax.broadcasted_iota(jnp.int32, (Q, Q), 0)
    cols = lax.broadcasted_iota(jnp.int32, (Q, Q), 1)
    return rows >= cols


def spread(table, lane):
    return jnp.broadcast_to(table[:, lane : lane + 1], (Q, LANES))


def fill_tables(dt, logs, dt_tab, log_tab, log_rows, low, groups, per):
    log_rows[...] = jnp.transpose(logs)
    for g in range(groups):
        shift = (LANES - (low + g) * per) % LANES
        dt_tab[g] = pltpu.roll(dt, shift, 1) if shift else dt
        log_tab[g] = pltpu.roll(logs, shift, 1) if shift else logs


def scan_forward(proj_ref, cw_ref, cb_ref, vec_ref, skip_ref, out_ref, sum_ref, start_ref,
                 shifted, act, state, dt_tab, log_tab, log_rows, *, inner, nstate, groups, per):
    first = pl.program_id(0) == 0
    conv = inner + 2 * nstate

    @pl.when(first)
    def _():
        shifted[0:8, :] = jnp.zeros((8, conv), F32)
        state[...] = jnp.zeros_like(state)

    shifted[8 : 8 + Q, :] = proj_ref[:, 0:conv]
    wide = 256
    for low in range(0, conv, wide):
        part = pl.ds(low, wide)
        total = cb_ref[0:1, part] + cw_ref[0:1, part] * shifted[5 : 5 + Q, part]
        for k in range(1, 4):
            total = total + cw_ref[k : k + 1, part] * shifted[5 + k : 5 + k + Q, part]
        sum_ref[:, part] = total
        act[:, part] = total * sigmoid(total)
    shifted[0:8, :] = shifted[Q : Q + 8, :]

    dt = softplus(proj_ref[:, conv : conv + LANES] + vec_ref[0:1, :])
    causal = tri_lower()
    logs = jnp.dot(causal.astype(F32), dt * vec_ref[1:2, :], precision=HI, preferred_element_type=F32)
    fill_tables(dt, logs, dt_tab, log_tab, log_rows, 0, groups, per)
    keys_b = act[:, inner : inner + nstate]
    keys_c = act[:, inner + nstate : conv].astype(BF16)
    b_cols = jnp.transpose(keys_b).astype(BF16)
    cross = mm(keys_c, b_cols)
    start_ref[...] = state[...].astype(BF16)
    span = per * HEAD
    low_half = lax.broadcasted_iota(jnp.int32, (Q, LANES), 1) < HEAD

    def group(g, carry):
        base = pl.multiple_of(g * span, span)
        dts, lgs = dt_tab[g], log_tab[g]
        carried = mm(keys_c, start_ref[:, pl.ds(base, span)])
        tails_all = []
        lasts = []
        for j in range(per // 2):
            cols = pl.ds(pl.multiple_of(base + j * LANES, LANES), LANES)
            h = g * per + 2 * j
            col0, col1 = spread(lgs, 2 * j), spread(lgs, 2 * j + 1)
            row0, row1 = log_rows[pl.ds(h, 1), :], log_rows[pl.ds(h + 1, 1), :]
            values = act[:, cols]
            stepped = (values * jnp.where(low_half, spread(dts, 2 * j), spread(dts, 2 * j + 1)))
            stepped_b = stepped.astype(BF16)
            mix0 = (jnp.exp(jnp.where(causal, col0 - row0, NEG)) * cross).astype(BF16)
            mix1 = (jnp.exp(jnp.where(causal, col1 - row1, NEG)) * cross).astype(BF16)
            zero = jnp.zeros_like(stepped_b)
            pairs = jnp.concatenate(
                [jnp.where(low_half, stepped_b, zero), jnp.where(low_half, zero, stepped_b)], axis=0)
            local = mm(jnp.concatenate([mix0, mix1], axis=1), pairs)
            both = jnp.where(low_half, col0, col1)
            last = both[Q - 1 : Q, :]
            out = local + carried[:, j * LANES : (j + 1) * LANES] * jnp.exp(both)
            out_ref[:, cols] = out + skip_ref[0:1, cols] * values
            tails_all.append((stepped * jnp.exp(last - both)).astype(BF16))
            lasts.append(jnp.exp(last))
        fresh = mm(b_cols, jnp.concatenate(tails_all, axis=1))
        cols = pl.ds(base, span)
        state[:, cols] = state[:, cols] * jnp.concatenate(lasts, axis=1) + fresh
        return carry

    lax.fori_loop(0, groups, group, 0)


def run_scan_forward(proj, cw, cb, vec, skip_cols, inner, nstate, groups, per):
    length = proj.shape[0]
    blocks = length // Q
    conv = inner + 2 * nstate
    whole = lambda shape: pl.BlockSpec(shape, lambda i: (0, 0))
    rows = lambda width: pl.BlockSpec((Q, width), lambda i: (i, 0))
    return pl.pallas_call(
        functools.partial(scan_forward, inner=inner, nstate=nstate, groups=groups, per=per),
        grid=(blocks,),
        in_specs=[rows(proj.shape[1]), whole(cw.shape), whole(cb.shape), whole(vec.shape), whole(skip_cols.shape)],
        out_specs=[rows(inner), rows(conv), pl.BlockSpec((nstate, inner), lambda i: (i, 0))],
        out_shape=[
            jax.ShapeDtypeStruct((length, inner), F32),
            jax.ShapeDtypeStruct((length, conv), F32),
            jax.ShapeDtypeStruct((blocks * nstate, inner), BF16),
        ],
        scratch_shapes=[
            pltpu.VMEM((Q + 8, conv), F32),
            pltpu.VMEM((Q, conv), F32),
            pltpu.VMEM((nstate, inner), F32),
            pltpu.VMEM((groups, Q, LANES), F32),
            pltpu.VMEM((groups, Q, LANES), F32),
            pltpu.VMEM((LANES, Q), F32),
        ],
        compiler_params=pltpu.CompilerParams(vmem_limit_bytes=60 << 20),
        cost_estimate=pl.CostEstimate(flops=12_000_000_000, bytes_accessed=60_000_000, transcendentals=20_000_000),
        name="scan_forward",
    )(proj, cw, cb, vec, skip_cols)


def piece_copies(place_ref, pieces, refs, target, sems):
    copies = []
    for index, (start, half, size, lane) in enumerate(pieces):
        rows, cols = refs[index].shape
        if half is not None:
            start = pl.multiple_of(start + jnp.bitwise_xor(place_ref[1], half) * size, 16)
        window = target.at[pl.ds(start, rows), pl.ds(lane, cols)]
        copies.append(pltpu.make_async_copy(refs[index], window, sems.at[index]))
    return copies


def load_pieces(*args):
    for copy in piece_copies(*args):
        copy.start()


def wait_pieces(*args):
    for copy in piece_copies(*args):
        copy.wait()


def columns_of(place_ref, position, order, width):
    return pl.ds(pl.multiple_of(jnp.bitwise_xor(place_ref[0], order[position]) * width, LANES), width)


def project_in(place_ref, tok_ref, gain_ref, *rest, pieces, order):
    refs, (normed_ref, proj_ref, weight, sems) = rest[: len(pieces)], rest[len(pieces) :]
    first = pl.program_id(0) == 0

    @pl.when(first)
    def _():
        load_pieces(place_ref, pieces, refs, weight, sems)

    width = tok_ref.shape[1] // len(order)
    tok = tok_ref[...].astype(F32)
    scale = lax.rsqrt(jnp.mean(tok * tok, axis=1, keepdims=True) + EPS)
    for position in range(len(order)):
        cols = columns_of(place_ref, position, order, width)
        value = tok_ref[:, cols].astype(F32) * scale * gain_ref[0:1, cols]
        normed_ref[:, position * width : (position + 1) * width] = value.astype(BF16)

    @pl.when(first)
    def _():
        wait_pieces(place_ref, pieces, refs, weight, sems)

    total = proj_ref.shape[1]
    step = 384
    for low in range(0, total, step):
        proj_ref[:, low : low + step] = mm_t(normed_ref[...], weight[low : low + step, :])


def grid_of(grid, in_specs, out_specs, scratch):
    return pltpu.PrefetchScalarGridSpec(
        num_scalar_prefetch=1, grid=grid, in_specs=in_specs, out_specs=out_specs, scratch_shapes=scratch)


def anywhere(count):
    return [pl.BlockSpec(memory_space=pl.ANY)] * count


def row_block(block, width):
    return pl.BlockSpec((block, width), lambda i, s: (i, 0))


def fixed(shape):
    return pl.BlockSpec(shape, lambda i, s: (0,) * len(shape))


def run_project_in(place, tok, gain, weight, total, order, block=256):
    pieces, arrays = weight
    length, width = tok.shape
    return pl.pallas_call(
        functools.partial(project_in, pieces=pieces, order=order),
        grid_spec=grid_of(
            (length // block,),
            [row_block(block, width), fixed(gain.shape)] + anywhere(len(pieces)),
            [row_block(block, width), row_block(block, total)],
            [pltpu.VMEM((total, width), BF16), pltpu.SemaphoreType.DMA((len(pieces),))],
        ),
        out_shape=[jax.ShapeDtypeStruct((length, width), BF16), jax.ShapeDtypeStruct((length, total), F32)],
        compiler_params=pltpu.CompilerParams(vmem_limit_bytes=50 << 20),
        cost_estimate=pl.CostEstimate(flops=20_000_000_000, bytes_accessed=30_000_000, transcendentals=1000),
        name="project_in",
    )(place, tok, gain, *arrays)


def gating(place_ref, normed_ref, cot_ref, scan_ref, gain_ref, *rest, wg_pieces, ow_pieces, order):
    n_g, n_o = len(wg_pieces), len(ow_pieces)
    wg_refs, ow_refs = rest[:n_g], rest[n_g : n_g + n_o]
    (mixed_ref, dscan_ref, dgate_ref, dgain_ref, wg, ow, gate_s, gated_s, scaled_s,
     g_sems, o_sems) = rest[n_g + n_o :]
    inner = wg.shape[0]
    parts = len(order)
    width = inner // parts
    first = pl.program_id(0) == 0

    @pl.when(first)
    def _():
        load_pieces(place_ref, wg_pieces, wg_refs, wg, g_sems)
        load_pieces(place_ref, ow_pieces, ow_refs, ow, o_sems)
        dgain_ref[...] = jnp.zeros_like(dgain_ref)
        wait_pieces(place_ref, wg_pieces, wg_refs, wg, g_sems)

    def fold(v):
        total = v[:, 0:LANES]
        for low in range(LANES, v.shape[1], LANES):
            total = total + v[:, low : low + LANES]
        return total

    power = None
    for p in range(parts):
        cols = slice(p * width, (p + 1) * width)
        gate = mm_t(normed_ref[...], wg[cols, :])
        gated = scan_ref[:, cols] * (gate * sigmoid(gate))
        gate_s[:, cols] = gate
        gated_s[:, cols] = gated
        term = fold(gated * gated)
        power = term if power is None else power + term
    scale = lax.rsqrt(jnp.sum(power, axis=1, keepdims=True) / inner + EPS)

    @pl.when(first)
    def _():
        wait_pieces(place_ref, ow_pieces, ow_refs, ow, o_sems)

    match = None
    for p in range(parts):
        true = columns_of(place_ref, p, order, width)
        rows = slice(p * width, (p + 1) * width)
        grad = mm_t(cot_ref[...], ow[rows, :])
        gated = gated_s[:, true]
        gain = gain_ref[0:1, true]
        unit = gated * scale
        mixed_ref[:, rows] = (unit * gain).astype(BF16)
        dgain_ref[0:1, true] += jnp.sum(grad * unit, axis=0, keepdims=True)
        scaled = grad * gain
        scaled_s[:, true] = scaled
        term = fold(scaled * gated)
        match = term if match is None else match + term
    pull = jnp.sum(match, axis=1, keepdims=True) * (scale * scale) / inner
    for p in range(parts):
        cols = slice(p * width, (p + 1) * width)
        gate = gate_s[:, cols]
        sig = sigmoid(gate)
        silu = gate * sig
        dgated = scale * (scaled_s[:, cols] - gated_s[:, cols] * pull)
        dscan_ref[:, cols] = dgated * silu
        dgate_ref[:, cols] = (dgated * scan_ref[:, cols] * (sig + silu * (1.0 - sig))).astype(BF16)


def run_gating(place, normed, gate_weight, out_weight, cot, scan_out, gain, order, block=256):
    wg_pieces, wg_arrays = gate_weight
    ow_pieces, ow_arrays = out_weight
    length, width = normed.shape
    inner = scan_out.shape[1]
    return pl.pallas_call(
        functools.partial(gating, wg_pieces=wg_pieces, ow_pieces=ow_pieces, order=order),
        grid_spec=grid_of(
            (length // block,),
            [row_block(block, width), row_block(block, width), row_block(block, inner), fixed((1, inner))]
            + anywhere(len(wg_pieces) + len(ow_pieces)),
            [row_block(block, inner), row_block(block, inner), row_block(block, inner), fixed((1, inner))],
            [pltpu.VMEM((inner, width), BF16), pltpu.VMEM((inner, width), BF16)]
            + [pltpu.VMEM((block, inner), F32)] * 3
            + [pltpu.SemaphoreType.DMA((len(wg_pieces),)), pltpu.SemaphoreType.DMA((len(ow_pieces),))],
        ),
        out_shape=[
            jax.ShapeDtypeStruct((length, inner), BF16),
            jax.ShapeDtypeStruct((length, inner), F32),
            jax.ShapeDtypeStruct((length, inner), BF16),
            jax.ShapeDtypeStruct((1, inner), F32),
        ],
        compiler_params=pltpu.CompilerParams(vmem_limit_bytes=62 << 20),
        cost_estimate=pl.CostEstimate(flops=40_000_000_000, bytes_accessed=70_000_000, transcendentals=10_000_000),
        name="gating",
    )(place, normed, cot, scan_out, gain, *wg_arrays, *ow_arrays)


def gate_back(place_ref, dgate_ref, *rest, pieces):
    refs, (grad_ref, weight, sems) = rest[: len(pieces)], rest[len(pieces) :]

    @pl.when(pl.program_id(0) == 0)
    def _():
        load_pieces(place_ref, pieces, refs, weight, sems)
        wait_pieces(place_ref, pieces, refs, weight, sems)

    step = 384
    for low in range(0, grad_ref.shape[1], step):
        grad_ref[:, low : low + step] = mm(dgate_ref[...], weight[:, low : low + step])


def run_gate_back(place, dgate, model, weight, block=256):
    pieces, arrays = weight
    length, inner = dgate.shape
    return pl.pallas_call(
        functools.partial(gate_back, pieces=pieces),
        grid_spec=grid_of(
            (length // block,),
            [row_block(block, inner)] + anywhere(len(pieces)),
            row_block(block, model),
            [pltpu.VMEM((inner, model), BF16), pltpu.SemaphoreType.DMA((len(pieces),))],
        ),
        out_shape=jax.ShapeDtypeStruct((length, model), F32),
        compiler_params=pltpu.CompilerParams(vmem_limit_bytes=40 << 20),
        cost_estimate=pl.CostEstimate(flops=16_000_000_000, bytes_accessed=22_000_000, transcendentals=0),
        name="gate_back",
    )(place, dgate, *arrays)


def input_back(place_ref, part_ref, tok_ref, cot_ref, gain_ref, *rest, count, pieces, order):
    dproj_refs, rest = rest[:count], rest[count:]
    refs, (grad_ref, dgain_ref, weight, dn, sems) = rest[: len(pieces)], rest[len(pieces) :]
    first = pl.program_id(0) == 0

    @pl.when(first)
    def _():
        load_pieces(place_ref, pieces, refs, weight, sems)
        dgain_ref[...] = jnp.zeros_like(dgain_ref)
        wait_pieces(place_ref, pieces, refs, weight, sems)

    model = tok_ref.shape[1]
    width = model // len(order)
    tok = tok_ref[...].astype(F32)
    scale = lax.rsqrt(jnp.mean(tok * tok, axis=1, keepdims=True) + EPS)
    match = None
    for position in range(len(order)):
        spot = slice(position * width, (position + 1) * width)
        true = columns_of(place_ref, position, order, width)
        grad, low = part_ref[:, spot], 0
        for ref in dproj_refs:
            grad = grad + mm(ref[...], weight[low : low + ref.shape[1], spot])
            low += ref.shape[1]
        value = tok_ref[:, true].astype(F32)
        dgain_ref[0:1, true] += jnp.sum(grad * (value * scale), axis=0, keepdims=True)
        grad = grad * gain_ref[0:1, true]
        dn[:, spot] = grad
        term = jnp.sum(grad * value, axis=1, keepdims=True)
        match = term if match is None else match + term
    pull = match * (scale * scale * scale) / model
    for position in range(len(order)):
        spot = slice(position * width, (position + 1) * width)
        true = columns_of(place_ref, position, order, width)
        value = tok_ref[:, true].astype(F32)
        grad_ref[:, true] = cot_ref[:, true].astype(F32) + (scale * dn[:, spot] - value * pull)


def run_input_back(place, part, dprojs, tok, cot, gain, weight, order, block=256):
    pieces, arrays = weight
    length, model = tok.shape
    widths = [d.shape[1] for d in dprojs]
    return pl.pallas_call(
        functools.partial(input_back, count=len(dprojs), pieces=pieces, order=order),
        grid_spec=grid_of(
            (length // block,),
            [row_block(block, model), row_block(block, model), row_block(block, model), fixed((1, model))]
            + [row_block(block, w) for w in widths] + anywhere(len(pieces)),
            [row_block(block, model), fixed((1, model))],
            [pltpu.VMEM((sum(widths), model), BF16), pltpu.VMEM((block, model), F32),
             pltpu.SemaphoreType.DMA((len(pieces),))],
        ),
        out_shape=[jax.ShapeDtypeStruct((length, model), F32), jax.ShapeDtypeStruct((1, model), F32)],
        compiler_params=pltpu.CompilerParams(vmem_limit_bytes=50 << 20),
        cost_estimate=pl.CostEstimate(flops=22_000_000_000, bytes_accessed=46_000_000, transcendentals=1000),
        name="input_back",
    )(place, part, tok, cot, gain, *dprojs, *arrays)


def project_out(place_ref, mixed_ref, tok_ref, *rest, pieces):
    refs, (out_ref, weight, sems) = rest[: len(pieces)], rest[len(pieces) :]

    @pl.when(pl.program_id(0) == 0)
    def _():
        load_pieces(place_ref, pieces, refs, weight, sems)
        wait_pieces(place_ref, pieces, refs, weight, sems)

    step = 384
    for low in range(0, out_ref.shape[1], step):
        cols = slice(low, low + step)
        out_ref[:, cols] = (tok_ref[:, cols].astype(F32) + mm(mixed_ref[...], weight[:, cols])).astype(BF16)


def run_project_out(place, mixed, tok, weight, block=256):
    pieces, arrays = weight
    length, model = tok.shape
    inner = mixed.shape[1]
    return pl.pallas_call(
        functools.partial(project_out, pieces=pieces),
        grid_spec=grid_of(
            (length // block,),
            [row_block(block, inner), row_block(block, model)] + anywhere(len(pieces)),
            row_block(block, model),
            [pltpu.VMEM((inner, model), BF16), pltpu.SemaphoreType.DMA((len(pieces),))],
        ),
        out_shape=jax.ShapeDtypeStruct((length, model), BF16),
        compiler_params=pltpu.CompilerParams(vmem_limit_bytes=40 << 20),
        cost_estimate=pl.CostEstimate(flops=14_000_000_000, bytes_accessed=20_000_000, transcendentals=0),
        name="project_out",
    )(place, mixed, tok, *arrays)


def scan_backward(proj_ref, tail_ref, sum_ref, keys_ref, out_ref, dout_ref, start_ref, cw_ref, cwk_ref, vec_ref,
                  skip_ref, pick_ref, *rest, nstate, low, groups, per, begin, last):
    if not begin:
        old_cross_ref, old_keys_ref, old_raw_ref = rest[:3]
        rest = rest[3:]
    dproj_ref, dcw_ref, dcb_ref, dskip_ref, dvec_ref = rest[:5]
    rest = rest[5:]
    if not last:
        cross_ref, keys_ref_out, raw_ref = rest[:3]
        rest = rest[3:]
    dsum, dstate, edge, logs_v, tails_v, steps_v, dt_tab, log_tab, log_rows, dcross, dkeys = rest
    first = pl.program_id(0) == 0
    span_all = groups * per * HEAD
    conv = dsum.shape[1]

    @pl.when(first)
    def _():
        dsum[Q : Q + 8, :] = jnp.zeros((8, conv), F32)
        dstate[...] = jnp.zeros_like(dstate)
        edge[...] = jnp.zeros_like(edge)
        dcw_ref[...] = jnp.zeros_like(dcw_ref)
        dcb_ref[...] = jnp.zeros_like(dcb_ref)
        dskip_ref[...] = jnp.zeros_like(dskip_ref)
        dvec_ref[...] = jnp.zeros_like(dvec_ref)

    raw = tail_ref[:, 2 * nstate : 2 * nstate + LANES] + vec_ref[0:1, :]
    dt = softplus(raw)
    lower = tri_lower()
    rate = vec_ref[1:2, :]
    logs = jnp.dot(lower.astype(F32), dt * rate, precision=HI, preferred_element_type=F32)
    fill_tables(dt, logs, dt_tab, log_tab, log_rows, low, groups, per)
    sum_b = keys_ref[:, 0:nstate]
    sum_c = keys_ref[:, nstate : 2 * nstate]
    sig_b, sig_c = sigmoid(sum_b), sigmoid(sum_c)
    keys_b32, keys_c32 = sum_b * sig_b, sum_c * sig_c
    keys_b, keys_c = keys_b32.astype(BF16), keys_c32.astype(BF16)
    c_cols = jnp.transpose(keys_c32).astype(BF16)
    cross = mm(keys_b, c_cols)
    span = per * HEAD
    low_half = lax.broadcasted_iota(jnp.int32, (Q, LANES), 1) < HEAD
    upper = lax.broadcasted_iota(jnp.int32, (Q, Q), 0) <= lax.broadcasted_iota(jnp.int32, (Q, Q), 1)
    if not begin:
        dcross[...] = old_cross_ref[...]
        dkeys[...] = old_keys_ref[...]
    else:
        dcross[...] = jnp.zeros_like(dcross)
        dkeys[...] = jnp.zeros_like(dkeys)

    def group(g, carry):
        base = pl.multiple_of(g * span, span)
        whole = pl.ds(base, span)
        dts, lgs = dt_tab[g], log_tab[g]
        dstate_b = dstate[:, whole].astype(BF16)
        from_state = mm(keys_b, dstate_b)
        tails_all, outs_all, lasts = [], [], []
        dcr = None
        for j in range(per // 2):
            cols = pl.ds(pl.multiple_of(base + j * LANES, LANES), LANES)
            h = (low + g) * per + 2 * j
            col0, col1 = spread(lgs, 2 * j), spread(lgs, 2 * j + 1)
            row0, row1 = log_rows[pl.ds(h, 1), :], log_rows[pl.ds(h + 1, 1), :]
            total = sum_ref[:, cols]
            sig = sigmoid(total)
            values = total * sig
            step = jnp.where(low_half, spread(dts, 2 * j), spread(dts, 2 * j + 1))
            stepped = values * step
            stepped_b = stepped.astype(BF16)
            dout = dout_ref[:, cols]
            dout_b = dout.astype(BF16)
            decay0 = jnp.exp(jnp.where(upper, row0 - col0, NEG))
            decay1 = jnp.exp(jnp.where(upper, row1 - col1, NEG))
            mix = jnp.concatenate([(decay0 * cross).astype(BF16), (decay1 * cross).astype(BF16)], axis=1)
            zero = jnp.zeros_like(dout_b)
            douts = jnp.concatenate(
                [jnp.where(low_half, dout_b, zero), jnp.where(low_half, zero, dout_b)], axis=0)
            local = mm(mix, douts)
            dmix = mm_t(stepped_b, douts)
            term = dmix[:, 0:Q] * decay0 + dmix[:, Q : 2 * Q] * decay1
            dcr = term if dcr is None else dcr + term
            both = jnp.where(low_half, col0, col1)
            last = both[Q - 1 : Q, :]
            tail = jnp.exp(last - both)
            passed = from_state[:, j * LANES : (j + 1) * LANES] * tail
            dstepped = local + passed
            skip = skip_ref[0:1, cols]
            scan = out_ref[:, cols] - skip * values
            logs_v[:, cols] = dout_b.astype(F32) * scan - stepped_b.astype(F32) * local
            tails_v[:, cols] = stepped * passed
            steps_v[:, cols] = dstepped * values
            dvalues = dstepped * step + dout * skip
            dskip_ref[0:1, cols] += jnp.sum(dout * values, axis=0, keepdims=True)
            dsum[0:Q, cols] = dvalues * (sig + values * (1.0 - sig))
            tails_all.append((stepped * tail).astype(BF16))
            outs_all.append((dout * jnp.exp(both)).astype(BF16))
            lasts.append(jnp.exp(last))
        dcross[...] += dcr
        outs = jnp.concatenate(outs_all, axis=1)
        starts = start_ref[:, whole]
        dkeys[:, nstate : 2 * nstate] += mm_t(outs, starts)
        dkeys[:, 0:nstate] += mm_t(jnp.concatenate(tails_all, axis=1), dstate_b)
        kept = dstate[:, whole] * jnp.concatenate(lasts, axis=1)
        edge[0:1, whole] = jnp.sum(kept * starts.astype(F32), axis=0, keepdims=True)
        dstate[:, whole] = kept + mm(c_cols, outs)
        return carry

    lax.fori_loop(0, groups, group, 0)

    if last:
        dcr = dcross[...]
        exact = lambda u, v: jnp.dot(u, v, precision=HI, preferred_element_type=F32)
        d_b = dkeys[:, 0:nstate] + exact(dcr, keys_c32)
        d_c = dkeys[:, nstate : 2 * nstate] + exact(jnp.transpose(dcr), keys_b32)
        dsum[0:Q, span_all : span_all + nstate] = d_b * (sig_b + keys_b32 * (1.0 - sig_b))
        dsum[0:Q, span_all + nstate : conv] = d_c * (sig_c + keys_c32 * (1.0 - sig_c))
    else:
        cross_ref[...] = dcross[...]
        keys_ref_out[...] = dkeys[...]

    def reduce_heads(v):
        high = v.astype(BF16)
        low = (v - high.astype(F32)).astype(BF16)
        return mm(high, pick_ref[...]) + mm(low, pick_ref[...])

    dlogs = reduce_heads(logs_v[...])
    dtails = reduce_heads(tails_v[...])
    dlogit = (
        jnp.dot(upper.astype(F32), dlogs, precision=HI, preferred_element_type=F32)
        + jnp.dot(1.0 - upper.astype(F32), dtails, precision=HI, preferred_element_type=F32)
        + reduce_heads(edge[...])[0:1, :]
    )
    dstep = reduce_heads(steps_v[...]) + dlogit * rate
    draw = dstep * sigmoid(raw)
    dvec_ref[0:1, :] += jnp.sum(draw, axis=0, keepdims=True)
    dvec_ref[1:2, :] += jnp.sum(dlogit * dt * rate, axis=0, keepdims=True)
    if last:
        dproj_ref[:, conv : conv + LANES] = (draw + old_raw_ref[...]).astype(BF16)
    elif begin:
        raw_ref[...] = draw
    else:
        raw_ref[...] = draw + old_raw_ref[...]

    wide = 256
    for start in range(0, conv, wide):
        part = pl.ds(start, wide)
        if start < span_all:
            source, taps_ref, local = proj_ref, cw_ref, part
        else:
            source, taps_ref, local = tail_ref, cwk_ref, pl.ds(start - span_all, wide)
        taken = source[:, local]
        total = None
        for k in range(4):
            moved = dsum[3 - k : 3 - k + Q, part]
            dcw_ref[k : k + 1, part] += jnp.sum(taken * moved, axis=0, keepdims=True)
            term = taps_ref[k : k + 1, local] * moved
            total = term if total is None else total + term
            if k == 3:
                dcb_ref[0:1, part] += jnp.sum(moved, axis=0, keepdims=True)
        dproj_ref[:, part] = total.astype(BF16)
    dsum[Q : Q + 8, :] = dsum[0:8, :]


def run_scan_backward(proj, sums, scan_out, dscan, starts, cw, vec, skip_cols, pick, inner, nstate, low, groups, per,
                      previous, last):
    length = proj.shape[0]
    blocks = length // Q
    span = groups * per * HEAD
    begin = previous is None
    conv = span + (2 * nstate if last else 0)
    where = low * per * HEAD // span
    whole = lambda shape: pl.BlockSpec(shape, lambda i: (0, 0))
    rows = lambda width, col=0: pl.BlockSpec((Q, width), lambda i: (blocks - 1 - i, col))
    part = lambda height: pl.BlockSpec((height, span), lambda i: (0, where))
    tail = 2 * nstate + LANES
    out_specs = [rows(conv + (LANES if last else 0)), whole((4, conv)), whole((1, conv)), whole((1, span)),
                 whole((8, LANES))]
    out_shape = [
        jax.ShapeDtypeStruct((length, conv + (LANES if last else 0)), BF16),
        jax.ShapeDtypeStruct((4, conv), F32),
        jax.ShapeDtypeStruct((1, conv), F32),
        jax.ShapeDtypeStruct((1, span), F32),
        jax.ShapeDtypeStruct((8, LANES), F32),
    ]
    carried = [rows(Q), rows(2 * nstate), rows(LANES)]
    if not last:
        out_specs += carried
        out_shape += [jax.ShapeDtypeStruct((length, w), F32) for w in (Q, 2 * nstate, LANES)]
    return pl.pallas_call(
        functools.partial(scan_backward, nstate=nstate, low=low, groups=groups, per=per, begin=begin, last=last),
        grid=(blocks,),
        in_specs=[
            rows(span, where), rows(tail, inner // tail), rows(span, where), rows(2 * nstate, inner // (2 * nstate)),
            rows(span, where), rows(span, where),
            pl.BlockSpec((nstate, span), lambda i: (blocks - 1 - i, where)),
            part(4), pl.BlockSpec((4, 2 * nstate), lambda i: (0, inner // (2 * nstate))),
            whole(vec.shape), part(1), pl.BlockSpec((span, LANES), lambda i: (where, 0)),
        ] + ([] if begin else carried),
        out_specs=out_specs,
        out_shape=out_shape,
        scratch_shapes=[
            pltpu.VMEM((Q + 8, conv), F32),
            pltpu.VMEM((nstate, span), F32),
            pltpu.VMEM((8, span), F32),
            pltpu.VMEM((Q, span), F32),
            pltpu.VMEM((Q, span), F32),
            pltpu.VMEM((Q, span), F32),
            pltpu.VMEM((groups, Q, LANES), F32),
            pltpu.VMEM((groups, Q, LANES), F32),
            pltpu.VMEM((LANES, Q), F32),
            pltpu.VMEM((Q, Q), F32),
            pltpu.VMEM((Q, 2 * nstate), F32),
        ],
        compiler_params=pltpu.CompilerParams(vmem_limit_bytes=50 << 20),
        cost_estimate=pl.CostEstimate(flops=40_000_000_000, bytes_accessed=40_000_000, transcendentals=15_000_000),
        name="scan_backward",
    )(proj, proj, sums, sums, scan_out, dscan, starts, cw, cw, vec, skip_cols, pick, *(previous or ()))


def bits_of(size):
    return [1 << b for b in range(size.bit_length() - 1)]


def swap(value, axis, bit, size):
    return lax.ppermute(value, axis, [(i, i ^ bit) for i in range(size)])


def after(value, *deps):
    return lax.optimization_barrier((value,) + deps)[0] if deps else value


def order_of(size):
    flipped = []
    for index in range(size):
        value = 0
        for low, high in zip(bits_of(size), reversed(bits_of(size))):
            value |= high if index & low else 0
        flipped.append(value)
    return flipped


class Gather:
    def __init__(self, shard, order, rep_index, groups, copies, lanes, chunks):
        self.order, self.groups, self.copies = order, groups, copies
        self.size = shard.shape
        self.lanes = lanes
        self.half = shard.shape[0] // 2
        self.rows = self.half // chunks
        self.shard = shard
        parity = rep_index & 1
        self.mine = [lax.dynamic_slice_in_dim(shard, parity * self.half + c * self.rows, self.rows, 0)
                     for c in range(chunks)]
        self.there, self.across = [None] * chunks, [None] * chunks

    def far(self, chunk, *deps):
        value = after(self.mine[chunk], *deps)
        self.there[chunk] = swap(value, "shard", 2, self.groups)

    def side(self, chunk):
        self.across[chunk] = swap(self.there[chunk], "rep", 1, self.copies)

    def finish(self):
        have = {0: [(0, None, 0, self.shard)]}
        have[2] = [(c * self.rows, h, self.half, v) for h, vs in ((0, self.there), (1, self.across))
                   for c, v in enumerate(vs)]
        for source in (0, 2):
            have[source ^ 1] = [(r, h, s, swap(v, "shard", 1, self.groups)) for r, h, s, v in have[source]]
        pieces, arrays = [], []
        for position, source in enumerate(self.order):
            for row, half, size, value in have[source]:
                if self.lanes:
                    pieces.append((row, half, size, position * self.size[1]))
                else:
                    pieces.append((row + position * self.size[0], half, size, 0))
                arrays.append(value)
        return tuple(pieces), tuple(arrays)


class Total:
    def __init__(self, kept, sent, axis, rep_index, groups, copies):
        self.axis, self.rep_index = axis, rep_index
        self.stages = [("shard", bit, groups) for bit in bits_of(groups)]
        self.stages += [("rep", bit, copies) for bit in bits_of(copies)]
        self.back = list(reversed(self.stages[len(bits_of(groups)) :]))
        self.value, self.out = kept, sent
        self.fly()

    def fly(self):
        self.coming = swap(self.out, *self.stages[0])

    def step(self, *deps):
        coming = after(self.coming, *deps)
        self.stages.pop(0)
        value = self.value
        if not self.stages:
            self.value = (value.astype(F32) + coming.astype(F32)).astype(BF16)
            self.out = self.value
            return self.out
        name, bit, _ = self.stages[0]
        if name == "shard":
            half = value.shape[self.axis] // 2
            low, high = 0, half
            axis = self.axis
        else:
            half = value.shape[0] // 2
            turn = (self.rep_index & bit) != 0
            low = jnp.where(turn, half, 0)
            high = half - low
            axis = 0
        cut = lambda v, start: lax.dynamic_slice_in_dim(v, start, half, axis).astype(F32)
        self.out = (cut(value, high) + cut(coming, high)).astype(BF16)
        self.value = cut(value, low) + cut(coming, low)
        self.fly()
        return self.out

    def widen(self, *deps):
        name, bit, size = self.back.pop(0)
        other = swap(after(self.value, *deps), name, bit, size)
        turn = (self.rep_index & bit) != 0
        low, high = jnp.where(turn, other, self.value), jnp.where(turn, self.value, other)
        if self.back:
            self.value = jnp.concatenate([low, high])
        else:
            self.value = [low.astype(F32), high.astype(F32)]
        return self.value


def outer(left, right):
    return lax.dot_general(left, right, (((0,), (0,)), ((), ())), preferred_element_type=F32).astype(BF16)


def on_device(groups, copies, tokens, norm_gain, in_weight, conv_weight, conv_bias, dt_bias, a_log, skip, gate_gain,
              out_weight, cotangent):
    if tokens.shape[0] != 1 or groups != 4:
        raise ValueError("unexpected sizes")
    order = order_of(groups)
    shard_index = lax.axis_index("shard")
    rep_index = lax.axis_index("rep")
    tok, cot = tokens[0], cotangent[0]
    inner = gate_gain.shape[0] * groups
    conv = conv_bias.shape[0] * groups
    heads = dt_bias.shape[0] * groups
    nstate = (conv - inner) // 2
    model = tok.shape[1]
    taps = conv_weight.shape[0]
    outputs_all = in_weight.shape[1]
    place = jnp.stack([shard_index, rep_index & 1]).astype(jnp.int32)

    turned = in_weight.T
    total = conv + LANES
    conv_part = jnp.pad(turned[inner:], ((0, total + inner - outputs_all), (0, 0)))
    make = lambda shard, lanes, chunks: Gather(shard, order, rep_index, groups, copies, lanes, chunks)
    wc = make(conv_part, True, 2)
    wg = make(turned[:inner], True, 1)
    ow = make(out_weight, False, 1)

    small = (norm_gain, conv_bias, dt_bias, a_log, skip, gate_gain, conv_weight)
    packed = jnp.concatenate([v.reshape(-1) for v in small])
    wc.far(0)
    wc.far(1, wc.there[0])
    wc.side(0)
    wc.side(1)
    wg.far(0, wc.there[1])
    ow.far(0, wc.across[1])
    wg.side(0)
    ow.side(0)
    rows = [packed, swap(packed, "shard", 1, groups)]
    far = swap(packed, "shard", 2, groups)
    rows += [far, swap(far, "shard", 1, groups)]
    for bit in bits_of(groups):
        turn = (shard_index & bit) != 0
        rows = [jnp.where(turn, rows[j ^ bit], rows[j]) for j in range(groups)]
    everyone = jnp.stack(rows).astype(F32)
    parts, low = [], 0
    for v in small:
        parts.append(everyone[:, low : low + v.size])
        low += v.size
    gain, cb, db, al, sk, gg = (v.reshape(-1) for v in parts[:6])
    cw = parts[6].reshape(groups, taps, -1).transpose(1, 0, 2).reshape(taps, conv)
    gain, cb, gg = gain[None], cb[None], gg[None]
    vec = jnp.pad(jnp.stack([db, -jnp.exp(al)]), ((0, 6), (0, LANES - heads)))
    skip_cols = jnp.repeat(sk, inner // heads)[None]
    pick = (jnp.arange(inner)[:, None] // (inner // heads) == jnp.arange(LANES)[None]).astype(BF16)

    wc, wg, ow = wc.finish(), wg.finish(), ow.finish()
    normed, proj = run_project_in(place, tok, gain, wc, total, order)
    per = 8
    scan_out, sums, starts = run_scan_forward(proj, cw, cb, vec, skip_cols, inner, nstate, heads // per, per)
    mixed, dscan, dgate, dgg = run_gating(place, normed, wg, ow, cot, scan_out, gg, order)

    chain = lambda kept, sent, axis: Total(kept, sent, axis, rep_index, groups, copies)
    half = inner // 2
    out_sent = outer(mixed[:, half:], cot)
    o = chain(outer(mixed[:, :half], cot), out_sent, 0)
    half = model // 2
    left, right = normed[:, :half], normed[:, half:]
    gate_sent = outer(dgate, right)
    g = chain(outer(dgate, left), gate_sent, 1)

    blocks = heads // per
    cuts = [blocks * v // 3 for v in range(4)]
    marks = [o.step(g.value)]
    marks.append(g.step(*marks))
    chains, grads, carried = [o, g], [], None
    for index in range(3):
        low, high = cuts[index], cuts[index + 1]
        last = index == 2
        found = run_scan_backward(
            proj, sums, scan_out, after(dscan, *marks), starts, cw, vec, skip_cols, pick, inner, nstate, low,
            high - low, per, carried, last)
        grads.append(found[:5])
        carried = tuple(found[5:])
        marks = []
        for old in chains[: 1 if index == 0 else None]:
            marks.append(old.step(found[0], *marks))
        dproj = after(found[0], *marks)
        sent = outer(dproj, right)
        kept = outer(dproj, left)
        new = chain(kept, sent, 1)
        marks.append(new.step(kept))
        chains.append(new)

    def exchange(value):
        for axis, size in (("shard", groups), ("rep", copies)):
            for bit in bits_of(size):
                value = value + swap(value, axis, bit, size)
        return value

    def advance(*fence):
        moved = []
        for old in chains:
            if old.stages:
                moved.append(old.step(*fence, *moved))
            elif old.back:
                old.widen(*fence)
        return moved

    output = run_project_out(place, after(mixed, *marks), tok, ow)
    marks = advance(output)
    part = run_gate_back(place, after(dgate, *marks), model, wg)
    marks = advance(part)
    input_grad, dgain = run_input_back(place, after(part, *marks), [v[0] for v in grads], tok, cot, gain, wc, order)
    advance(dgain)
    while any(old.stages or old.back for old in chains):
        advance()

    in_total = jnp.concatenate([v for old in chains[1:] for v in old.value])[:outputs_all].T
    out_total = jnp.concatenate(o.value)

    dcw = jnp.concatenate([v[1] for v in grads], axis=1)
    dcb = jnp.concatenate([v[2][0] for v in grads])
    dskip = jnp.concatenate([v[3][0] for v in grads]).reshape(heads, -1).sum(1)
    dvec = sum(v[4] for v in grads)
    pieces = (dcb, dvec[0, :heads], dvec[1, :heads], dskip, dgg[0])
    flat = jnp.concatenate([v.reshape(groups, -1) for v in pieces]
                           + [dcw.reshape(taps, groups, -1).transpose(1, 0, 2).reshape(groups, -1)], axis=1)
    flat = exchange(jnp.concatenate([dgain[0].reshape(groups, -1), flat], axis=1))
    own = lax.dynamic_slice_in_dim(flat, shard_index, 1, 0)[0]
    shares, low = [], 0
    for v in small:
        shares.append(own[low : low + v.size].reshape(v.shape))
        low += v.size
    d_gain, d_cb, d_db, d_al, d_sk, d_gg, d_cw = shares
    return (output[None], input_grad[None], d_gain, in_total, d_cw, d_cb, d_db, d_al, d_sk, d_gg, out_total)


def solution(mesh):
    whole = P(("shard", "rep"), None, None)
    row, matrix, cols = P("shard"), P("shard", None), P(None, "shard")
    return jax.shard_map(
        functools.partial(on_device, mesh.shape["shard"], mesh.shape["rep"]),
        mesh=mesh,
        in_specs=(whole, row, matrix, cols, row, row, row, row, row, matrix, whole),
        out_specs=(whole, whole, row, matrix, cols, row, row, row, row, row, matrix),
        check_vma=False,
    )
```

time: 1890 us -> 750 us (0.40)
  waiting for transfers between devices: 741 us -> 235 us
  matrix products: 494 us -> 55.1 us
  Pallas kernels: 0 us -> 279 us
  local copies, waits for them, and re-layouts: 285 us -> 43.8 us
  other arithmetic: 271 us -> 59.5 us
  blocking collectives: 76.2 us -> 0 us
  starting transfers between devices: 0.24 us -> 67.1 us
    dot_general x58 -> x10, matrix products: 494 us -> 55.1 us  [outer(): lax.dot_general(left, right, (((0,), (0,)), ((), ())), preferred_element_...]
    psum x1 -> x0, waiting for transfers between devices: 378 us -> none  [on_device(): lax.psum((owned[0], owned[1], owned[2], owned[3], owned[4], owned[5], own...]
    pallas_call x0 -> x9, Pallas kernels: none -> 279 us  [the longest x3 97.7 us: run_scan_backward(): pl.pallas_call(functools.partial(scan_backward, nstate=nstate, low=low, g...]
    reduce_scatter x2 -> x0, waiting for transfers between devices: 267 us -> none  [the longest x1 267 us: on_device(): lax.psum_scatter(in_grad, 'shard', scatter_dimension=0, tiled=True)]
    ppermute x0 -> x67, waiting for transfers between devices: none -> 235 us  [swap(): return lax.ppermute(value, axis, [(i, i ^ bit) for i in range(size)])]
    reduce_sum x16 -> x1, other arithmetic: 104 us -> 0.11 us  [on_device(): dskip = jnp.concatenate([v[3][0] for v in grads]).reshape(heads, -1).sum(1)]
    mul x48 -> x0, local copies, waits for them, and re-layouts: 103 us -> none  [the longest x24 56.3 us: stretch_step(): scaled = values * tails[:, :, None]]
    all_gather x2 -> x0, waiting for transfers between devices: 94 us -> none  [the longest x1 94 us: on_device(): lax.all_gather(in_weight, 'shard', axis=0, tiled=True)]
  transfers between devices with their start and end apart: 6 -> 67, of which waited for: 3 -> 21; matrix products, arithmetic and copies ran while one was open for 46% -> 16% of each run, Pallas kernels for 0% -> 32%
where the time goes in v1:
time: 750 us; the launch traced here: 742 us
  Pallas kernels  279 us (37%)
  waiting for transfers between devices  235 us (31%)
  starting transfers between devices  67.1 us (9%)
  other arithmetic  59.5 us (8%)
  matrix products  55.1 us (7%)
  local copies, waits for them, and re-layouts  43.8 us (6%)
    ppermute x67, waiting for transfers between devices, swap(): return lax.ppermute(value, axis, [(i, i ^ bit) for i in range(size)])  235 us
    pallas_call x3, Pallas kernels, run_scan_backward(): pl.pallas_call(functools.partial(scan_backward, nstate=nstate, low=low, g...  97.7 us
    ppermute x67, starting transfers between devices, swap(): return lax.ppermute(value, axis, [(i, i ^ bit) for i in range(size)])  67.1 us
    dot_general x10, matrix products, outer(): lax.dot_general(left, right, (((0,), (0,)), ((), ())), preferred_element_...  55.1 us
    pallas_call x1, Pallas kernels, run_scan_forward(): pl.pallas_call(functools.partial(scan_forward, inner=inner, nstate=nstate...  48.5 us
    pallas_call x1, Pallas kernels, run_gating(): pl.pallas_call(functools.partial(gating, wg_pieces=wg_pieces, ow_pieces=o...  42.5 us
    pallas_call x1, Pallas kernels, run_input_back(): pl.pallas_call(functools.partial(input_back, count=len(dprojs), pieces=pi...  27.3 us
    pallas_call x1, Pallas kernels, run_project_in(): pl.pallas_call(functools.partial(project_in, pieces=pieces, order=order),...  23.7 us
  transfers between devices with their start and end apart: 67, of which 21 were waited for; matrix products, arithmetic and copies ran while one was open for 16% of the time, Pallas kernels for 32%

profile of v1, /device:TPU:0, one launch (start us, length us, event | category | flops | bytes accessed | tf_op | source)
XLA Modules:
  0.0 741.6 jit_solution(9663842564535867391)
XLA Ops:
  6.0 15.0 %collective-permute-done.3.rest_1_.rest_4_ = bf16[864,384]{1,0:T(8,128)(2,1)} collective-permute-done((bf16[864,384]{1,0:T(8,128)(2,1)S(1)}, bf16[864,384]{1,0:T(8,128)(2,1)}, u32[]{:S(2)}, u32[]{:S(2)}) %collective-permute-start.3) | collective-permute-done | bytes 663584 | tf_op jit(solution)/shard_map/ppermute | solution.py:672
  22.8 14.4 %collective-permute-done.4.rest_2_.rest_5_ = bf16[864,384]{1,0:T(8,128)(2,1)} collective-permute-done((bf16[864,384]{1,0:T(8,128)(2,1)S(1)}, bf16[864,384]{1,0:T(8,128)(2,1)}, u32[]{:S(2)}, u32[]{:S(2)}) %collective-permute-start.4) | collective-permute-done | bytes 663584 | tf_op jit(solution)/shard_map/ppermute | solution.py:672
  73.9 13.0 %collective-permute-done.12.rest_1_ = bf16[1536,384]{1,0:T(8,128)(2,1)S(1)} collective-permute-done((bf16[1536,384]{1,0:T(8,128)(2,1)}, bf16[1536,384]{1,0:T(8,128)(2,1)S(1)}, u32[]{:S(2)}, u32[]{:S(2)}) %collective-permute-start.12) | collective-permute-done | bytes 1179680 | tf_op jit(solution)/shard_map/ppermute | solution.py:672
  88.4 23.2 %collective-permute-done.17.rest_7_.rest_1_ = bf16[384,1536]{1,0:T(8,128)(2,1)} collective-permute-done((bf16[384,1536]{1,0:T(8,128)(2,1)}, bf16[384,1536]{1,0:T(8,128)(2,1)}, u32[]{:S(2)}, u32[]{:S(2)}) %collective-permute-start.17) | collective-permute-done | bytes 1179680 | tf_op jit(solution)/shard_map/ppermute | solution.py:672
  141.4 23.7 %project_in.1 = (bf16[1024,1536]{1,0:T(8,128)(2,1)}, f32[1024,3456]{1,0:T(8,128)}) custom-call(s32[2]{0:T(128)S(1)} %pad_add_fusion.place_ref, bf16[1024,1536]{1,0:T(8,128)(2,1)} %bitcast.45, f32[1,1536]{1,0:T(1,128)S(1)} %bitcast.41, bf16[3456,384]{1,0:T(8,128)(2,1)} %pad.8.rest_0_.rest_3_, bf16[864,384]{1,0:T(8,128)(2,1)} %collective-permute-done.3.rest_1_.rest_4_, ...), custom_call_target="tpu_custom_call" | custom-call | flops 20000000000 | bytes 30000000 | tf_op jit(solution)/shard_map/project_in/pallas_call | solution.py:222
  165.1 48.5 %scan_forward.1 = (f32[1024,3072]{1,0:T(8,128)}, f32[1024,3328]{1,0:T(8,128)}, bf16[1024,3072]{1,0:T(8,128)(2,1)}) custom-call(f32[1024,3456]{1,0:T(8,128)} %get-tuple-element.85.proj_ref.tail_ref, f32[4,3328]{1,0:T(4,128)} %reshape.119.cw_ref.cwk_ref, f32[1,3328]{1,0:T(1,128)} %broadcast_in_dim_reshape.13.cb_ref, f32[8,128]{1,0:T(8,128)} %select_maximum_fusion.vec_ref, ...), custom_call_target="tpu_custom_call" | custom-call | flops 12000000000 | bytes 60000000 | tf_op jit(solution)/shard_map/scan_forward/pallas_call | solution.py:127
  215.7 42.5 %gating.1 = (bf16[1024,3072]{1,0:T(8,128)(2,1)}, f32[1024,3072]{1,0:T(8,128)}, bf16[1024,3072]{1,0:T(8,128)(2,1)}, f32[1,3072]{1,0:T(1,128)}) custom-call(s32[2]{0:T(128)} %copy-done.19, bf16[1024,1536]{1,0:T(8,128)(2,1)} %get-tuple-element.84.normed_ref, bf16[1024,1536]{1,0:T(8,128)(2,1)} %bitcast.55, f32[1024,3072]{1,0:T(8,128)} %get-tuple-element.86.scan_ref.out_ref, ...), custom_call_target="tpu_custom_call" | custom-call | flops 40000000000 | bytes 70000000 | tf_op jit(solution)/shard_map/gating/pallas_call | solution.py:305
  258.2 9.2 %convolution_convert_fusion = bf16[1536,1536]{1,0:T(8,128)(2,1)} fusion(bf16[1024,3072]{1,0:T(8,128)(2,1)} %get-tuple-element.122.mixed_ref, bf16[1,1024,1536]{2,1,0:T(8,128)(2,1)} %param.21), kind=kOutput, calls=%fused_computation.1 | convolution fusion | flops 4834197504 | bytes 11010048 | tf_op jit(solution)/shard_map/dot_general | solution.py:776
  276.8 7.8 %convolution_convert_fusion.1 = bf16[1536,1536]{1,0:T(8,128)(2,1)S(1)} fusion(bf16[1024,3072]{1,0:T(8,128)(2,1)} %get-tuple-element.122.mixed_ref, bf16[1,1024,1536]{2,1,0:T(8,128)(2,1)} %param.21), kind=kOutput, calls=%fused_computation.2 | convolution fusion | flops 4834197504 | bytes 11010048 | tf_op jit(solution)/shard_map/dot_general | solution.py:776
  284.6 8.5 %convolution_convert_fusion.3 = bf16[3072,768]{1,0:T(8,128)(2,1)S(1)} fusion(bf16[1024,3072]{1,0:T(8,128)(2,1)} %get-tuple-element.128.dgate_ref, bf16[1024,1536]{1,0:T(8,128)(2,1)S(1)} %copy-done.53), kind=kOutput, calls=%fused_computation.4 | convolution fusion | flops 4834197504 | bytes 12582912 | tf_op jit(solution)/shard_map/dot_general | solution.py:776
  303.9 31.4 %scan_backward.3 = (bf16[1024,1024]{1,0:T(8,128)(2,1)}, f32[4,1024]{1,0:T(4,128)S(1)}, f32[1,1024]{1,0:T(1,128)S(1)}, f32[1,1024]{1,0:T(1,128)S(1)}, f32[8,128]{...) custom-call(f32[1024,3456]{1,0:T(8,128)} %get-tuple-element.85.proj_ref.tail_ref, ...), custom_call_target="tpu_custom_call" | custom-call | flops 40000000000 | bytes 40000000 | tf_op jit(solution)/shard_map/scan_backward/pallas_call | solution.py:636
  335.4 15.6 %collective-permute-done.23 = bf16[768,1536]{1,0:T(8,128)(2,1)S(1)} collective-permute-done((bf16[768,1536]{1,0:T(8,128)(2,1)}, bf16[768,1536]{1,0:T(8,128)(2,1)S(1)}, u32[]{:S(2)}, u32[]{:S(2)}) %collective-permute-start.23) | collective-permute-done | bytes 2359328 | tf_op jit(solution)/shard_map/ppermute | solution.py:672
  366.7 31.9 %scan_backward.4 = (bf16[1024,1024]{1,0:T(8,128)(2,1)}, f32[4,1024]{1,0:T(4,128)S(1)}, f32[1,1024]{1,0:T(1,128)S(1)}, f32[1,1024]{1,0:T(1,128)S(1)}, f32[8,128]{...) custom-call(f32[1024,3456]{1,0:T(8,128)} %get-tuple-element.85.proj_ref.tail_ref, ...), custom_call_target="tpu_custom_call" | custom-call | flops 40000000000 | bytes 40000000 | tf_op jit(solution)/shard_map/scan_backward/pallas_call | solution.py:636
  400.3 12.1 %collective-permute-done.28 = bf16[3072,384]{1,0:T(8,128)(2,1)} collective-permute-done((bf16[3072,384]{1,0:T(8,128)(2,1)}, bf16[3072,384]{1,0:T(8,128)(2,1)}, u32[]{:S(2)}, u32[]{:S(2)}) %collective-permute-start.28) | collective-permute-done | bytes 2359328 | tf_op jit(solution)/shard_map/ppermute | solution.py:672
  416.5 12.3 %collective-permute-done.29 = bf16[1024,384]{1,0:T(8,128)(2,1)} collective-permute-done((bf16[1024,384]{1,0:T(8,128)(2,1)}, bf16[1024,384]{1,0:T(8,128)(2,1)}, u32[]{:S(2)}, u32[]{:S(2)}) %collective-permute-start.29) | collective-permute-done | bytes 786464 | tf_op jit(solution)/shard_map/ppermute | solution.py:672
  444.8 34.4 %scan_backward.5 = (bf16[1024,1408]{1,0:T(8,128)(2,1)}, f32[4,1280]{1,0:T(4,128)S(1)}, f32[1,1280]{1,0:T(1,128)S(1)}, f32[1,1024]{1,0:T(1,128)S(1)}, f32[8,128]{1,0:T(8,128)S(1)}) custom-call(f32[1024,3456]{1,0:T(8,128)} %get-tuple-element.85.proj_ref.tail_ref, f32[1024,3456]{1,0:T(8,128)} %get-tuple-element.85.proj_ref.tail_ref, ...), custom_call_target="tpu_custom_call" | custom-call | flops 40000000000 | bytes 40000000 | tf_op jit(solution)/shard_map/scan_backward/pallas_call | solution.py:636
  509.4 19.7 %project_out.1 = bf16[1024,1536]{1,0:T(8,128)(2,1)} custom-call(s32[2]{0:T(128)S(1)} %copy-done.20, bf16[1024,3072]{1,0:T(8,128)(2,1)} %get-tuple-element.122.mixed_ref, bf16[1024,1536]{1,0:T(8,128)(2,1)S(1)} %bitcast.47, bf16[768,1536]{1,0:T(8,128)(2,1)S(1)} %copy-done.2, bf16[384,1536]{1,0:T(8,128)(2,1)} %collective-permute-done.17.rest_7_.rest_1_, ...), custom_call_target="tpu_custom_call" | custom-call | flops 14000000000 | bytes 20000000 | tf_op jit(solution)/shard_map/project_out/pallas_call | solution.py:435
  538.1 19.9 %gate_back.1.part_ref = f32[1024,1536]{1,0:T(8,128)} custom-call(s32[2]{0:T(128)S(1)} %copy-done.20, bf16[1024,3072]{1,0:T(8,128)(2,1)} %get-tuple-element.128.dgate_ref, bf16[3072,384]{1,0:T(8,128)(2,1)S(1)} %copy-done.1, bf16[1536,384]{1,0:T(8,128)(2,1)S(1)} %copy-done.8, bf16[1536,384]{1,0:T(8,128)(2,1)} %collective-permute-done.13.rest_2_, ...), custom_call_target="tpu_custom_call" | custom-call | flops 16000000000 | bytes 22000000 | tf_op jit(solution)/shard_map/gate_back/pallas_call | solution.py:344
  563.4 12.6 %collective-permute-done.64 = bf16[96,1536]{1,0:T(8,128)(2,1)S(1)} collective-permute-done((bf16[96,1536]{1,0:T(8,128)(2,1)S(1)}, bf16[96,1536]{1,0:T(8,128)(2,1)S(1)}, u32[]{:S(2)}, u32[]{:S(2)}) %collective-permute-start.64) | collective-permute-done | bytes 294944 | tf_op jit(solution)/shard_map/ppermute | solution.py:672
  576.2 27.3 %input_back.1 = (f32[1024,1536]{1,0:T(8,128)}, f32[1,1536]{1,0:T(1,128)S(1)}) custom-call(s32[2]{0:T(128)S(1)} %copy-done.20, f32[1024,1536]{1,0:T(8,128)} %gate_back.1.part_ref, bf16[1024,1536]{1,0:T(8,128)(2,1)} %bitcast.46, bf16[1024,1536]{1,0:T(8,128)(2,1)} %bitcast.56, f32[1,1536]{1,0:T(1,128)S(1)} %bitcast.42, ...), custom_call_target="tpu_custom_call" | custom-call | flops 22000001024 | bytes 46000000 | tf_op jit(solution)/shard_map/input_back/pallas_call | solution.py:400
  610.5 16.7 %collective-permute-done.52 = bf16[128,384]{1,0:T(8,128)(2,1)S(1)} collective-permute-done((bf16[128,384]{1,0:T(8,128)(2,1)S(1)}, bf16[128,384]{1,0:T(8,128)(2,1)S(1)}, u32[]{:S(2)}, u32[]{:S(2)}) %collective-permute-start.52) | collective-permute-done | bytes 98336 | tf_op jit(solution)/shard_map/ppermute | solution.py:672
  652.9 12.5 %collective-permute-done.48 = f32[4,5348]{1,0:T(4,128)S(1)} collective-permute-done((f32[4,5348]{1,0:T(4,128)S(1)}, f32[4,5348]{1,0:T(4,128)S(1)}, u32[]{:S(2)}, u32[]{:S(2)}) %collective-permute-start.48) | collective-permute-done | bytes 85600 | tf_op jit(solution)/shard_map/ppermute | solution.py:672
  682.5 20.0 %collective-permute-done.66 = bf16[384,1536]{1,0:T(8,128)(2,1)S(1)} collective-permute-done((bf16[384,1536]{1,0:T(8,128)(2,1)S(1)}, bf16[384,1536]{1,0:T(8,128)(2,1)S(1)}, u32[]{:S(2)}, u32[]{:S(2)}) %collective-permute-start.66) | collective-permute-done | bytes 1179680 | tf_op jit(solution)/shard_map/ppermute | solution.py:672
  705.8 22.0 %collective-permute-done.51 = bf16[1536,384]{1,0:T(8,128)(2,1)S(1)} collective-permute-done((bf16[1536,384]{1,0:T(8,128)(2,1)S(1)}, bf16[1536,384]{1,0:T(8,128)(2,1)S(1)}, u32[]{:S(2)}, u32[]{:S(2)}) %collective-permute-start.51) | collective-permute-done | bytes 1179680 | tf_op jit(solution)/shard_map/ppermute | solution.py:672
  (383 shorter events, 245.4 us)
Async XLA Ops:
  47.9 83.8 %collective-permute-start.7 = (bf16[3456,384]{1,0:T(8,128)(2,1)}, bf16[3456,384]{1,0:T(8,128)(2,1)}, u32[]{:S(2)}, u32[]{:S(2)}) collective-permute-start(bf16[3456,384]{1,0:T(8,128)(2,1)} %pad.8.rest_0_.rest_3_), channel_id=1, source_target_pairs={{0,8},{8,0},{16,24},{24,16},{1,9},{9,1},{17,25},{25,17},{2,10},{10... | collective-permute-start | bytes 7962632 | tf_op jit(solution)/shard_map/ppermute | solution.py:672
  66.9 44.7 %collective-permute-start.17 = (bf16[384,1536]{1,0:T(8,128)(2,1)}, bf16[384,1536]{1,0:T(8,128)(2,1)}, u32[]{:S(2)}, u32[]{:S(2)}) collective-permute-start(bf16[384,1536]{1,0:T(8,128)(2,1)} %constant_dynamic-slice_fusion), channel_id=1, source_target_pairs={{0,16},{8,24},{16,0},{24,8},{1,17},{9,25},{17,1},{25,9},{2,18},{10... | collective-permute-start | bytes 3538952 | tf_op jit(solution)/shard_map/ppermute | solution.py:672
  68.1 63.0 %collective-permute-start.14 = (bf16[3072,384]{1,0:T(8,128)(2,1)S(1)}, bf16[3072,384]{1,0:T(8,128)(2,1)}, u32[]{:S(2)}, u32[]{:S(2)}) collective-permute-start(bf16[3072,384]{1,0:T(8,128)(2,1)S(1)} %slice.121.rest_0_), channel_id=1, source_target_pairs={{0,8},{8,0},{16,24},{24,16},{1,9},{9,1},{17,25},{25,17},{2,10},{10... | collective-permute-start | bytes 7077896 | tf_op jit(solution)/shard_map/ppermute | solution.py:672
  73.7 57.4 %collective-permute-start.11 = (bf16[864,384]{1,0:T(8,128)(2,1)}, bf16[864,384]{1,0:T(8,128)(2,1)}, u32[]{:S(2)}, u32[]{:S(2)}) collective-permute-start(bf16[864,384]{1,0:T(8,128)(2,1)} %copy-done.13), channel_id=1, source_target_pairs={{0,8},{8,0},{16,24},{24,16},{1,9},{9,1},{17,25},{25,17},{2,10},{10... | collective-permute-start | bytes 1990664 | tf_op jit(solution)/shard_map/ppermute | solution.py:672
  86.9 44.8 %collective-permute-start.13 = (bf16[1536,384]{1,0:T(8,128)(2,1)S(1)}, bf16[1536,384]{1,0:T(8,128)(2,1)}, u32[]{:S(2)}, u32[]{:S(2)}) collective-permute-start(bf16[1536,384]{1,0:T(8,128)(2,1)S(1)} %collective-permute-done.12.rest_1_), channel_id=1, source_target_pairs={{0,1},{1,0},{2,3},{3,2},{4,5},{5,4},{6,7},{7,6},{8,9},{9,8},{10,11... | collective-permute-start | bytes 3538952 | tf_op jit(solution)/shard_map/ppermute | solution.py:672
  131.1 82.4 %collective-permute-start.19 = (bf16[768,1536]{1,0:T(8,128)(2,1)}, bf16[768,1536]{1,0:T(8,128)(2,1)}, u32[]{:S(2)}, u32[]{:S(2)}) collective-permute-start(bf16[768,1536]{1,0:T(8,128)(2,1)} %rest_0_.1), channel_id=1, source_target_pairs={{0,8},{8,0},{16,24},{24,16},{1,9},{9,1},{17,25},{25,17},{2,10},{10... | collective-permute-start | bytes 7077896 | tf_op jit(solution)/shard_map/ppermute | solution.py:672
  131.2 82.4 %collective-permute-start.15 = (bf16[1536,384]{1,0:T(8,128)(2,1)S(1)}, bf16[1536,384]{1,0:T(8,128)(2,1)S(1)}, u32[]{:S(2)}, u32[]{:S(2)}) collective-permute-start(bf16[1536,384]{1,0:T(8,128)(2,1)S(1)} %collective-permute-done.12.rest_1_), channel_id=1, source_target_pairs={{0,8},{8,0},{16,24},{24,16},{1,9},{9,1},{17,25},{25,17},{2,10},{10... | collective-permute-start | bytes 3538952 | tf_op jit(solution)/shard_map/ppermute | solution.py:672
  131.7 82.9 %collective-permute-start.20 = (bf16[384,1536]{1,0:T(8,128)(2,1)}, bf16[384,1536]{1,0:T(8,128)(2,1)S(1)}, u32[]{:S(2)}, u32[]{:S(2)}) collective-permute-start(bf16[384,1536]{1,0:T(8,128)(2,1)} %collective-permute-done.17.rest_7_.rest_1_), channel_id=1, source_target_pairs={{0,8},{8,0},{16,24},{24,16},{1,9},{9,1},{17,25},{25,17},{2,10},{10... | collective-permute-start | bytes 3538952 | tf_op jit(solution)/shard_map/ppermute | solution.py:672
  131.7 84.0 %collective-permute-start.16 = (bf16[1536,384]{1,0:T(8,128)(2,1)}, bf16[1536,384]{1,0:T(8,128)(2,1)}, u32[]{:S(2)}, u32[]{:S(2)}) collective-permute-start(bf16[1536,384]{1,0:T(8,128)(2,1)} %collective-permute-done.13.rest_2_), channel_id=1, source_target_pairs={{0,8},{8,0},{16,24},{24,16},{1,9},{9,1},{17,25},{25,17},{2,10},{10... | collective-permute-start | bytes 3538952 | tf_op jit(solution)/shard_map/ppermute | solution.py:672
  139.2 76.5 %collective-permute-start.21 = (bf16[384,1536]{1,0:T(8,128)(2,1)}, bf16[384,1536]{1,0:T(8,128)(2,1)}, u32[]{:S(2)}, u32[]{:S(2)}) collective-permute-start(bf16[384,1536]{1,0:T(8,128)(2,1)} %collective-permute-done.18.rest_8_.rest_2_), channel_id=1, source_target_pairs={{0,8},{8,0},{16,24},{24,16},{1,9},{9,1},{17,25},{25,17},{2,10},{10... | collective-permute-start | bytes 3538952 | tf_op jit(solution)/shard_map/ppermute | solution.py:672
  297.1 53.9 %collective-permute-start.23 = (bf16[768,1536]{1,0:T(8,128)(2,1)}, bf16[768,1536]{1,0:T(8,128)(2,1)S(1)}, u32[]{:S(2)}, u32[]{:S(2)}) collective-permute-start(bf16[768,1536]{1,0:T(8,128)(2,1)} %get-tuple-element.159), channel_id=1, source_target_pairs={{0,16},{8,24},{16,0},{24,8},{1,17},{9,25},{17,1},{25,9},{2,18},{10... | collective-permute-start | bytes 7077896 | tf_op jit(solution)/shard_map/ppermute | solution.py:672
  357.9 54.4 %collective-permute-start.28 = (bf16[3072,384]{1,0:T(8,128)(2,1)}, bf16[3072,384]{1,0:T(8,128)(2,1)}, u32[]{:S(2)}, u32[]{:S(2)}) collective-permute-start(bf16[3072,384]{1,0:T(8,128)(2,1)} %get-tuple-element.158), channel_id=1, source_target_pairs={{0,16},{8,24},{16,0},{24,8},{1,17},{9,25},{17,1},{25,9},{2,18},{10... | collective-permute-start | bytes 7077896 | tf_op jit(solution)/shard_map/ppermute | solution.py:672
  359.4 39.3 %collective-permute-start.25 = (bf16[384,1536]{1,0:T(8,128)(2,1)}, bf16[384,1536]{1,0:T(8,128)(2,1)S(1)}, u32[]{:S(2)}, u32[]{:S(2)}) collective-permute-start(bf16[384,1536]{1,0:T(8,128)(2,1)} %get-tuple-element.163), channel_id=1, source_target_pairs={{0,1},{1,0},{2,3},{3,2},{4,5},{5,4},{6,7},{7,6},{8,9},{9,8},{10,11... | collective-permute-start | bytes 3538952 | tf_op jit(solution)/shard_map/ppermute | solution.py:672
  366.2 62.5 %collective-permute-start.29 = (bf16[1024,384]{1,0:T(8,128)(2,1)}, bf16[1024,384]{1,0:T(8,128)(2,1)}, u32[]{:S(2)}, u32[]{:S(2)}) collective-permute-start(bf16[1024,384]{1,0:T(8,128)(2,1)} %get-tuple-element.176), channel_id=1, source_target_pairs={{0,16},{8,24},{16,0},{24,8},{1,17},{9,25},{17,1},{25,9},{2,18},{10... | collective-permute-start | bytes 2359304 | tf_op jit(solution)/shard_map/ppermute | solution.py:672
  434.0 45.2 %collective-permute-start.27 = (bf16[192,1536]{1,0:T(8,128)(2,1)}, bf16[192,1536]{1,0:T(8,128)(2,1)S(1)}, u32[]{:S(2)}, u32[]{:S(2)}) collective-permute-start(bf16[192,1536]{1,0:T(8,128)(2,1)} %get-tuple-element.169), channel_id=1, source_target_pairs={{0,2},{1,3},{2,0},{3,1},{4,6},{5,7},{6,4},{7,5},{8,10},{9,11},{10,... | collective-permute-start | bytes 1769480 | tf_op jit(solution)/shard_map/ppermute | solution.py:672
  435.5 44.6 %collective-permute-start.31 = (bf16[1536,384]{1,0:T(8,128)(2,1)}, bf16[1536,384]{1,0:T(8,128)(2,1)S(1)}, u32[]{:S(2)}, u32[]{:S(2)}) collective-permute-start(bf16[1536,384]{1,0:T(8,128)(2,1)} %get-tuple-element.162), channel_id=1, source_target_pairs={{0,1},{1,0},{2,3},{3,2},{4,5},{5,4},{6,7},{7,6},{8,9},{9,8},{10,11... | collective-permute-start | bytes 3538952 | tf_op jit(solution)/shard_map/ppermute | solution.py:672
  437.0 43.3 %collective-permute-start.32 = (bf16[512,384]{1,0:T(8,128)(2,1)S(1)}, bf16[512,384]{1,0:T(8,128)(2,1)S(1)}, u32[]{:S(2)}, u32[]{:S(2)}) collective-permute-start(bf16[512,384]{1,0:T(8,128)(2,1)S(1)} %get-tuple-element.184), channel_id=1, source_target_pairs={{0,1},{1,0},{2,3},{3,2},{4,5},{5,4},{6,7},{7,6},{8,9},{9,8},{10,11... | collective-permute-start | bytes 1179656 | tf_op jit(solution)/shard_map/ppermute | solution.py:672
  536.1 39.9 %collective-permute-start.43 = (bf16[704,384]{1,0:T(8,128)(2,1)S(1)}, bf16[704,384]{1,0:T(8,128)(2,1)S(1)}, u32[]{:S(2)}, u32[]{:S(2)}) collective-permute-start(bf16[704,384]{1,0:T(8,128)(2,1)S(1)} %get-tuple-element.172), channel_id=1, source_target_pairs={{0,1},{1,0},{2,3},{3,2},{4,5},{5,4},{6,7},{7,6},{8,9},{9,8},{10,11... | collective-permute-start | bytes 1622024 | tf_op jit(solution)/shard_map/ppermute | solution.py:672
  560.7 42.8 %collective-permute-start.55 = (bf16[128,384]{1,0:T(8,128)(2,1)S(1)}, bf16[128,384]{1,0:T(8,128)(2,1)S(1)}, u32[]{:S(2)}, u32[]{:S(2)}) collective-permute-start(bf16[128,384]{1,0:T(8,128)(2,1)S(1)} %add_convert_fusion.22), channel_id=1, source_target_pairs={{0,4},{1,5},{2,6},{3,7},{4,0},{5,1},{6,2},{7,3},{8,12},{9,13},{10,... | collective-permute-start | bytes 294920 | tf_op jit(solution)/shard_map/ppermute | solution.py:672
  605.6 66.6 %collective-permute-start.65 = (bf16[192,1536]{1,0:T(8,128)(2,1)}, bf16[192,1536]{1,0:T(8,128)(2,1)}, u32[]{:S(2)}, u32[]{:S(2)}) collective-permute-start(bf16[192,1536]{1,0:T(8,128)(2,1)} %pad_maximum_fusion.3), channel_id=1, source_target_pairs={{0,2},{1,3},{2,0},{3,1},{4,6},{5,7},{6,4},{7,5},{8,10},{9,11},{10,... | collective-permute-start | bytes 1769480 | tf_op jit(solution)/shard_map/ppermute | solution.py:672
  647.3 81.4 %collective-permute-start.58 = (bf16[512,384]{1,0:T(8,128)(2,1)}, bf16[512,384]{1,0:T(8,128)(2,1)S(1)}, u32[]{:S(2)}, u32[]{:S(2)}) collective-permute-start(bf16[512,384]{1,0:T(8,128)(2,1)} %pad_maximum_fusion.6), channel_id=1, source_target_pairs={{0,1},{1,0},{2,3},{3,2},{4,5},{5,4},{6,7},{7,6},{8,9},{9,8},{10,11... | collective-permute-start | bytes 1179656 | tf_op jit(solution)/shard_map/ppermute | solution.py:672
  648.7 79.8 %collective-permute-start.54 = (bf16[512,384]{1,0:T(8,128)(2,1)}, bf16[512,384]{1,0:T(8,128)(2,1)S(1)}, u32[]{:S(2)}, u32[]{:S(2)}) collective-permute-start(bf16[512,384]{1,0:T(8,128)(2,1)} %pad_maximum_fusion.5), channel_id=1, source_target_pairs={{0,1},{1,0},{2,3},{3,2},{4,5},{5,4},{6,7},{7,6},{8,9},{9,8},{10,11... | collective-permute-start | bytes 1179656 | tf_op jit(solution)/shard_map/ppermute | solution.py:672
  675.8 52.0 %collective-permute-start.51 = (bf16[1536,384]{1,0:T(8,128)(2,1)S(1)}, bf16[1536,384]{1,0:T(8,128)(2,1)S(1)}, u32[]{:S(2)}, u32[]{:S(2)}) collective-permute-start(bf16[1536,384]{1,0:T(8,128)(2,1)S(1)} %pad_maximum_fusion), channel_id=1, source_target_pairs={{0,1},{1,0},{2,3},{3,2},{4,5},{5,4},{6,7},{7,6},{8,9},{9,8},{10,11... | collective-permute-start | bytes 3538952 | tf_op jit(solution)/shard_map/ppermute | solution.py:672
  680.9 55.5 %collective-permute-start.63 = (bf16[704,384]{1,0:T(8,128)(2,1)S(1)}, bf16[704,384]{1,0:T(8,128)(2,1)S(1)}, u32[]{:S(2)}, u32[]{:S(2)}) collective-permute-start(bf16[704,384]{1,0:T(8,128)(2,1)S(1)} %pad_maximum_fusion.4), channel_id=1, source_target_pairs={{0,1},{1,0},{2,3},{3,2},{4,5},{5,4},{6,7},{7,6},{8,9},{9,8},{10,11... | collective-permute-start | bytes 1622024 | tf_op jit(solution)/shard_map/ppermute | solution.py:672
  (106 other events, 2094.1 us)

commit v2 on v1

--- a/solution.py
+++ b/solution.py
@@ -706,12 +706,13 @@
     def side(self, chunk):
         self.across[chunk] = swap(self.there[chunk], "rep", 1, self.copies)
 
-    def finish(self):
+    def finish(self, *deps):
         have = {0: [(0, None, 0, self.shard)]}
         have[2] = [(c * self.rows, h, self.half, v) for h, vs in ((0, self.there), (1, self.across))
                    for c, v in enumerate(vs)]
         for source in (0, 2):
-            have[source ^ 1] = [(r, h, s, swap(v, "shard", 1, self.groups)) for r, h, s, v in have[source]]
+            have[source ^ 1] = [(r, h, s, swap(after(v, *deps) if v is self.across[-1] else v, "shard", 1, self.groups))
+                                for r, h, s, v in have[source]]
         pieces, arrays = [], []
         for position, source in enumerate(self.order):
             for row, half, size, value in have[source]:
@@ -724,52 +725,73 @@
 
 
 class Total:
-    def __init__(self, kept, sent, axis, rep_index, groups, copies):
+    def __init__(self, kept, sent, axis, rep_index, groups, copies, narrow=False):
         self.axis, self.rep_index = axis, rep_index
-        self.stages = [("shard", bit, groups) for bit in bits_of(groups)]
-        self.stages += [("rep", bit, copies) for bit in bits_of(copies)]
-        self.back = list(reversed(self.stages[len(bits_of(groups)) :]))
-        self.value, self.out = kept, sent
+        self.sizes = {"shard": groups, "rep": copies}
+        self.stages = [("shard", index, 1) for index in range(len(bits_of(groups)))]
+        count = len(bits_of(copies))
+        over = [("rep", 0, 1)] + [("rep", index, min(2, count - index)) for index in range(1, count, 2)]
+        self.stages += over
+        self.back = list(reversed(over))
+        if narrow:
+            self.back = [(name, shift + bit, 1) for name, shift, width in self.back for bit in range(width)]
+        self.value, self.out = kept, [sent]
         self.fly()
 
+    @classmethod
+    def join(cls, chains):
+        first = chains[0]
+        new = object.__new__(cls)
+        new.axis, new.rep_index, new.sizes = first.axis, first.rep_index, first.sizes
+        new.stages, new.back = first.stages, first.back
+        new.value = jnp.concatenate([v.value for v in chains])
+        new.coming = [jnp.concatenate(v) for v in zip(*(c.coming for c in chains))]
+        return new
+
     def fly(self):
-        self.coming = swap(self.out, *self.stages[0])
+        name, shift, _ = self.stages[0]
+        self.coming = [swap(v, name, (k + 1) << shift, self.sizes[name]) for k, v in enumerate(self.out)]
+
+    def done(self):
+        return not self.stages and not self.back
 
     def step(self, *deps):
-        coming = after(self.coming, *deps)
+        coming = [after(v, *deps) for v in self.coming]
+        if not self.stages:
+            return self.widen(coming)
         self.stages.pop(0)
-        value = self.value
+        terms = [self.value] + coming
         if not self.stages:
-            self.value = (value.astype(F32) + coming.astype(F32)).astype(BF16)
-            self.out = self.value
-            return self.out
-        name, bit, _ = self.stages[0]
-        if name == "shard":
-            half = value.shape[self.axis] // 2
-            low, high = 0, half
-            axis = self.axis
-        else:
-            half = value.shape[0] // 2
-            turn = (self.rep_index & bit) != 0
-            low = jnp.where(turn, half, 0)
-            high = half - low
-            axis = 0
-        cut = lambda v, start: lax.dynamic_slice_in_dim(v, start, half, axis).astype(F32)
-        self.out = (cut(value, high) + cut(coming, high)).astype(BF16)
-        self.value = cut(value, low) + cut(coming, low)
+            self.value = sum(v.astype(F32) for v in terms).astype(BF16)
+            self.fly_back()
+            return [self.value]
+        name, shift, width = self.stages[0]
+        parts = 1 << width
+        axis = self.axis if name == "shard" else 0
+        size = self.value.shape[axis] // parts
+        mine = 0 if name == "shard" else (self.rep_index >> shift) & (parts - 1)
+        cut = lambda start: sum(lax.dynamic_slice_in_dim(v, start, size, axis).astype(F32) for v in terms)
+        self.out = [cut((mine ^ k) * size).astype(BF16) for k in range(1, parts)]
+        self.value = cut(mine * size)
         self.fly()
         return self.out
 
-    def widen(self, *deps):
-        name, bit, size = self.back.pop(0)
-        other = swap(after(self.value, *deps), name, bit, size)
-        turn = (self.rep_index & bit) != 0
-        low, high = jnp.where(turn, other, self.value), jnp.where(turn, self.value, other)
-        if self.back:
-            self.value = jnp.concatenate([low, high])
-        else:
-            self.value = [low.astype(F32), high.astype(F32)]
-        return self.value
+    def fly_back(self):
+        name, shift, width = self.back[0]
+        self.coming = [swap(self.value, name, k << shift, self.sizes[name]) for k in range(1, 1 << width)]
+
+    def widen(self, coming):
+        name, shift, width = self.back.pop(0)
+        parts = [self.value] + coming
+        for bit in range(width):
+            turn = ((self.rep_index >> (shift + bit)) & 1) != 0
+            parts = [jnp.where(turn, parts[k ^ (1 << bit)], parts[k]) for k in range(len(parts))]
+        if not self.back:
+            self.value = [v.astype(F32) for v in parts]
+            return self.value
+        self.value = jnp.concatenate(parts)
+        self.fly_back()
+        return [self.value]
 
 
 def outer(left, right):
@@ -804,13 +826,11 @@
     small = (norm_gain, conv_bias, dt_bias, a_log, skip, gate_gain, conv_weight)
     packed = jnp.concatenate([v.reshape(-1) for v in small])
     wc.far(0)
-    wc.far(1, wc.there[0])
+    wc.far(1)
     wc.side(0)
     wc.side(1)
     wg.far(0, wc.there[1])
-    ow.far(0, wc.across[1])
-    wg.side(0)
-    ow.side(0)
+    ow.far(0, wc.there[1])
     rows = [packed, swap(packed, "shard", 1, groups)]
     far = swap(packed, "shard", 2, groups)
     rows += [far, swap(far, "shard", 1, groups)]
@@ -829,70 +849,60 @@
     skip_cols = jnp.repeat(sk, inner // heads)[None]
     pick = (jnp.arange(inner)[:, None] // (inner // heads) == jnp.arange(LANES)[None]).astype(BF16)
 
-    wc, wg, ow = wc.finish(), wg.finish(), ow.finish()
+    wc = wc.finish(gain, cb, gg, cw, vec, skip_cols, pick)
     normed, proj = run_project_in(place, tok, gain, wc, total, order)
+    for weight in (wg, ow):
+        weight.there[0] = after(weight.there[0], normed)
+        weight.side(0)
+    proj = after(proj, wg.there[0], ow.there[0])
     per = 8
     scan_out, sums, starts = run_scan_forward(proj, cw, cb, vec, skip_cols, inner, nstate, heads // per, per)
+    wg, ow = wg.finish(scan_out), ow.finish(scan_out)
     mixed, dscan, dgate, dgg = run_gating(place, normed, wg, ow, cot, scan_out, gg, order)
 
-    chain = lambda kept, sent, axis: Total(kept, sent, axis, rep_index, groups, copies)
+    chain = lambda kept, sent, axis, *way: Total(kept, sent, axis, rep_index, groups, copies, *way)
     half = inner // 2
     out_sent = outer(mixed[:, half:], cot)
     o = chain(outer(mixed[:, :half], cot), out_sent, 0)
     half = model // 2
     left, right = normed[:, :half], normed[:, half:]
     gate_sent = outer(dgate, right)
-    g = chain(outer(dgate, left), gate_sent, 1)
+    marks = o.step(gate_sent)
+    g = chain(outer(after(dgate, *marks), left), gate_sent, 1, True)
+    marks = marks + g.step(g.value)
 
     blocks = heads // per
     cuts = [blocks * v // 3 for v in range(4)]
-    marks = [o.step(g.value)]
-    marks.append(g.step(*marks))
     chains, grads, carried = [o, g], [], None
     for index in range(3):
         low, high = cuts[index], cuts[index + 1]
-        last = index == 2
         found = run_scan_backward(
             proj, sums, scan_out, after(dscan, *marks), starts, cw, vec, skip_cols, pick, inner, nstate, low,
-            high - low, per, carried, last)
+            high - low, per, carried, index == 2)
         grads.append(found[:5])
         carried = tuple(found[5:])
-        marks = []
-        for old in chains[: 1 if index == 0 else None]:
-            marks.append(old.step(found[0], *marks))
-        dproj = after(found[0], *marks)
+        dproj, marks = found[0], []
+        if index == 1:
+            marks = o.step(dproj)
+        if index == 2:
+            ab = Total.join(chains[2:])
+            marks = o.coming + g.step(dproj, *o.coming)
+            marks = marks + ab.step(dproj, *marks)
+        dproj = after(dproj, *marks)
         sent = outer(dproj, right)
         kept = outer(dproj, left)
         new = chain(kept, sent, 1)
-        marks.append(new.step(kept))
+        marks = marks + new.step(kept)
+        if index < 2:
+            marks = marks + (o, g)[index].step(kept, *marks)
         chains.append(new)
-
-    def exchange(value):
-        for axis, size in (("shard", groups), ("rep", copies)):
-            for bit in bits_of(size):
-                value = value + swap(value, axis, bit, size)
-        return value
-
-    def advance(*fence):
-        moved = []
-        for old in chains:
-            if old.stages:
-                moved.append(old.step(*fence, *moved))
-            elif old.back:
-                old.widen(*fence)
-        return moved
-
-    output = run_project_out(place, after(mixed, *marks), tok, ow)
-    marks = advance(output)
+    c = chains[4]
+
     part = run_gate_back(place, after(dgate, *marks), model, wg)
-    marks = advance(part)
+    marks = g.coming + ab.coming
+    marks = marks + o.step(part, *marks)
+    marks = marks + c.step(part, *marks)
     input_grad, dgain = run_input_back(place, after(part, *marks), [v[0] for v in grads], tok, cot, gain, wc, order)
-    advance(dgain)
-    while any(old.stages or old.back for old in chains):
-        advance()
-
-    in_total = jnp.concatenate([v for old in chains[1:] for v in old.value])[:outputs_all].T
-    out_total = jnp.concatenate(o.value)
 
     dcw = jnp.concatenate([v[1] for v in grads], axis=1)
     dcb = jnp.concatenate([v[2][0] for v in grads])
@@ -901,7 +911,32 @@
     pieces = (dcb, dvec[0, :heads], dvec[1, :heads], dskip, dgg[0])
     flat = jnp.concatenate([v.reshape(groups, -1) for v in pieces]
                            + [dcw.reshape(taps, groups, -1).transpose(1, 0, 2).reshape(groups, -1)], axis=1)
-    flat = exchange(jnp.concatenate([dgain[0].reshape(groups, -1), flat], axis=1))
+    flat = jnp.concatenate([dgain[0].reshape(groups, -1), flat], axis=1)
+    abc = Total.join([ab, c])
+    marks = abc.step(dgain, *o.coming)
+    marks = marks + g.step(*marks)
+    marks = marks + o.step(*marks)
+    flat = after(flat, *marks)
+    for bit in bits_of(groups):
+        flat = flat + swap(flat, "shard", bit, groups)
+    output = run_project_out(place, after(mixed, flat, *marks), tok, ow)
+    marks = o.coming + abc.coming
+    marks = marks + g.step(output, *marks)
+    marks = marks + abc.step(output, *marks)
+    flat = after(flat, *marks)
+    for bit in bits_of(copies):
+        flat = flat + swap(flat, "rep", bit, copies)
+    chains = [o, g, abc]
+    while not all(old.done() for old in chains):
+        for old in (g, abc, o):
+            if not old.done():
+                old.step()
+
+    cut = ab.value.shape[0]
+    halves = [v[:cut] for v in abc.value] + [v[cut:] for v in abc.value]
+    in_total = jnp.concatenate(g.value + halves)[:outputs_all].T
+    out_total = jnp.concatenate(o.value)
+
     own = lax.dynamic_slice_in_dim(flat, shard_index, 1, 0)[0]
     shares, low = [], 0
     for v in small:

time: 750 us -> 662 us (0.88)
  waiting for transfers between devices: 235 us -> 167 us
  local copies, waits for them, and re-layouts: 43.8 us -> 32.5 us
  other arithmetic: 59.5 us -> 51.6 us
    ppermute x67 -> x61, waiting for transfers between devices: 235 us -> 167 us  [swap(): return lax.ppermute(value, axis, [(i, i ^ bit) for i in range(size)])]
    ppermute x67 -> x61, starting transfers between devices: 67.1 us -> 60.1 us  [swap(): return lax.ppermute(value, axis, [(i, i ^ bit) for i in range(size)])]
    convert_element_type x13 -> x10, other arithmetic: 14.4 us -> 20.3 us  [the longest x6 14.7 us: step(): self.out = [cut((mine ^ k) * size).astype(BF16) for k in range(1, parts)]]
    add x17 -> x11, other arithmetic: 18.6 us -> 14.5 us  [the longest x6 12.8 us: step(): sum((lax.dynamic_slice_in_dim(v, start, size, axis).astype(F32) for v in...]
  transfers between devices with their start and end apart: 67 -> 61, of which waited for: 21 -> 17; matrix products, arithmetic and copies ran while one was open for 16% -> 16% of each run, Pallas kernels for 32% -> 37%
where the time goes in v2:
time: 662 us; the launch traced here: 654 us
  Pallas kernels  282 us (43%)
  waiting for transfers between devices  167 us (25%)
  starting transfers between devices  60.1 us (9%)
  matrix products  59.1 us (9%)
  other arithmetic  51.6 us (8%)
  local copies, waits for them, and re-layouts  32.5 us (5%)
    ppermute x61, waiting for transfers between devices, swap(): return lax.ppermute(value, axis, [(i, i ^ bit) for i in range(size)])  167 us
    pallas_call x3, Pallas kernels, run_scan_backward(): pl.pallas_call(functools.partial(scan_backward, nstate=nstate, low=low, g...  97.7 us
    ppermute x61, starting transfers between devices, swap(): return lax.ppermute(value, axis, [(i, i ^ bit) for i in range(size)])  60.1 us
    dot_general x10, matrix products, outer(): lax.dot_general(left, right, (((0,), (0,)), ((), ())), preferred_element_...  59.1 us
    pallas_call x1, Pallas kernels, run_scan_forward(): pl.pallas_call(functools.partial(scan_forward, inner=inner, nstate=nstate...  48.7 us
    pallas_call x1, Pallas kernels, run_gating(): pl.pallas_call(functools.partial(gating, wg_pieces=wg_pieces, ow_pieces=o...  42.4 us
    pallas_call x1, Pallas kernels, run_input_back(): pl.pallas_call(functools.partial(input_back, count=len(dprojs), pieces=pi...  27.4 us
    pallas_call x1, Pallas kernels, run_project_in(): pl.pallas_call(functools.partial(project_in, pieces=pieces, order=order),...  24.2 us
  transfers between devices with their start and end apart: 61, of which 17 were waited for; matrix products, arithmetic and copies ran while one was open for 16% of the time, Pallas kernels for 37%

profile of v2, /device:TPU:0, one launch (start us, length us, event | category | flops | bytes accessed | tf_op | source)
XLA Modules:
  0.0 653.6 jit_solution(7929971560076448320)
XLA Ops:
  21.0 8.9 %collective-permute-done.3.rest_1_.rest_4_ = bf16[864,384]{1,0:T(8,128)(2,1)} collective-permute-done((bf16[864,384]{1,0:T(8,128)(2,1)}, bf16[864,384]{1,0:T(8,128)(2,1)}, u32[]{:S(2)}, u32[]{:S(2)}) %collective-permute-start.3) | collective-permute-done | bytes 663584 | tf_op jit(solution)/shard_map/ppermute | solution.py:672
  31.5 12.2 %collective-permute-done.4.rest_2_.rest_5_ = bf16[864,384]{1,0:T(8,128)(2,1)} collective-permute-done((bf16[864,384]{1,0:T(8,128)(2,1)}, bf16[864,384]{1,0:T(8,128)(2,1)}, u32[]{:S(2)}, u32[]{:S(2)}) %collective-permute-start.4) | collective-permute-done | bytes 663584 | tf_op jit(solution)/shard_map/ppermute | solution.py:672
  50.1 10.4 %collective-permute-done.6.rest_4_.rest_7_ = bf16[864,384]{1,0:T(8,128)(2,1)} collective-permute-done((bf16[864,384]{1,0:T(8,128)(2,1)}, bf16[864,384]{1,0:T(8,128)(2,1)}, u32[]{:S(2)}, u32[]{:S(2)}) %collective-permute-start.6) | collective-permute-done | bytes 663584 | tf_op jit(solution)/shard_map/ppermute | solution.py:672
  67.2 24.2 %project_in.1 = (bf16[1024,1536]{1,0:T(8,128)(2,1)}, f32[1024,3456]{1,0:T(8,128)}) custom-call(s32[2]{0:T(128)S(1)} %pad_add_fusion.place_ref, bf16[1024,1536]{1,0:T(8,128)(2,1)} %bitcast.45, f32[1,1536]{1,0:T(1,128)S(1)} %bitcast.41, bf16[3456,384]{1,0:T(8,128)(2,1)} %pad.8.rest_0_.rest_3_, bf16[864,384]{1,0:T(8,128)(2,1)} %collective-permute-done.3.rest_1_.rest_4_, ...), custom_call_target="tpu_custom_call" | custom-call | flops 20000000000 | bytes 30000000 | tf_op jit(solution)/shard_map/project_in/pallas_call | solution.py:222
  95.7 22.9 %collective-permute-done.13.rest_7_.rest_1_ = bf16[384,1536]{1,0:T(8,128)(2,1)} collective-permute-done((bf16[384,1536]{1,0:T(8,128)(2,1)S(1)}, bf16[384,1536]{1,0:T(8,128)(2,1)}, u32[]{:S(2)}, u32[]{:S(2)}) %collective-permute-start.13) | collective-permute-done | bytes 1179680 | tf_op jit(solution)/shard_map/ppermute | solution.py:672
  120.6 48.7 %scan_forward.1 = (f32[1024,3072]{1,0:T(8,128)}, f32[1024,3328]{1,0:T(8,128)}, bf16[1024,3072]{1,0:T(8,128)(2,1)}) custom-call(f32[1024,3456]{1,0:T(8,128)} %get-tuple-element.94.proj_ref.tail_ref, f32[4,3328]{1,0:T(4,128)} %reshape.119.cw_ref.cwk_ref, f32[1,3328]{1,0:T(1,128)} %broadcast_in_dim_reshape.13.cb_ref, f32[8,128]{1,0:T(8,128)} %select_maximum_fusion.vec_ref, ...), custom_call_target="tpu_custom_call" | custom-call | flops 12000000000 | bytes 60000000 | tf_op jit(solution)/shard_map/scan_forward/pallas_call | solution.py:127
  175.9 42.4 %gating.1 = (bf16[1024,3072]{1,0:T(8,128)(2,1)}, f32[1024,3072]{1,0:T(8,128)}, bf16[1024,3072]{1,0:T(8,128)(2,1)}, f32[1,3072]{1,0:T(1,128)}) custom-call(s32[2]{0:T(128)} %copy-done.6, bf16[1024,1536]{1,0:T(8,128)(2,1)} %get-tuple-element.88.normed_ref, bf16[1024,1536]{1,0:T(8,128)(2,1)} %bitcast.53, f32[1024,3072]{1,0:T(8,128)} %get-tuple-element.95.scan_ref.out_ref, ...), custom_call_target="tpu_custom_call" | custom-call | flops 40000000000 | bytes 70000000 | tf_op jit(solution)/shard_map/gating/pallas_call | solution.py:305
  218.3 7.8 %convolution_convert_fusion = bf16[1536,1536]{1,0:T(8,128)(2,1)S(1)} fusion(bf16[1024,3072]{1,0:T(8,128)(2,1)} %get-tuple-element.156.mixed_ref, bf16[1,1024,1536]{2,1,0:T(8,128)(2,1)} %param.21), kind=kOutput, calls=%fused_computation.1 | convolution fusion | flops 4834197504 | bytes 11010048 | tf_op jit(solution)/shard_map/dot_general | solution.py:798
  226.3 8.7 %convolution_convert_fusion.3 = bf16[3072,768]{1,0:T(8,128)(2,1)S(1)} fusion(bf16[1024,3072]{1,0:T(8,128)(2,1)} %get-tuple-element.128.dgate_ref, bf16[1024,1536]{1,0:T(8,128)(2,1)S(1)} %copy-done.47), kind=kOutput, calls=%fused_computation.4 | convolution fusion | flops 4834197504 | bytes 12582912 | tf_op jit(solution)/shard_map/dot_general | solution.py:798
  235.5 7.7 %convolution_convert_fusion.1 = bf16[1536,1536]{1,0:T(8,128)(2,1)S(1)} fusion(bf16[1024,3072]{1,0:T(8,128)(2,1)} %get-tuple-element.156.mixed_ref, bf16[1,1024,1536]{2,1,0:T(8,128)(2,1)S(1)} %copy-done.46), kind=kOutput, calls=%fused_computation.2 | convolution fusion | flops 4834197504 | bytes 11010048 | tf_op jit(solution)/shard_map/dot_general | solution.py:798
  247.3 8.5 %convolution_convert_fusion.2 = bf16[3072,768]{1,0:T(8,128)(2,1)S(1)} fusion(bf16[1024,3072]{1,0:T(8,128)(2,1)} %get-tuple-element.128.dgate_ref, bf16[1024,1536]{1,0:T(8,128)(2,1)S(1)} %copy-done.47), kind=kOutput, calls=%fused_computation.3 | convolution fusion | flops 4834197504 | bytes 12582912 | tf_op jit(solution)/shard_map/dot_general | solution.py:798
  259.4 31.4 %scan_backward.3 = (bf16[1024,1024]{1,0:T(8,128)(2,1)}, f32[4,1024]{1,0:T(4,128)S(1)}, f32[1,1024]{1,0:T(1,128)S(1)}, f32[1,1024]{1,0:T(1,128)S(1)}, f32[8,128]{...) custom-call(f32[1024,3456]{1,0:T(8,128)} %get-tuple-element.94.proj_ref.tail_ref, ...), custom_call_target="tpu_custom_call" | custom-call | flops 40000000000 | bytes 40000000 | tf_op jit(solution)/shard_map/scan_backward/pallas_call | solution.py:636
  290.9 5.4 convolution_convert_fusion.8
  308.1 31.8 %scan_backward.4 = (bf16[1024,1024]{1,0:T(8,128)(2,1)}, f32[4,1024]{1,0:T(4,128)S(1)}, f32[1,1024]{1,0:T(1,128)S(1)}, f32[1,1024]{1,0:T(1,128)S(1)}, f32[8,128]{...) custom-call(f32[1024,3456]{1,0:T(8,128)} %get-tuple-element.94.proj_ref.tail_ref, ...), custom_call_target="tpu_custom_call" | custom-call | flops 40000000000 | bytes 40000000 | tf_op jit(solution)/shard_map/scan_backward/pallas_call | solution.py:636
  362.8 4.9 collective-permute-done.33
  368.6 34.4 %scan_backward.5 = (bf16[1024,1408]{1,0:T(8,128)(2,1)}, f32[4,1280]{1,0:T(4,128)S(1)}, f32[1,1280]{1,0:T(1,128)S(1)}, f32[1,1024]{1,0:T(1,128)S(1)}, f32[8,128]{1,0:T(8,128)S(1)}) custom-call(f32[1024,3456]{1,0:T(8,128)} %get-tuple-element.94.proj_ref.tail_ref, f32[1024,3456]{1,0:T(8,128)} %get-tuple-element.94.proj_ref.tail_ref, ...), custom_call_target="tpu_custom_call" | custom-call | flops 40000000000 | bytes 40000000 | tf_op jit(solution)/shard_map/scan_backward/pallas_call | solution.py:636
  422.3 4.7 convolution_convert_fusion.5
  430.9 20.5 %gate_back.1.part_ref = f32[1024,1536]{1,0:T(8,128)} custom-call(s32[2]{0:T(128)S(1)} %copy-done.7, bf16[1024,3072]{1,0:T(8,128)(2,1)} %get-tuple-element.128.dgate_ref, bf16[3072,384]{1,0:T(8,128)(2,1)S(1)} %copy-done.1, bf16[1536,384]{1,0:T(8,128)(2,1)} %collective-permute-done.12.rest_1_, bf16[1536,384]{1,0:T(8,128)(2,1)} %collective-permute-done.14.rest_2_, ...), custom_call_target="tpu_custom_call" | custom-call | flops 16000000000 | bytes 22000000 | tf_op jit(solution)/shard_map/gate_back/pallas_call | solution.py:344
  460.5 27.4 %input_back.1 = (f32[1024,1536]{1,0:T(8,128)}, f32[1,1536]{1,0:T(1,128)S(1)}) custom-call(s32[2]{0:T(128)S(1)} %copy-done.7, f32[1024,1536]{1,0:T(8,128)} %gate_back.1.part_ref, bf16[1024,1536]{1,0:T(8,128)(2,1)} %bitcast.46, bf16[1024,1536]{1,0:T(8,128)(2,1)} %bitcast.54, f32[1,1536]{1,0:T(1,128)S(1)} %bitcast.42, ...), custom_call_target="tpu_custom_call" | custom-call | flops 22000001024 | bytes 46000000 | tf_op jit(solution)/shard_map/input_back/pallas_call | solution.py:400
  506.0 20.8 %project_out.1 = bf16[1024,1536]{1,0:T(8,128)(2,1)} custom-call(s32[2]{0:T(128)S(1)} %copy-done.7, bf16[1024,3072]{1,0:T(8,128)(2,1)} %get-tuple-element.156.mixed_ref, bf16[1024,1536]{1,0:T(8,128)(2,1)S(1)} %bitcast.47, bf16[768,1536]{1,0:T(8,128)(2,1)} %rest_0_.1, bf16[384,1536]{1,0:T(8,128)(2,1)} %collective-permute-done.13.rest_7_.rest_1_, ...), custom_call_target="tpu_custom_call" | custom-call | flops 14000000000 | bytes 20000000 | tf_op jit(solution)/shard_map/project_out/pallas_call | solution.py:435
  549.1 21.7 %collective-permute-done.53 = f32[4,5348]{1,0:T(4,128)S(1)} collective-permute-done((f32[4,5348]{1,0:T(4,128)S(1)}, f32[4,5348]{1,0:T(4,128)S(1)}, u32[]{:S(2)}, u32[]{:S(2)}) %collective-permute-start.53) | collective-permute-done | bytes 85600 | tf_op jit(solution)/shard_map/ppermute | solution.py:672
  573.3 18.8 %collective-permute-done.58 = bf16[432,384]{1,0:T(8,128)(2,1)S(1)} collective-permute-done((bf16[432,384]{1,0:T(8,128)(2,1)S(1)}, bf16[432,384]{1,0:T(8,128)(2,1)S(1)}, u32[]{:S(2)}, u32[]{:S(2)}) %collective-permute-start.58) | collective-permute-done | bytes 331808 | tf_op jit(solution)/shard_map/ppermute | solution.py:672
  600.3 25.4 %collective-permute-done.60 = bf16[1728,384]{1,0:T(8,128)(2,1)S(1)} collective-permute-done((bf16[1728,384]{1,0:T(8,128)(2,1)}, bf16[1728,384]{1,0:T(8,128)(2,1)S(1)}, u32[]{:S(2)}, u32[]{:S(2)}) %collective-permute-start.60) | collective-permute-done | bytes 1327136 | tf_op jit(solution)/shard_map/ppermute | solution.py:672
  626.1 21.8 %collective-permute-done.56 = bf16[1536,384]{1,0:T(8,128)(2,1)S(1)} collective-permute-done((bf16[1536,384]{1,0:T(8,128)(2,1)S(1)}, bf16[1536,384]{1,0:T(8,128)(2,1)S(1)}, u32[]{:S(2)}, u32[]{:S(2)}) %collective-permute-start.56) | collective-permute-done | bytes 1179680 | tf_op jit(solution)/shard_map/ppermute | solution.py:672
  (325 shorter events, 180.0 us)
Async XLA Ops:
  15.6 51.6 %collective-permute-start.7 = (bf16[3456,384]{1,0:T(8,128)(2,1)}, bf16[3456,384]{1,0:T(8,128)(2,1)}, u32[]{:S(2)}, u32[]{:S(2)}) collective-permute-start(bf16[3456,384]{1,0:T(8,128)(2,1)} %pad.8.rest_0_.rest_3_), channel_id=1, source_target_pairs={{0,8},{8,0},{16,24},{24,16},{1,9},{9,1},{17,25},{25,17},{2,10},{10... | collective-permute-start | bytes 7962632 | tf_op jit(solution)/shard_map/ppermute | solution.py:672
  64.6 105.2 %collective-permute-start.15 = (bf16[3072,384]{1,0:T(8,128)(2,1)S(1)}, bf16[3072,384]{1,0:T(8,128)(2,1)}, u32[]{:S(2)}, u32[]{:S(2)}) collective-permute-start(bf16[3072,384]{1,0:T(8,128)(2,1)S(1)} %slice.136.rest_0_), channel_id=1, source_target_pairs={{0,8},{8,0},{16,24},{24,16},{1,9},{9,1},{17,25},{25,17},{2,10},{10... | collective-permute-start | bytes 7077896 | tf_op jit(solution)/shard_map/ppermute | solution.py:672
  65.7 52.9 %collective-permute-start.13 = (bf16[384,1536]{1,0:T(8,128)(2,1)S(1)}, bf16[384,1536]{1,0:T(8,128)(2,1)}, u32[]{:S(2)}, u32[]{:S(2)}) collective-permute-start(bf16[384,1536]{1,0:T(8,128)(2,1)S(1)} %constant_dynamic-slice_fusion), channel_id=1, source_target_pairs={{0,16},{8,24},{16,0},{24,8},{1,17},{9,25},{17,1},{25,9},{2,18},{10... | collective-permute-start | bytes 3538952 | tf_op jit(solution)/shard_map/ppermute | solution.py:672
  94.2 75.1 %collective-permute-start.14 = (bf16[1536,384]{1,0:T(8,128)(2,1)}, bf16[1536,384]{1,0:T(8,128)(2,1)}, u32[]{:S(2)}, u32[]{:S(2)}) collective-permute-start(bf16[1536,384]{1,0:T(8,128)(2,1)} %collective-permute-done.12.rest_1_), channel_id=1, source_target_pairs={{0,1},{1,0},{2,3},{3,2},{4,5},{5,4},{6,7},{7,6},{8,9},{9,8},{10,11... | collective-permute-start | bytes 3538952 | tf_op jit(solution)/shard_map/ppermute | solution.py:672
  118.6 50.8 %collective-permute-start.18 = (bf16[384,1536]{1,0:T(8,128)(2,1)}, bf16[384,1536]{1,0:T(8,128)(2,1)}, u32[]{:S(2)}, u32[]{:S(2)}) collective-permute-start(bf16[384,1536]{1,0:T(8,128)(2,1)} %collective-permute-done.13.rest_7_.rest_1_), channel_id=1, source_target_pairs={{0,1},{1,0},{2,3},{3,2},{4,5},{5,4},{6,7},{7,6},{8,9},{9,8},{10,11... | collective-permute-start | bytes 3538952 | tf_op jit(solution)/shard_map/ppermute | solution.py:672
  120.1 49.9 %collective-permute-start.19 = (bf16[768,1536]{1,0:T(8,128)(2,1)}, bf16[768,1536]{1,0:T(8,128)(2,1)}, u32[]{:S(2)}, u32[]{:S(2)}) collective-permute-start(bf16[768,1536]{1,0:T(8,128)(2,1)} %rest_0_.1), channel_id=1, source_target_pairs={{0,8},{8,0},{16,24},{24,16},{1,9},{9,1},{17,25},{25,17},{2,10},{10... | collective-permute-start | bytes 7077896 | tf_op jit(solution)/shard_map/ppermute | solution.py:672
  120.1 49.9 %collective-permute-start.16 = (bf16[1536,384]{1,0:T(8,128)(2,1)}, bf16[1536,384]{1,0:T(8,128)(2,1)}, u32[]{:S(2)}, u32[]{:S(2)}) collective-permute-start(bf16[1536,384]{1,0:T(8,128)(2,1)} %collective-permute-done.12.rest_1_), channel_id=1, source_target_pairs={{0,8},{8,0},{16,24},{24,16},{1,9},{9,1},{17,25},{25,17},{2,10},{10... | collective-permute-start | bytes 3538952 | tf_op jit(solution)/shard_map/ppermute | solution.py:672
  246.8 56.9 %collective-permute-start.23 = (bf16[768,1536]{1,0:T(8,128)(2,1)}, bf16[768,1536]{1,0:T(8,128)(2,1)}, u32[]{:S(2)}, u32[]{:S(2)}) collective-permute-start(bf16[768,1536]{1,0:T(8,128)(2,1)} %get-tuple-element.167), channel_id=1, source_target_pairs={{0,16},{8,24},{16,0},{24,8},{1,17},{9,25},{17,1},{25,9},{2,18},{10... | collective-permute-start | bytes 7077896 | tf_op jit(solution)/shard_map/ppermute | solution.py:672
  296.4 61.6 %collective-permute-start.30 = (bf16[3072,384]{1,0:T(8,128)(2,1)}, bf16[3072,384]{1,0:T(8,128)(2,1)}, u32[]{:S(2)}, u32[]{:S(2)}) collective-permute-start(bf16[3072,384]{1,0:T(8,128)(2,1)} %get-tuple-element.166), channel_id=1, source_target_pairs={{0,16},{8,24},{16,0},{24,8},{1,17},{9,25},{17,1},{25,9},{2,18},{10... | collective-permute-start | bytes 7077896 | tf_op jit(solution)/shard_map/ppermute | solution.py:672
  307.5 32.4 %collective-permute-start.26 = (bf16[384,1536]{1,0:T(8,128)(2,1)S(1)}, bf16[384,1536]{1,0:T(8,128)(2,1)S(1)}, u32[]{:S(2)}, u32[]{:S(2)}) collective-permute-start(bf16[384,1536]{1,0:T(8,128)(2,1)S(1)} %get-tuple-element.171), channel_id=1, source_target_pairs={{0,1},{1,0},{2,3},{3,2},{4,5},{5,4},{6,7},{7,6},{8,9},{9,8},{10,11... | collective-permute-start | bytes 3538952 | tf_op jit(solution)/shard_map/ppermute | solution.py:672
  347.9 55.3 %collective-permute-start.27 = (bf16[96,1536]{1,0:T(8,128)(2,1)}, bf16[96,1536]{1,0:T(8,128)(2,1)S(1)}, u32[]{:S(2)}, u32[]{:S(2)}) collective-permute-start(bf16[96,1536]{1,0:T(8,128)(2,1)} %get-tuple-element.185), channel_id=1, source_target_pairs={{0,2},{1,3},{2,0},{3,1},{4,6},{5,7},{6,4},{7,5},{8,10},{9,11},{10,... | collective-permute-start | bytes 884744 | tf_op jit(solution)/shard_map/ppermute | solution.py:672
  349.4 53.8 %collective-permute-start.28 = (bf16[96,1536]{1,0:T(8,128)(2,1)}, bf16[96,1536]{1,0:T(8,128)(2,1)S(1)}, u32[]{:S(2)}, u32[]{:S(2)}) collective-permute-start(bf16[96,1536]{1,0:T(8,128)(2,1)} %get-tuple-element.184), channel_id=1, source_target_pairs={{0,4},{1,5},{2,6},{3,7},{4,0},{5,1},{6,2},{7,3},{8,12},{9,13},{10,... | collective-permute-start | bytes 884744 | tf_op jit(solution)/shard_map/ppermute | solution.py:672
  356.0 47.3 %collective-permute-start.29 = (bf16[96,1536]{1,0:T(8,128)(2,1)S(1)}, bf16[96,1536]{1,0:T(8,128)(2,1)S(1)}, u32[]{:S(2)}, u32[]{:S(2)}) collective-permute-start(bf16[96,1536]{1,0:T(8,128)(2,1)S(1)} %copy-done.43), channel_id=1, source_target_pairs={{0,6},{1,7},{2,4},{3,5},{4,2},{5,3},{6,0},{7,1},{8,14},{9,15},{10,... | collective-permute-start | bytes 884744 | tf_op jit(solution)/shard_map/ppermute | solution.py:672
  361.4 41.8 %collective-permute-start.32 = (bf16[1536,384]{1,0:T(8,128)(2,1)S(1)}, bf16[1536,384]{1,0:T(8,128)(2,1)S(1)}, u32[]{:S(2)}, u32[]{:S(2)}) collective-permute-start(bf16[1536,384]{1,0:T(8,128)(2,1)S(1)} %get-tuple-element.169), channel_id=1, source_target_pairs={{0,1},{1,0},{2,3},{3,2},{4,5},{5,4},{6,7},{7,6},{8,9},{9,8},{10,11... | collective-permute-start | bytes 3538952 | tf_op jit(solution)/shard_map/ppermute | solution.py:672
  367.7 35.4 %collective-permute-start.34 = (bf16[1024,384]{1,0:T(8,128)(2,1)S(1)}, bf16[1024,384]{1,0:T(8,128)(2,1)S(1)}, u32[]{:S(2)}, u32[]{:S(2)}) collective-permute-start(bf16[1024,384]{1,0:T(8,128)(2,1)S(1)} %get-tuple-element.189), channel_id=1, source_target_pairs={{0,16},{8,24},{16,0},{24,8},{1,17},{9,25},{17,1},{25,9},{2,18},{10... | collective-permute-start | bytes 2359304 | tf_op jit(solution)/shard_map/ppermute | solution.py:672
  417.3 34.1 %collective-permute-start.36 = (bf16[384,384]{1,0:T(8,128)(2,1)}, bf16[384,384]{1,0:T(8,128)(2,1)S(1)}, u32[]{:S(2)}, u32[]{:S(2)}) collective-permute-start(bf16[384,384]{1,0:T(8,128)(2,1)} %get-tuple-element.182), channel_id=1, source_target_pairs={{0,2},{1,3},{2,0},{3,1},{4,6},{5,7},{6,4},{7,5},{8,10},{9,11},{10,... | collective-permute-start | bytes 884744 | tf_op jit(solution)/shard_map/ppermute | solution.py:672
  418.9 32.6 %collective-permute-start.37 = (bf16[384,384]{1,0:T(8,128)(2,1)}, bf16[384,384]{1,0:T(8,128)(2,1)S(1)}, u32[]{:S(2)}, u32[]{:S(2)}) collective-permute-start(bf16[384,384]{1,0:T(8,128)(2,1)} %get-tuple-element.181), channel_id=1, source_target_pairs={{0,4},{1,5},{2,6},{3,7},{4,0},{5,1},{6,2},{7,3},{8,12},{9,13},{10,... | collective-permute-start | bytes 884744 | tf_op jit(solution)/shard_map/ppermute | solution.py:672
  453.9 35.7 %collective-permute-start.42 = (bf16[96,1536]{1,0:T(8,128)(2,1)S(1)}, bf16[96,1536]{1,0:T(8,128)(2,1)}, u32[]{:S(2)}, u32[]{:S(2)}) collective-permute-start(bf16[96,1536]{1,0:T(8,128)(2,1)S(1)} %add_convert_fusion.9), channel_id=1, source_target_pairs={{0,2},{1,3},{2,0},{3,1},{4,6},{5,7},{6,4},{7,5},{8,10},{9,11},{10,... | collective-permute-start | bytes 884744 | tf_op jit(solution)/shard_map/ppermute | solution.py:672
  454.7 34.9 %collective-permute-start.43 = (bf16[96,1536]{1,0:T(8,128)(2,1)S(1)}, bf16[96,1536]{1,0:T(8,128)(2,1)}, u32[]{:S(2)}, u32[]{:S(2)}) collective-permute-start(bf16[96,1536]{1,0:T(8,128)(2,1)S(1)} %add_convert_fusion.9), channel_id=1, source_target_pairs={{0,4},{1,5},{2,6},{3,7},{4,0},{5,1},{6,2},{7,3},{8,12},{9,13},{10,... | collective-permute-start | bytes 884744 | tf_op jit(solution)/shard_map/ppermute | solution.py:672
  531.3 64.4 %collective-permute-start.55 = (bf16[768,384]{1,0:T(8,128)(2,1)}, bf16[768,384]{1,0:T(8,128)(2,1)}, u32[]{:S(2)}, u32[]{:S(2)}) collective-permute-start(bf16[768,384]{1,0:T(8,128)(2,1)} %pad_maximum_fusion.5), channel_id=1, source_target_pairs={{0,4},{1,5},{2,6},{3,7},{4,0},{5,1},{6,2},{7,3},{8,12},{9,13},{10,... | collective-permute-start | bytes 1769480 | tf_op jit(solution)/shard_map/ppermute | solution.py:672
  537.2 36.1 %collective-permute-start.57 = (bf16[432,384]{1,0:T(8,128)(2,1)S(1)}, bf16[432,384]{1,0:T(8,128)(2,1)S(1)}, u32[]{:S(2)}, u32[]{:S(2)}) collective-permute-start(bf16[432,384]{1,0:T(8,128)(2,1)S(1)} %fusion.21), channel_id=1, source_target_pairs={{0,6},{1,7},{2,4},{3,5},{4,2},{5,3},{6,0},{7,1},{8,14},{9,15},{10,... | collective-permute-start | bytes 995336 | tf_op jit(solution)/shard_map/ppermute | solution.py:672
  538.7 53.4 %collective-permute-start.58 = (bf16[432,384]{1,0:T(8,128)(2,1)S(1)}, bf16[432,384]{1,0:T(8,128)(2,1)S(1)}, u32[]{:S(2)}, u32[]{:S(2)}) collective-permute-start(bf16[432,384]{1,0:T(8,128)(2,1)S(1)} %fusion.21), channel_id=1, source_target_pairs={{0,4},{1,5},{2,6},{3,7},{4,0},{5,1},{6,2},{7,3},{8,12},{9,13},{10,... | collective-permute-start | bytes 995336 | tf_op jit(solution)/shard_map/ppermute | solution.py:672
  538.7 53.4 %collective-permute-start.59 = (bf16[432,384]{1,0:T(8,128)(2,1)S(1)}, bf16[432,384]{1,0:T(8,128)(2,1)S(1)}, u32[]{:S(2)}, u32[]{:S(2)}) collective-permute-start(bf16[432,384]{1,0:T(8,128)(2,1)S(1)} %fusion.21), channel_id=1, source_target_pairs={{0,2},{1,3},{2,0},{3,1},{4,6},{5,7},{6,4},{7,5},{8,10},{9,11},{10,... | collective-permute-start | bytes 995336 | tf_op jit(solution)/shard_map/ppermute | solution.py:672
  597.2 50.8 %collective-permute-start.56 = (bf16[1536,384]{1,0:T(8,128)(2,1)S(1)}, bf16[1536,384]{1,0:T(8,128)(2,1)S(1)}, u32[]{:S(2)}, u32[]{:S(2)}) collective-permute-start(bf16[1536,384]{1,0:T(8,128)(2,1)S(1)} %pad_maximum_fusion.4), channel_id=1, source_target_pairs={{0,1},{1,0},{2,3},{3,2},{4,5},{5,4},{6,7},{7,6},{8,9},{9,8},{10,11... | collective-permute-start | bytes 3538952 | tf_op jit(solution)/shard_map/ppermute | solution.py:672
  (88 other events, 1209.4 us)

commit v3 on v2

--- a/solution.py
+++ b/solution.py
@@ -725,7 +725,7 @@
 
 
 class Total:
-    def __init__(self, kept, sent, axis, rep_index, groups, copies, narrow=False):
+    def __init__(self, kept, sent, axis, rep_index, groups, copies):
         self.axis, self.rep_index = axis, rep_index
         self.sizes = {"shard": groups, "rep": copies}
         self.stages = [("shard", index, 1) for index in range(len(bits_of(groups)))]
@@ -733,8 +733,6 @@
         over = [("rep", 0, 1)] + [("rep", index, min(2, count - index)) for index in range(1, count, 2)]
         self.stages += over
         self.back = list(reversed(over))
-        if narrow:
-            self.back = [(name, shift + bit, 1) for name, shift, width in self.back for bit in range(width)]
         self.value, self.out = kept, [sent]
         self.fly()
 
@@ -776,6 +774,13 @@
         self.fly()
         return self.out
 
+    def reduce(self, *deps):
+        terms = [self.value] + [after(v, *deps) for v in self.coming]
+        mine = sum(v.astype(F32) for v in terms).astype(BF16)
+        self.value = [lax.psum(mine, "rep")]
+        self.stages, self.back = [], []
+        return [mine]
+
     def fly_back(self):
         name, shift, width = self.back[0]
         self.coming = [swap(self.value, name, k << shift, self.sizes[name]) for k in range(1, 1 << width)]
@@ -826,7 +831,7 @@
     small = (norm_gain, conv_bias, dt_bias, a_log, skip, gate_gain, conv_weight)
     packed = jnp.concatenate([v.reshape(-1) for v in small])
     wc.far(0)
-    wc.far(1)
+    wc.far(1, wg.mine[0], ow.mine[0])
     wc.side(0)
     wc.side(1)
     wg.far(0, wc.there[1])
@@ -860,7 +865,7 @@
     wg, ow = wg.finish(scan_out), ow.finish(scan_out)
     mixed, dscan, dgate, dgg = run_gating(place, normed, wg, ow, cot, scan_out, gg, order)
 
-    chain = lambda kept, sent, axis, *way: Total(kept, sent, axis, rep_index, groups, copies, *way)
+    chain = lambda kept, sent, axis: Total(kept, sent, axis, rep_index, groups, copies)
     half = inner // 2
     out_sent = outer(mixed[:, half:], cot)
     o = chain(outer(mixed[:, :half], cot), out_sent, 0)
@@ -868,7 +873,7 @@
     left, right = normed[:, :half], normed[:, half:]
     gate_sent = outer(dgate, right)
     marks = o.step(gate_sent)
-    g = chain(outer(after(dgate, *marks), left), gate_sent, 1, True)
+    g = chain(outer(after(dgate, *marks), left), gate_sent, 1)
     marks = marks + g.step(g.value)
 
     blocks = heads // per
@@ -882,25 +887,24 @@
         grads.append(found[:5])
         carried = tuple(found[5:])
         dproj, marks = found[0], []
-        if index == 1:
-            marks = o.step(dproj)
         if index == 2:
             ab = Total.join(chains[2:])
-            marks = o.coming + g.step(dproj, *o.coming)
+            marks = g.step(dproj)
             marks = marks + ab.step(dproj, *marks)
         dproj = after(dproj, *marks)
         sent = outer(dproj, right)
         kept = outer(dproj, left)
         new = chain(kept, sent, 1)
         marks = marks + new.step(kept)
-        if index < 2:
-            marks = marks + (o, g)[index].step(kept, *marks)
+        if index == 0:
+            marks = marks + o.reduce(kept, *marks)
+        if index == 1:
+            marks = marks + g.step(kept, *marks)
         chains.append(new)
     c = chains[4]
 
     part = run_gate_back(place, after(dgate, *marks), model, wg)
-    marks = g.coming + ab.coming
-    marks = marks + o.step(part, *marks)
+    marks = ab.coming + g.step(part, *ab.coming)
     marks = marks + c.step(part, *marks)
     input_grad, dgain = run_input_back(place, after(part, *marks), [v[0] for v in grads], tok, cot, gain, wc, order)
 
@@ -913,29 +917,23 @@
                            + [dcw.reshape(taps, groups, -1).transpose(1, 0, 2).reshape(groups, -1)], axis=1)
     flat = jnp.concatenate([dgain[0].reshape(groups, -1), flat], axis=1)
     abc = Total.join([ab, c])
-    marks = abc.step(dgain, *o.coming)
+    marks = abc.step(dgain, *g.coming, *o.value)
     marks = marks + g.step(*marks)
-    marks = marks + o.step(*marks)
-    flat = after(flat, *marks)
-    for bit in bits_of(groups):
-        flat = flat + swap(flat, "shard", bit, groups)
-    output = run_project_out(place, after(mixed, flat, *marks), tok, ow)
-    marks = o.coming + abc.coming
-    marks = marks + g.step(output, *marks)
-    marks = marks + abc.step(output, *marks)
-    flat = after(flat, *marks)
-    for bit in bits_of(copies):
-        flat = flat + swap(flat, "rep", bit, copies)
-    chains = [o, g, abc]
-    while not all(old.done() for old in chains):
-        for old in (g, abc, o):
+    output = run_project_out(place, after(mixed, *marks), tok, ow)
+    marks = abc.step(output, *g.coming)
+    flat = after(flat, output, *marks)
+    for axis, size in (("shard", groups), ("rep", copies)):
+        for bit in bits_of(size):
+            flat = flat + swap(flat, axis, bit, size)
+    while not all(old.done() for old in (g, abc)):
+        for old in (g, abc):
             if not old.done():
                 old.step()
 
     cut = ab.value.shape[0]
     halves = [v[:cut] for v in abc.value] + [v[cut:] for v in abc.value]
     in_total = jnp.concatenate(g.value + halves)[:outputs_all].T
-    out_total = jnp.concatenate(o.value)
+    out_total = o.value[0].astype(F32)
 
     own = lax.dynamic_slice_in_dim(flat, shard_index, 1, 0)[0]
     shares, low = [], 0

time: 662 us -> 692 us (1.045)
  between operations: 2.04 us -> 15.4 us
  local copies, waits for them, and re-layouts: 32.5 us -> 45.3 us
    psum x0 -> x1, waiting for transfers between devices: none -> 50.4 us  [reduce(): self.value = [lax.psum(mine, 'rep')]]
    ppermute x61 -> x54, waiting for transfers between devices: 167 us -> 121 us  [swap(): return lax.ppermute(value, axis, [(i, i ^ bit) for i in range(size)])]
    convert_element_type x0 -> x2, other arithmetic: none -> 8.6 us  [the longest x1 4.64 us: on_device(): out_total = o.value[0].astype(F32)]
    ppermute x61 -> x54, starting transfers between devices: 60.1 us -> 64.4 us  [swap(): return lax.ppermute(value, axis, [(i, i ^ bit) for i in range(size)])]
    convert_element_type x6 -> x8, other arithmetic: 14.7 us -> 15.2 us  [step(): self.out = [cut((mine ^ k) * size).astype(BF16) for k in range(1, parts)]]
  transfers between devices with their start and end apart: 61 -> 55, of which waited for: 17 -> 20; matrix products, arithmetic and copies ran while one was open for 16% -> 15% of each run, Pallas kernels for 37% -> 35%
where the time goes in v3:
time: 692 us; the launch traced here: 684 us
  Pallas kernels  281 us (41%)
  waiting for transfers between devices  172 us (25%)
  starting transfers between devices  64.4 us (9%)
  matrix products  56.2 us (8%)
  other arithmetic  49.1 us (7%)
  local copies, waits for them, and re-layouts  45.3 us (7%)
  between operations  15.4 us (2%)
    ppermute x54, waiting for transfers between devices, swap(): return lax.ppermute(value, axis, [(i, i ^ bit) for i in range(size)])  121 us
    pallas_call x3, Pallas kernels, run_scan_backward(): pl.pallas_call(functools.partial(scan_backward, nstate=nstate, low=low, g...  97.9 us
    ppermute x54, starting transfers between devices, swap(): return lax.ppermute(value, axis, [(i, i ^ bit) for i in range(size)])  64.4 us
    dot_general x10, matrix products, outer(): lax.dot_general(left, right, (((0,), (0,)), ((), ())), preferred_element_...  56.2 us
    psum x1, waiting for transfers between devices, reduce(): self.value = [lax.psum(mine, 'rep')]  50.4 us
    pallas_call x1, Pallas kernels, run_scan_forward(): pl.pallas_call(functools.partial(scan_forward, inner=inner, nstate=nstate...  48.7 us
    pallas_call x1, Pallas kernels, run_gating(): pl.pallas_call(functools.partial(gating, wg_pieces=wg_pieces, ow_pieces=o...  42.4 us
    pallas_call x1, Pallas kernels, run_input_back(): pl.pallas_call(functools.partial(input_back, count=len(dprojs), pieces=pi...  27.1 us
  transfers between devices with their start and end apart: 55, of which 20 were waited for; matrix products, arithmetic and copies ran while one was open for 15% of the time, Pallas kernels for 35%

profile of v3, /device:TPU:0, one launch (start us, length us, event | category | flops | bytes accessed | tf_op | source)
XLA Modules:
  0.0 683.5 jit_solution(17876429829613922849)
XLA Ops:
  36.1 8.9 %collective-permute-done.4.rest_2_.rest_5_ = bf16[864,384]{1,0:T(8,128)(2,1)} collective-permute-done((bf16[864,384]{1,0:T(8,128)(2,1)}, bf16[864,384]{1,0:T(8,128)(2,1)}, u32[]{:S(2)}, u32[]{:S(2)}) %collective-permute-start.4) | collective-permute-done | bytes 663584 | tf_op jit(solution)/shard_map/ppermute | solution.py:672
  46.5 12.3 %collective-permute-done.3.rest_1_.rest_4_ = bf16[864,384]{1,0:T(8,128)(2,1)} collective-permute-done((bf16[864,384]{1,0:T(8,128)(2,1)}, bf16[864,384]{1,0:T(8,128)(2,1)}, u32[]{:S(2)}, u32[]{:S(2)}) %collective-permute-start.3) | collective-permute-done | bytes 663584 | tf_op jit(solution)/shard_map/ppermute | solution.py:672
  65.1 10.4 %collective-permute-done.5.rest_3_.rest_6_ = bf16[864,384]{1,0:T(8,128)(2,1)} collective-permute-done((bf16[864,384]{1,0:T(8,128)(2,1)}, bf16[864,384]{1,0:T(8,128)(2,1)}, u32[]{:S(2)}, u32[]{:S(2)}) %collective-permute-start.5) | collective-permute-done | bytes 663584 | tf_op jit(solution)/shard_map/ppermute | solution.py:672
  79.1 23.8 %project_in.1 = (bf16[1024,1536]{1,0:T(8,128)(2,1)}, f32[1024,3456]{1,0:T(8,128)}) custom-call(s32[2]{0:T(128)S(1)} %pad_add_fusion.place_ref, bf16[1024,1536]{1,0:T(8,128)(2,1)} %bitcast.45, f32[1,1536]{1,0:T(1,128)S(1)} %bitcast.41, bf16[3456,384]{1,0:T(8,128)(2,1)} %pad.8.rest_0_.rest_3_, bf16[864,384]{1,0:T(8,128)(2,1)} %collective-permute-done.3.rest_1_.rest_4_, ...), custom_call_target="tpu_custom_call" | custom-call | flops 20000000000 | bytes 30000000 | tf_op jit(solution)/shard_map/project_in/pallas_call | solution.py:222
  106.8 22.9 %collective-permute-done.12.rest_1_ = bf16[1536,384]{1,0:T(8,128)(2,1)} collective-permute-done((bf16[1536,384]{1,0:T(8,128)(2,1)}, bf16[1536,384]{1,0:T(8,128)(2,1)}, u32[]{:S(2)}, u32[]{:S(2)}) %collective-permute-start.12) | collective-permute-done | bytes 1179680 | tf_op jit(solution)/shard_map/ppermute | solution.py:672
  131.8 48.7 %scan_forward.1 = (f32[1024,3072]{1,0:T(8,128)}, f32[1024,3328]{1,0:T(8,128)}, bf16[1024,3072]{1,0:T(8,128)(2,1)}) custom-call(f32[1024,3456]{1,0:T(8,128)} %get-tuple-element.89.proj_ref.tail_ref, f32[4,3328]{1,0:T(4,128)} %reshape.119.cw_ref.cwk_ref, f32[1,3328]{1,0:T(1,128)} %broadcast_in_dim_reshape.13.cb_ref, f32[8,128]{1,0:T(8,128)} %select_maximum_fusion.vec_ref, ...), custom_call_target="tpu_custom_call" | custom-call | flops 12000000000 | bytes 60000000 | tf_op jit(solution)/shard_map/scan_forward/pallas_call | solution.py:127
  187.1 42.4 %gating.1 = (bf16[1024,3072]{1,0:T(8,128)(2,1)}, f32[1024,3072]{1,0:T(8,128)}, bf16[1024,3072]{1,0:T(8,128)(2,1)}, f32[1,3072]{1,0:T(1,128)}) custom-call(s32[2]{0:T(128)} %copy-done.12, bf16[1024,1536]{1,0:T(8,128)(2,1)} %get-tuple-element.83.normed_ref, bf16[1024,1536]{1,0:T(8,128)(2,1)} %bitcast.55, f32[1024,3072]{1,0:T(8,128)} %get-tuple-element.90.scan_ref.out_ref, ...), custom_call_target="tpu_custom_call" | custom-call | flops 40000000000 | bytes 70000000 | tf_op jit(solution)/shard_map/gating/pallas_call | solution.py:305
  229.4 7.8 %convolution_convert_fusion = bf16[1536,1536]{1,0:T(8,128)(2,1)S(1)} fusion(bf16[1024,3072]{1,0:T(8,128)(2,1)} %get-tuple-element.132.mixed_ref, bf16[1,1024,1536]{2,1,0:T(8,128)(2,1)} %param.21), kind=kOutput, calls=%fused_computation.1 | convolution fusion | flops 4834197504 | bytes 11010048 | tf_op jit(solution)/shard_map/dot_general | solution.py:803
  237.5 8.7 %convolution_convert_fusion.3 = bf16[3072,768]{1,0:T(8,128)(2,1)S(1)} fusion(bf16[1024,3072]{1,0:T(8,128)(2,1)} %get-tuple-element.121.dgate_ref, bf16[1024,1536]{1,0:T(8,128)(2,1)S(1)} %copy-done.39), kind=kOutput, calls=%fused_computation.4 | convolution fusion | flops 4834197504 | bytes 12582912 | tf_op jit(solution)/shard_map/dot_general | solution.py:803
  246.6 7.5 %convolution_convert_fusion.1 = bf16[1536,1536]{1,0:T(8,128)(2,1)S(1)} fusion(bf16[1024,3072]{1,0:T(8,128)(2,1)} %get-tuple-element.132.mixed_ref, bf16[1,1024,1536]{2,1,0:T(8,128)(2,1)S(1)} %copy-done.36), kind=kOutput, calls=%fused_computation.2 | convolution fusion | flops 4834197504 | bytes 11010048 | tf_op jit(solution)/shard_map/dot_general | solution.py:803
  257.5 8.5 %convolution_convert_fusion.2 = bf16[3072,768]{1,0:T(8,128)(2,1)S(1)} fusion(bf16[1024,3072]{1,0:T(8,128)(2,1)} %get-tuple-element.121.dgate_ref, bf16[1024,1536]{1,0:T(8,128)(2,1)S(1)} %copy-done.39), kind=kOutput, calls=%fused_computation.3 | convolution fusion | flops 4834197504 | bytes 12582912 | tf_op jit(solution)/shard_map/dot_general | solution.py:803
  269.7 31.5 %scan_backward.3 = (bf16[1024,1024]{1,0:T(8,128)(2,1)}, f32[4,1024]{1,0:T(4,128)S(1)}, f32[1,1024]{1,0:T(1,128)S(1)}, f32[1,1024]{1,0:T(1,128)S(1)}, f32[8,128]{...) custom-call(f32[1024,3456]{1,0:T(8,128)} %get-tuple-element.89.proj_ref.tail_ref, ...), custom_call_target="tpu_custom_call" | custom-call | flops 40000000000 | bytes 40000000 | tf_op jit(solution)/shard_map/scan_backward/pallas_call | solution.py:636
  317.5 32.0 %scan_backward.4 = (bf16[1024,1024]{1,0:T(8,128)(2,1)}, f32[4,1024]{1,0:T(4,128)S(1)}, f32[1,1024]{1,0:T(1,128)S(1)}, f32[1,1024]{1,0:T(1,128)S(1)}, f32[8,128]{...) custom-call(f32[1024,3456]{1,0:T(8,128)} %get-tuple-element.89.proj_ref.tail_ref, ...), custom_call_target="tpu_custom_call" | custom-call | flops 40000000000 | bytes 40000000 | tf_op jit(solution)/shard_map/scan_backward/pallas_call | solution.py:636
  366.1 34.4 %scan_backward.5 = (bf16[1024,1408]{1,0:T(8,128)(2,1)}, f32[4,1280]{1,0:T(4,128)S(1)}, f32[1,1280]{1,0:T(1,128)S(1)}, f32[1,1024]{1,0:T(1,128)S(1)}, f32[8,128]{1,0:T(8,128)S(1)}) custom-call(f32[1024,3456]{1,0:T(8,128)} %get-tuple-element.89.proj_ref.tail_ref, f32[1024,3456]{1,0:T(8,128)} %get-tuple-element.89.proj_ref.tail_ref, ...), custom_call_target="tpu_custom_call" | custom-call | flops 40000000000 | bytes 40000000 | tf_op jit(solution)/shard_map/scan_backward/pallas_call | solution.py:636
  428.6 20.6 %gate_back.1.part_ref = f32[1024,1536]{1,0:T(8,128)} custom-call(s32[2]{0:T(128)S(1)} %copy-done.13, bf16[1024,3072]{1,0:T(8,128)(2,1)} %get-tuple-element.121.dgate_ref, bf16[3072,384]{1,0:T(8,128)(2,1)S(1)} %copy-done.1, bf16[1536,384]{1,0:T(8,128)(2,1)} %collective-permute-done.12.rest_1_, bf16[1536,384]{1,0:T(8,128)(2,1)} %collective-permute-done.14.rest_2_, ...), custom_call_target="tpu_custom_call" | custom-call | flops 16000000000 | bytes 22000000 | tf_op jit(solution)/shard_map/gate_back/pallas_call | solution.py:344
  450.8 5.5 collective-permute-done.36
  457.7 14.4 %collective-permute-start.38 = (bf16[384,384]{1,0:T(8,128)(2,1)S(1)}, bf16[384,384]{1,0:T(8,128)(2,1)S(1)}, u32[]{:S(2)}, u32[]{:S(2)}) collective-permute-start(bf16[384,384]{1,0:T(8,128)(2,1)S(1)} %add_convert_fusion.8), channel_id=1, source_target_pairs={{0,2},{1,3},{2,0},{3,1},{4,6},{5,7},{6,4},{7,5},{8,10},{9,11},{10,... | collective-permute-start | bytes 884744 | tf_op jit(solution)/shard_map/ppermute | solution.py:672
  476.7 27.1 %input_back.1 = (f32[1024,1536]{1,0:T(8,128)}, f32[1,1536]{1,0:T(1,128)S(1)}) custom-call(s32[2]{0:T(128)S(1)} %copy-done.13, f32[1024,1536]{1,0:T(8,128)} %gate_back.1.part_ref, bf16[1024,1536]{1,0:T(8,128)(2,1)} %bitcast.46, bf16[1024,1536]{1,0:T(8,128)(2,1)} %bitcast.56, f32[1,1536]{1,0:T(1,128)S(1)} %bitcast.42, ...), custom_call_target="tpu_custom_call" | custom-call | flops 22000001024 | bytes 46000000 | tf_op jit(solution)/shard_map/input_back/pallas_call | solution.py:400
  506.4 50.4 %all-reduce.4.cloned.1.call-done = bf16[768,1536]{1,0:T(8,128)(2,1)} async-done(((bf16[768,1536]{1,0:T(8,128)(2,1)}), bf16[768,1536]{1,0:T(8,128)(2,1)}) %all-reduce.4.cloned.1.call-update) | async-done | bytes 2359312 | tf_op jit(solution)/shard_map/psum | solution.py:780
  567.6 20.9 %project_out.1 = bf16[1024,1536]{1,0:T(8,128)(2,1)} custom-call(s32[2]{0:T(128)S(1)} %copy-done.13, bf16[1024,3072]{1,0:T(8,128)(2,1)} %get-tuple-element.132.mixed_ref, bf16[1024,1536]{1,0:T(8,128)(2,1)S(1)} %bitcast.47, bf16[768,1536]{1,0:T(8,128)(2,1)} %rest_0_.1, bf16[384,1536]{1,0:T(8,128)(2,1)} %collective-permute-done.13.rest_7_.rest_1_, ...), custom_call_target="tpu_custom_call" | custom-call | flops 14000000000 | bytes 20000000 | tf_op jit(solution)/shard_map/project_out/pallas_call | solution.py:435
  614.9 15.0 %collective-permute-done.51 = bf16[432,384]{1,0:T(8,128)(2,1)S(1)} collective-permute-done((bf16[432,384]{1,0:T(8,128)(2,1)S(1)}, bf16[432,384]{1,0:T(8,128)(2,1)S(1)}, u32[]{:S(2)}, u32[]{:S(2)}) %collective-permute-start.51) | collective-permute-done | bytes 331808 | tf_op jit(solution)/shard_map/ppermute | solution.py:672
  632.2 4.9 collective-permute-done.49
  640.4 22.4 %collective-permute-done.53 = bf16[1728,384]{1,0:T(8,128)(2,1)S(1)} collective-permute-done((bf16[1728,384]{1,0:T(8,128)(2,1)}, bf16[1728,384]{1,0:T(8,128)(2,1)S(1)}, u32[]{:S(2)}, u32[]{:S(2)}) %collective-permute-start.53) | collective-permute-done | bytes 1327136 | tf_op jit(solution)/shard_map/ppermute | solution.py:672
  667.9 8.4 %slice_bitcast_fusion = f32[384,6448]{0,1:T(8,128)} fusion(f32[6528,384]{1,0:T(8,128)} %slice_dynamic-update-slice_fusion.2), kind=kLoop, calls=%fused_computation | loop fusion | bytes 19808256 | tf_op jit(solution)/shard_map/transpose | solution.py:935
  (300 shorter events, 178.8 us)
Async XLA Ops:
  7.2 549.7 %all-reduce.4.cloned.1.call-start = ((), (), s32[]{:S(2)}) async-start(), calls=%async_computation | async-start | bytes 4718592 | tf_op jit(solution)/shard_map/psum | solution.py:780
  27.0 31.8 %collective-permute-start.3 = (bf16[864,384]{1,0:T(8,128)(2,1)}, bf16[864,384]{1,0:T(8,128)(2,1)}, u32[]{:S(2)}, u32[]{:S(2)}) collective-permute-start(bf16[864,384]{1,0:T(8,128)(2,1)} %get-tuple-element.176), channel_id=1, source_target_pairs={{0,16},{8,24},{16,0},{24,8},{1,17},{9,25},{17,1},{25,9},{2,18},{10... | collective-permute-start | bytes 1990664 | tf_op jit(solution)/shard_map/ppermute | solution.py:672
  30.7 47.6 %collective-permute-start.7 = (bf16[3456,384]{1,0:T(8,128)(2,1)}, bf16[3456,384]{1,0:T(8,128)(2,1)}, u32[]{:S(2)}, u32[]{:S(2)}) collective-permute-start(bf16[3456,384]{1,0:T(8,128)(2,1)} %pad.8.rest_0_.rest_3_), channel_id=1, source_target_pairs={{0,8},{8,0},{16,24},{24,16},{1,9},{9,1},{17,25},{25,17},{2,10},{10... | collective-permute-start | bytes 7962632 | tf_op jit(solution)/shard_map/ppermute | solution.py:672
  75.6 105.4 %collective-permute-start.15 = (bf16[3072,384]{1,0:T(8,128)(2,1)S(1)}, bf16[3072,384]{1,0:T(8,128)(2,1)}, u32[]{:S(2)}, u32[]{:S(2)}) collective-permute-start(bf16[3072,384]{1,0:T(8,128)(2,1)S(1)} %slice.134.rest_0_), channel_id=1, source_target_pairs={{0,8},{8,0},{16,24},{24,16},{1,9},{9,1},{17,25},{25,17},{2,10},{10... | collective-permute-start | bytes 7077896 | tf_op jit(solution)/shard_map/ppermute | solution.py:672
  76.7 53.1 %collective-permute-start.12 = (bf16[1536,384]{1,0:T(8,128)(2,1)}, bf16[1536,384]{1,0:T(8,128)(2,1)}, u32[]{:S(2)}, u32[]{:S(2)}) collective-permute-start(bf16[1536,384]{1,0:T(8,128)(2,1)} %constant_dynamic-slice_fusion.1), channel_id=1, source_target_pairs={{0,16},{8,24},{16,0},{24,8},{1,17},{9,25},{17,1},{25,9},{2,18},{10... | collective-permute-start | bytes 3538952 | tf_op jit(solution)/shard_map/ppermute | solution.py:672
  105.3 75.1 %collective-permute-start.18 = (bf16[384,1536]{1,0:T(8,128)(2,1)}, bf16[384,1536]{1,0:T(8,128)(2,1)}, u32[]{:S(2)}, u32[]{:S(2)}) collective-permute-start(bf16[384,1536]{1,0:T(8,128)(2,1)} %collective-permute-done.13.rest_7_.rest_1_), channel_id=1, source_target_pairs={{0,1},{1,0},{2,3},{3,2},{4,5},{5,4},{6,7},{7,6},{8,9},{9,8},{10,11... | collective-permute-start | bytes 3538952 | tf_op jit(solution)/shard_map/ppermute | solution.py:672
  129.8 50.8 %collective-permute-start.14 = (bf16[1536,384]{1,0:T(8,128)(2,1)}, bf16[1536,384]{1,0:T(8,128)(2,1)}, u32[]{:S(2)}, u32[]{:S(2)}) collective-permute-start(bf16[1536,384]{1,0:T(8,128)(2,1)} %collective-permute-done.12.rest_1_), channel_id=1, source_target_pairs={{0,1},{1,0},{2,3},{3,2},{4,5},{5,4},{6,7},{7,6},{8,9},{9,8},{10,11... | collective-permute-start | bytes 3538952 | tf_op jit(solution)/shard_map/ppermute | solution.py:672
  131.3 49.8 %collective-permute-start.19 = (bf16[768,1536]{1,0:T(8,128)(2,1)}, bf16[768,1536]{1,0:T(8,128)(2,1)}, u32[]{:S(2)}, u32[]{:S(2)}) collective-permute-start(bf16[768,1536]{1,0:T(8,128)(2,1)} %rest_0_.1), channel_id=1, source_target_pairs={{0,8},{8,0},{16,24},{24,16},{1,9},{9,1},{17,25},{25,17},{2,10},{10... | collective-permute-start | bytes 7077896 | tf_op jit(solution)/shard_map/ppermute | solution.py:672
  131.3 49.8 %collective-permute-start.20 = (bf16[384,1536]{1,0:T(8,128)(2,1)}, bf16[384,1536]{1,0:T(8,128)(2,1)}, u32[]{:S(2)}, u32[]{:S(2)}) collective-permute-start(bf16[384,1536]{1,0:T(8,128)(2,1)} %collective-permute-done.13.rest_7_.rest_1_), channel_id=1, source_target_pairs={{0,8},{8,0},{16,24},{24,16},{1,9},{9,1},{17,25},{25,17},{2,10},{10... | collective-permute-start | bytes 3538952 | tf_op jit(solution)/shard_map/ppermute | solution.py:672
  257.0 54.4 %collective-permute-start.25 = (bf16[768,1536]{1,0:T(8,128)(2,1)}, bf16[768,1536]{1,0:T(8,128)(2,1)}, u32[]{:S(2)}, u32[]{:S(2)}) collective-permute-start(bf16[768,1536]{1,0:T(8,128)(2,1)} %add_convert_fusion.2), channel_id=1, source_target_pairs={{0,16},{8,24},{16,0},{24,8},{1,17},{9,25},{17,1},{25,9},{2,18},{10... | collective-permute-start | bytes 7077896 | tf_op jit(solution)/shard_map/ppermute | solution.py:672
  306.0 56.0 %collective-permute-start.29 = (bf16[3072,384]{1,0:T(8,128)(2,1)}, bf16[3072,384]{1,0:T(8,128)(2,1)}, u32[]{:S(2)}, u32[]{:S(2)}) collective-permute-start(bf16[3072,384]{1,0:T(8,128)(2,1)} %get-tuple-element.154), channel_id=1, source_target_pairs={{0,16},{8,24},{16,0},{24,8},{1,17},{9,25},{17,1},{25,9},{2,18},{10... | collective-permute-start | bytes 7077896 | tf_op jit(solution)/shard_map/ppermute | solution.py:672
  354.3 46.2 %collective-permute-start.27 = (bf16[1024,384]{1,0:T(8,128)(2,1)}, bf16[1024,384]{1,0:T(8,128)(2,1)S(1)}, u32[]{:S(2)}, u32[]{:S(2)}) collective-permute-start(bf16[1024,384]{1,0:T(8,128)(2,1)} %get-tuple-element.171), channel_id=1, source_target_pairs={{0,16},{8,24},{16,0},{24,8},{1,17},{9,25},{17,1},{25,9},{2,18},{10... | collective-permute-start | bytes 2359304 | tf_op jit(solution)/shard_map/ppermute | solution.py:672
  365.5 35.2 %collective-permute-start.30 = (bf16[1536,384]{1,0:T(8,128)(2,1)S(1)}, bf16[1536,384]{1,0:T(8,128)(2,1)S(1)}, u32[]{:S(2)}, u32[]{:S(2)}) collective-permute-start(bf16[1536,384]{1,0:T(8,128)(2,1)S(1)} %get-tuple-element.156), channel_id=1, source_target_pairs={{0,1},{1,0},{2,3},{3,2},{4,5},{5,4},{6,7},{7,6},{8,9},{9,8},{10,11... | collective-permute-start | bytes 3538952 | tf_op jit(solution)/shard_map/ppermute | solution.py:672
  366.1 34.4 %collective-permute-start.28 = (bf16[1024,384]{1,0:T(8,128)(2,1)S(1)}, bf16[1024,384]{1,0:T(8,128)(2,1)S(1)}, u32[]{:S(2)}, u32[]{:S(2)}) collective-permute-start(bf16[1024,384]{1,0:T(8,128)(2,1)S(1)} %get-tuple-element.169), channel_id=1, source_target_pairs={{0,16},{8,24},{16,0},{24,8},{1,17},{9,25},{17,1},{25,9},{2,18},{10... | collective-permute-start | bytes 2359304 | tf_op jit(solution)/shard_map/ppermute | solution.py:672
  413.8 35.4 %collective-permute-start.33 = (bf16[1024,384]{1,0:T(8,128)(2,1)}, bf16[1024,384]{1,0:T(8,128)(2,1)S(1)}, u32[]{:S(2)}, u32[]{:S(2)}) collective-permute-start(bf16[1024,384]{1,0:T(8,128)(2,1)} %get-tuple-element.157), channel_id=1, source_target_pairs={{0,1},{1,0},{2,3},{3,2},{4,5},{5,4},{6,7},{7,6},{8,9},{9,8},{10,11... | collective-permute-start | bytes 2359304 | tf_op jit(solution)/shard_map/ppermute | solution.py:672
  415.1 34.1 %collective-permute-start.34 = (bf16[384,384]{1,0:T(8,128)(2,1)}, bf16[384,384]{1,0:T(8,128)(2,1)S(1)}, u32[]{:S(2)}, u32[]{:S(2)}) collective-permute-start(bf16[384,384]{1,0:T(8,128)(2,1)} %get-tuple-element.166), channel_id=1, source_target_pairs={{0,2},{1,3},{2,0},{3,1},{4,6},{5,7},{6,4},{7,5},{8,10},{9,11},{10,... | collective-permute-start | bytes 884744 | tf_op jit(solution)/shard_map/ppermute | solution.py:672
  416.7 34.1 %collective-permute-start.35 = (bf16[384,384]{1,0:T(8,128)(2,1)S(1)}, bf16[384,384]{1,0:T(8,128)(2,1)S(1)}, u32[]{:S(2)}, u32[]{:S(2)}) collective-permute-start(bf16[384,384]{1,0:T(8,128)(2,1)S(1)} %get-tuple-element.165), channel_id=1, source_target_pairs={{0,4},{1,5},{2,6},{3,7},{4,0},{5,1},{6,2},{7,3},{8,12},{9,13},{10,... | collective-permute-start | bytes 884744 | tf_op jit(solution)/shard_map/ppermute | solution.py:672
  419.3 37.0 %collective-permute-start.36 = (bf16[384,384]{1,0:T(8,128)(2,1)S(1)}, bf16[384,384]{1,0:T(8,128)(2,1)S(1)}, u32[]{:S(2)}, u32[]{:S(2)}) collective-permute-start(bf16[384,384]{1,0:T(8,128)(2,1)S(1)} %get-tuple-element.164), channel_id=1, source_target_pairs={{0,6},{1,7},{2,4},{3,5},{4,2},{5,3},{6,0},{7,1},{8,14},{9,15},{10,... | collective-permute-start | bytes 884744 | tf_op jit(solution)/shard_map/ppermute | solution.py:672
  426.5 48.6 %collective-permute-start.32 = (bf16[1408,384]{1,0:T(8,128)(2,1)S(1)}, bf16[1408,384]{1,0:T(8,128)(2,1)S(1)}, u32[]{:S(2)}, u32[]{:S(2)}) collective-permute-start(bf16[1408,384]{1,0:T(8,128)(2,1)S(1)} %get-tuple-element.159), channel_id=1, source_target_pairs={{0,16},{8,24},{16,0},{24,8},{1,17},{9,25},{17,1},{25,9},{2,18},{10... | collective-permute-start | bytes 3244040 | tf_op jit(solution)/shard_map/ppermute | solution.py:672
  457.7 99.2 %collective-permute-start.38 = (bf16[384,384]{1,0:T(8,128)(2,1)S(1)}, bf16[384,384]{1,0:T(8,128)(2,1)S(1)}, u32[]{:S(2)}, u32[]{:S(2)}) collective-permute-start(bf16[384,384]{1,0:T(8,128)(2,1)S(1)} %add_convert_fusion.8), channel_id=1, source_target_pairs={{0,2},{1,3},{2,0},{3,1},{4,6},{5,7},{6,4},{7,5},{8,10},{9,11},{10,... | collective-permute-start | bytes 884744 | tf_op jit(solution)/shard_map/ppermute | solution.py:672
  472.1 84.7 %collective-permute-start.39 = (bf16[384,384]{1,0:T(8,128)(2,1)S(1)}, bf16[384,384]{1,0:T(8,128)(2,1)}, u32[]{:S(2)}, u32[]{:S(2)}) collective-permute-start(bf16[384,384]{1,0:T(8,128)(2,1)S(1)} %add_convert_fusion.8), channel_id=1, source_target_pairs={{0,4},{1,5},{2,6},{3,7},{4,0},{5,1},{6,2},{7,3},{8,12},{9,13},{10,... | collective-permute-start | bytes 884744 | tf_op jit(solution)/shard_map/ppermute | solution.py:672
  473.8 83.1 %collective-permute-start.40 = (bf16[384,384]{1,0:T(8,128)(2,1)S(1)}, bf16[384,384]{1,0:T(8,128)(2,1)}, u32[]{:S(2)}, u32[]{:S(2)}) collective-permute-start(bf16[384,384]{1,0:T(8,128)(2,1)S(1)} %add_convert_fusion.8), channel_id=1, source_target_pairs={{0,6},{1,7},{2,4},{3,5},{4,2},{5,3},{6,0},{7,1},{8,14},{9,15},{10,... | collective-permute-start | bytes 884744 | tf_op jit(solution)/shard_map/ppermute | solution.py:672
  598.8 31.1 %collective-permute-start.51 = (bf16[432,384]{1,0:T(8,128)(2,1)S(1)}, bf16[432,384]{1,0:T(8,128)(2,1)S(1)}, u32[]{:S(2)}, u32[]{:S(2)}) collective-permute-start(bf16[432,384]{1,0:T(8,128)(2,1)S(1)} %copy-done.29), channel_id=1, source_target_pairs={{0,4},{1,5},{2,6},{3,7},{4,0},{5,1},{6,2},{7,3},{8,12},{9,13},{10,... | collective-permute-start | bytes 995336 | tf_op jit(solution)/shard_map/ppermute | solution.py:672
  631.5 31.3 %collective-permute-start.53 = (bf16[1728,384]{1,0:T(8,128)(2,1)}, bf16[1728,384]{1,0:T(8,128)(2,1)S(1)}, u32[]{:S(2)}, u32[]{:S(2)}) collective-permute-start(bf16[1728,384]{1,0:T(8,128)(2,1)} %pad_maximum_fusion.2), channel_id=1, source_target_pairs={{0,1},{1,0},{2,3},{3,2},{4,5},{5,4},{6,7},{7,6},{8,9},{9,8},{10,11... | collective-permute-start | bytes 3981320 | tf_op jit(solution)/shard_map/ppermute | solution.py:672
  (78 other events, 921.2 us)
Sparse Core Ops, SparseCore 0:
  411.6 145.1 all-reduce.3

commit v4 on v2

--- a/solution.py
+++ b/solution.py
@@ -698,21 +698,37 @@
         self.mine = [lax.dynamic_slice_in_dim(shard, parity * self.half + c * self.rows, self.rows, 0)
                      for c in range(chunks)]
         self.there, self.across = [None] * chunks, [None] * chunks
+        self.own, self.early = None, []
 
     def far(self, chunk, *deps):
         value = after(self.mine[chunk], *deps)
         self.there[chunk] = swap(value, "shard", 2, self.groups)
 
+    def whole(self, *deps):
+        self.there = [swap(after(self.shard, *deps), "shard", 2, self.groups)]
+        self.across = []
+
     def side(self, chunk):
         self.across[chunk] = swap(self.there[chunk], "rep", 1, self.copies)
 
+    def core(self, value, *deps):
+        return swap(after(value, *deps), "shard", 1, self.groups)
+
     def finish(self, *deps):
-        have = {0: [(0, None, 0, self.shard)]}
-        have[2] = [(c * self.rows, h, self.half, v) for h, vs in ((0, self.there), (1, self.across))
-                   for c, v in enumerate(vs)]
-        for source in (0, 2):
-            have[source ^ 1] = [(r, h, s, swap(after(v, *deps) if v is self.across[-1] else v, "shard", 1, self.groups))
-                                for r, h, s, v in have[source]]
+        own = self.own if self.own is not None else self.core(self.shard)
+        have = {0: [(0, None, 0, self.shard)], 1: [(0, None, 0, own)]}
+        if self.across:
+            have[2] = [(c * self.rows, h, self.half, v) for h, vs in ((0, self.there), (1, self.across))
+                       for c, v in enumerate(vs)]
+        else:
+            have[2] = [(0, None, 0, self.there[0])]
+        have[3] = []
+        for index, (row, half, size, value) in enumerate(have[2]):
+            if index < len(self.early):
+                partner = self.early[index]
+            else:
+                partner = self.core(value, *(deps if index == len(have[2]) - 1 else ()))
+            have[3].append((row, half, size, partner))
         pieces, arrays = [], []
         for position, source in enumerate(self.order):
             for row, half, size, value in have[source]:
@@ -829,8 +845,10 @@
     wc.far(1)
     wc.side(0)
     wc.side(1)
-    wg.far(0, wc.there[1])
-    ow.far(0, wc.there[1])
+    wc.own = wc.core(wc.shard)
+    wc.early = [wc.core(wc.there[0])]
+    wg.far(0, wc.there[1], wc.own, wc.early[0])
+    ow.whole(wc.there[1], wc.own, wc.early[0])
     rows = [packed, swap(packed, "shard", 1, groups)]
     far = swap(packed, "shard", 2, groups)
     rows += [far, swap(far, "shard", 1, groups)]
@@ -851,10 +869,9 @@
 
     wc = wc.finish(gain, cb, gg, cw, vec, skip_cols, pick)
     normed, proj = run_project_in(place, tok, gain, wc, total, order)
-    for weight in (wg, ow):
-        weight.there[0] = after(weight.there[0], normed)
-        weight.side(0)
-    proj = after(proj, wg.there[0], ow.there[0])
+    wg.there[0] = after(wg.there[0], normed)
+    wg.side(0)
+    proj = after(proj, wg.there[0])
     per = 8
     scan_out, sums, starts = run_scan_forward(proj, cw, cb, vec, skip_cols, inner, nstate, heads // per, per)
     wg, ow = wg.finish(scan_out), ow.finish(scan_out)
@@ -863,12 +880,12 @@
     chain = lambda kept, sent, axis, *way: Total(kept, sent, axis, rep_index, groups, copies, *way)
     half = inner // 2
     out_sent = outer(mixed[:, half:], cot)
-    o = chain(outer(mixed[:, :half], cot), out_sent, 0)
+    o = chain(outer(mixed[:, :half], cot), out_sent, 0, True)
     half = model // 2
     left, right = normed[:, :half], normed[:, half:]
     gate_sent = outer(dgate, right)
     marks = o.step(gate_sent)
-    g = chain(outer(after(dgate, *marks), left), gate_sent, 1, True)
+    g = chain(outer(after(dgate, *marks), left), gate_sent, 1)
     marks = marks + g.step(g.value)
 
     blocks = heads // per
@@ -885,23 +902,27 @@
         if index == 1:
             marks = o.step(dproj)
         if index == 2:
-            ab = Total.join(chains[2:])
-            marks = o.coming + g.step(dproj, *o.coming)
-            marks = marks + ab.step(dproj, *marks)
+            marks = ab.coming + g.step(dproj)
+            marks = marks + o.step(dproj, *marks)
         dproj = after(dproj, *marks)
         sent = outer(dproj, right)
         kept = outer(dproj, left)
         new = chain(kept, sent, 1)
-        marks = marks + new.step(kept)
-        if index < 2:
-            marks = marks + (o, g)[index].step(kept, *marks)
         chains.append(new)
-    c = chains[4]
+        if index == 0:
+            marks = marks + new.coming + o.step(kept)
+        if index == 1:
+            ab = Total.join(chains[2:])
+            marks = marks + ab.step(kept)
+            marks = marks + g.step(kept, *marks)
+        if index == 2:
+            marks = marks + new.step(kept)
 
     part = run_gate_back(place, after(dgate, *marks), model, wg)
-    marks = g.coming + ab.coming
+    abc = Total.join([ab, chains[4]])
+    marks = g.step(part)
+    marks = marks + abc.step(part, *marks)
     marks = marks + o.step(part, *marks)
-    marks = marks + c.step(part, *marks)
     input_grad, dgain = run_input_back(place, after(part, *marks), [v[0] for v in grads], tok, cot, gain, wc, order)
 
     dcw = jnp.concatenate([v[1] for v in grads], axis=1)
@@ -912,29 +933,20 @@
     flat = jnp.concatenate([v.reshape(groups, -1) for v in pieces]
                            + [dcw.reshape(taps, groups, -1).transpose(1, 0, 2).reshape(groups, -1)], axis=1)
     flat = jnp.concatenate([dgain[0].reshape(groups, -1), flat], axis=1)
-    abc = Total.join([ab, c])
-    marks = abc.step(dgain, *o.coming)
+    marks = abc.step(dgain, *g.coming, *o.coming)
     marks = marks + g.step(*marks)
     marks = marks + o.step(*marks)
-    flat = after(flat, *marks)
-    for bit in bits_of(groups):
-        flat = flat + swap(flat, "shard", bit, groups)
-    output = run_project_out(place, after(mixed, flat, *marks), tok, ow)
-    marks = o.coming + abc.coming
-    marks = marks + g.step(output, *marks)
-    marks = marks + abc.step(output, *marks)
-    flat = after(flat, *marks)
-    for bit in bits_of(copies):
-        flat = flat + swap(flat, "rep", bit, copies)
-    chains = [o, g, abc]
-    while not all(old.done() for old in chains):
-        for old in (g, abc, o):
-            if not old.done():
-                old.step()
-
-    cut = ab.value.shape[0]
-    halves = [v[:cut] for v in abc.value] + [v[cut:] for v in abc.value]
-    in_total = jnp.concatenate(g.value + halves)[:outputs_all].T
+    output = run_project_out(place, after(mixed, *marks), tok, ow)
+    marks = abc.step(output, *g.coming, *o.coming)
+    flat = after(flat, output, *marks)
+    for axis, size in (("shard", groups), ("rep", copies)):
+        for bit in bits_of(size):
+            flat = flat + swap(flat, axis, bit, size)
+    for old in (g, o, abc):
+        while not old.done():
+            old.step()
+
+    in_total = jnp.concatenate(g.value + abc.value)[:outputs_all].T
     out_total = jnp.concatenate(o.value)
 
     own = lax.dynamic_slice_in_dim(flat, shard_index, 1, 0)[0]

time: 662 us -> 649 us (0.980)
  local copies, waits for them, and re-layouts: 32.5 us -> 23.5 us
    ppermute x61 -> x57, starting transfers between devices: 60.1 us -> 54.4 us  [swap(): return lax.ppermute(value, axis, [(i, i ^ bit) for i in range(size)])]
    ppermute x61 -> x57, waiting for transfers between devices: 167 us -> 161 us  [swap(): return lax.ppermute(value, axis, [(i, i ^ bit) for i in range(size)])]
  transfers between devices with their start and end apart: 61 -> 57, of which waited for: 17 -> 16; matrix products, arithmetic and copies ran while one was open for 16% -> 16% of each run, Pallas kernels for 37% -> 37%
where the time goes in v4:
time: 649 us; the launch traced here: 640 us
  Pallas kernels  281 us (43%)
  waiting for transfers between devices  161 us (25%)
  matrix products  62.2 us (10%)
  other arithmetic  56.5 us (9%)
  starting transfers between devices  54.4 us (8%)
  local copies, waits for them, and re-layouts  23.5 us (4%)
    ppermute x57, waiting for transfers between devices, swap(): return lax.ppermute(value, axis, [(i, i ^ bit) for i in range(size)])  161 us
    pallas_call x3, Pallas kernels, run_scan_backward(): pl.pallas_call(functools.partial(scan_backward, nstate=nstate, low=low, g...  96.9 us
    dot_general x10, matrix products, outer(): lax.dot_general(left, right, (((0,), (0,)), ((), ())), preferred_element_...  62.2 us
    ppermute x57, starting transfers between devices, swap(): return lax.ppermute(value, axis, [(i, i ^ bit) for i in range(size)])  54.4 us
    pallas_call x1, Pallas kernels, run_scan_forward(): pl.pallas_call(functools.partial(scan_forward, inner=inner, nstate=nstate...  48.7 us
    pallas_call x1, Pallas kernels, run_gating(): pl.pallas_call(functools.partial(gating, wg_pieces=wg_pieces, ow_pieces=o...  42 us
    pallas_call x1, Pallas kernels, run_input_back(): pl.pallas_call(functools.partial(input_back, count=len(dprojs), pieces=pi...  27.4 us
    pallas_call x1, Pallas kernels, run_project_in(): pl.pallas_call(functools.partial(project_in, pieces=pieces, order=order),...  24.3 us
  transfers between devices with their start and end apart: 57, of which 16 were waited for; matrix products, arithmetic and copies ran while one was open for 16% of the time, Pallas kernels for 37%

profile of v4, /device:TPU:0, one launch (start us, length us, event | category | flops | bytes accessed | tf_op | source)
XLA Modules:
  0.0 640.5 jit_solution(3814820237093992029)
XLA Ops:
  21.1 8.9 %collective-permute-done.4.rest_2_.rest_5_ = bf16[864,384]{1,0:T(8,128)(2,1)} collective-permute-done((bf16[864,384]{1,0:T(8,128)(2,1)}, bf16[864,384]{1,0:T(8,128)(2,1)}, u32[]{:S(2)}, u32[]{:S(2)}) %collective-permute-start.4) | collective-permute-done | bytes 663584 | tf_op jit(solution)/shard_map/ppermute | solution.py:672
  31.5 12.2 %collective-permute-done.3.rest_1_.rest_4_ = bf16[864,384]{1,0:T(8,128)(2,1)} collective-permute-done((bf16[864,384]{1,0:T(8,128)(2,1)}, bf16[864,384]{1,0:T(8,128)(2,1)}, u32[]{:S(2)}, u32[]{:S(2)}) %collective-permute-start.3) | collective-permute-done | bytes 663584 | tf_op jit(solution)/shard_map/ppermute | solution.py:672
  50.1 10.4 %collective-permute-done.5.rest_3_.rest_6_ = bf16[864,384]{1,0:T(8,128)(2,1)} collective-permute-done((bf16[864,384]{1,0:T(8,128)(2,1)}, bf16[864,384]{1,0:T(8,128)(2,1)}, u32[]{:S(2)}, u32[]{:S(2)}) %collective-permute-start.5) | collective-permute-done | bytes 663584 | tf_op jit(solution)/shard_map/ppermute | solution.py:672
  65.3 24.3 %project_in.1 = (bf16[1024,1536]{1,0:T(8,128)(2,1)}, f32[1024,3456]{1,0:T(8,128)}) custom-call(s32[2]{0:T(128)S(1)} %pad_add_fusion.place_ref, bf16[1024,1536]{1,0:T(8,128)(2,1)} %bitcast.45, f32[1,1536]{1,0:T(1,128)S(1)} %bitcast.41, bf16[3456,384]{1,0:T(8,128)(2,1)} %pad.8.rest_0_.rest_3_, bf16[864,384]{1,0:T(8,128)(2,1)} %collective-permute-done.3.rest_1_.rest_4_, ...), custom_call_target="tpu_custom_call" | custom-call | flops 20000000000 | bytes 30000000 | tf_op jit(solution)/shard_map/project_in/pallas_call | solution.py:222
  93.8 48.7 %scan_forward.1 = (f32[1024,3072]{1,0:T(8,128)}, f32[1024,3328]{1,0:T(8,128)}, bf16[1024,3072]{1,0:T(8,128)(2,1)}) custom-call(f32[1024,3456]{1,0:T(8,128)} %get-tuple-element.89.proj_ref.tail_ref, f32[4,3328]{1,0:T(4,128)} %reshape.119.cw_ref.cwk_ref, f32[1,3328]{1,0:T(1,128)} %broadcast_in_dim_reshape.13.cb_ref, f32[8,128]{1,0:T(8,128)} %select_maximum_fusion.vec_ref, ...), custom_call_target="tpu_custom_call" | custom-call | flops 12000000000 | bytes 60000000 | tf_op jit(solution)/shard_map/scan_forward/pallas_call | solution.py:127
  143.1 6.0 collective-permute-done.15.rest_4_
  150.7 42.0 %gating.1 = (bf16[1024,3072]{1,0:T(8,128)(2,1)}, f32[1024,3072]{1,0:T(8,128)}, bf16[1024,3072]{1,0:T(8,128)(2,1)}, f32[1,3072]{1,0:T(1,128)}) custom-call(s32[2]{0:T(128)} %copy-done.6, bf16[1024,1536]{1,0:T(8,128)(2,1)} %get-tuple-element.85.normed_ref, bf16[1024,1536]{1,0:T(8,128)(2,1)} %bitcast.55, f32[1024,3072]{1,0:T(8,128)} %get-tuple-element.90.scan_ref.out_ref, ...), custom_call_target="tpu_custom_call" | custom-call | flops 40000000000 | bytes 70000000 | tf_op jit(solution)/shard_map/gating/pallas_call | solution.py:305
  192.8 7.8 %convolution_convert_fusion = bf16[1536,1536]{1,0:T(8,128)(2,1)S(1)} fusion(bf16[1024,3072]{1,0:T(8,128)(2,1)} %get-tuple-element.138.mixed_ref, bf16[1,1024,1536]{2,1,0:T(8,128)(2,1)} %param.21), kind=kOutput, calls=%fused_computation.1 | convolution fusion | flops 4834197504 | bytes 11010048 | tf_op jit(solution)/shard_map/dot_general | solution.py:814
  200.8 8.7 %convolution_convert_fusion.3 = bf16[3072,768]{1,0:T(8,128)(2,1)S(1)} fusion(bf16[1024,3072]{1,0:T(8,128)(2,1)} %get-tuple-element.125.dgate_ref, bf16[1024,1536]{1,0:T(8,128)(2,1)S(1)} %copy-done.27), kind=kOutput, calls=%fused_computation.8 | convolution fusion | flops 4834197504 | bytes 12582912 | tf_op jit(solution)/shard_map/dot_general | solution.py:814
  209.9 7.7 %convolution_convert_fusion.1 = bf16[1536,1536]{1,0:T(8,128)(2,1)S(1)} fusion(bf16[1024,3072]{1,0:T(8,128)(2,1)} %get-tuple-element.138.mixed_ref, bf16[1,1024,1536]{2,1,0:T(8,128)(2,1)S(1)} %copy-done.26), kind=kOutput, calls=%fused_computation.2 | convolution fusion | flops 4834197504 | bytes 11010048 | tf_op jit(solution)/shard_map/dot_general | solution.py:814
  221.8 8.5 %convolution_convert_fusion.2 = bf16[3072,768]{1,0:T(8,128)(2,1)S(1)} fusion(bf16[1024,3072]{1,0:T(8,128)(2,1)} %get-tuple-element.125.dgate_ref, bf16[1024,1536]{1,0:T(8,128)(2,1)S(1)} %copy-done.27), kind=kOutput, calls=%fused_computation.7 | convolution fusion | flops 4834197504 | bytes 12582912 | tf_op jit(solution)/shard_map/dot_general | solution.py:814
  233.9 31.4 %scan_backward.3 = (bf16[1024,1024]{1,0:T(8,128)(2,1)}, f32[4,1024]{1,0:T(4,128)S(1)}, f32[1,1024]{1,0:T(1,128)S(1)}, f32[1,1024]{1,0:T(1,128)S(1)}, f32[8,128]{...) custom-call(f32[1024,3456]{1,0:T(8,128)} %get-tuple-element.89.proj_ref.tail_ref, ...), custom_call_target="tpu_custom_call" | custom-call | flops 40000000000 | bytes 40000000 | tf_op jit(solution)/shard_map/scan_backward/pallas_call | solution.py:636
  265.4 5.5 convolution_convert_fusion.8
  282.3 31.5 %scan_backward.4 = (bf16[1024,1024]{1,0:T(8,128)(2,1)}, f32[4,1024]{1,0:T(4,128)S(1)}, f32[1,1024]{1,0:T(1,128)S(1)}, f32[1,1024]{1,0:T(1,128)S(1)}, f32[8,128]{...) custom-call(f32[1024,3456]{1,0:T(8,128)} %get-tuple-element.89.proj_ref.tail_ref, ...), custom_call_target="tpu_custom_call" | custom-call | flops 40000000000 | bytes 40000000 | tf_op jit(solution)/shard_map/scan_backward/pallas_call | solution.py:636
  338.0 37.1 %collective-permute-done.26 = bf16[3072,384]{1,0:T(8,128)(2,1)} collective-permute-done((bf16[3072,384]{1,0:T(8,128)(2,1)}, bf16[3072,384]{1,0:T(8,128)(2,1)}, u32[]{:S(2)}, u32[]{:S(2)}) %collective-permute-start.26) | collective-permute-done | bytes 2359328 | tf_op jit(solution)/shard_map/ppermute | solution.py:672
  379.6 34.0 %scan_backward.5 = (bf16[1024,1408]{1,0:T(8,128)(2,1)}, f32[4,1280]{1,0:T(4,128)S(1)}, f32[1,1280]{1,0:T(1,128)S(1)}, f32[1,1024]{1,0:T(1,128)S(1)}, f32[8,128]{1,0:T(8,128)S(1)}) custom-call(f32[1024,3456]{1,0:T(8,128)} %get-tuple-element.89.proj_ref.tail_ref, f32[1024,3456]{1,0:T(8,128)} %get-tuple-element.89.proj_ref.tail_ref, ...), custom_call_target="tpu_custom_call" | custom-call | flops 40000000000 | bytes 40000000 | tf_op jit(solution)/shard_map/scan_backward/pallas_call | solution.py:636
  417.2 5.8 convolution_convert_fusion.4
  438.6 20.6 %gate_back.1.part_ref = f32[1024,1536]{1,0:T(8,128)} custom-call(s32[2]{0:T(128)S(1)} %copy-done.7, bf16[1024,3072]{1,0:T(8,128)(2,1)} %get-tuple-element.125.dgate_ref, bf16[3072,384]{1,0:T(8,128)(2,1)S(1)} %copy-done.1, bf16[1536,384]{1,0:T(8,128)(2,1)} %collective-permute-done.12.rest_1_, bf16[1536,384]{1,0:T(8,128)(2,1)} %collective-permute-done.13.rest_2_, ...), custom_call_target="tpu_custom_call" | custom-call | flops 16000000000 | bytes 22000000 | tf_op jit(solution)/shard_map/gate_back/pallas_call | solution.py:344
  474.7 27.4 %input_back.1 = (f32[1024,1536]{1,0:T(8,128)}, f32[1,1536]{1,0:T(1,128)S(1)}) custom-call(s32[2]{0:T(128)S(1)} %copy-done.7, f32[1024,1536]{1,0:T(8,128)} %gate_back.1.part_ref, bf16[1024,1536]{1,0:T(8,128)(2,1)} %bitcast.46, bf16[1024,1536]{1,0:T(8,128)(2,1)} %bitcast.56, f32[1,1536]{1,0:T(1,128)S(1)} %bitcast.42, ...), custom_call_target="tpu_custom_call" | custom-call | flops 22000001024 | bytes 46000000 | tf_op jit(solution)/shard_map/input_back/pallas_call | solution.py:400
  502.3 14.0 %collective-permute-done.42 = bf16[192,1536]{1,0:T(8,128)(2,1)} collective-permute-done((bf16[192,1536]{1,0:T(8,128)(2,1)}, bf16[192,1536]{1,0:T(8,128)(2,1)}, u32[]{:S(2)}, u32[]{:S(2)}) %collective-permute-start.42) | collective-permute-done | bytes 589856 | tf_op jit(solution)/shard_map/ppermute | solution.py:672
  528.1 20.9 %project_out.1 = bf16[1024,1536]{1,0:T(8,128)(2,1)} custom-call(s32[2]{0:T(128)S(1)} %copy-done.7, bf16[1024,3072]{1,0:T(8,128)(2,1)} %get-tuple-element.138.mixed_ref, bf16[1024,1536]{1,0:T(8,128)(2,1)S(1)} %bitcast.47, bf16[768,1536]{1,0:T(8,128)(2,1)} %rest_0_.1, bf16[768,1536]{1,0:T(8,128)(2,1)} %collective-permute-done.17.rest_7_.rest_1_, ...), custom_call_target="tpu_custom_call" | custom-call | flops 14000000000 | bytes 20000000 | tf_op jit(solution)/shard_map/project_out/pallas_call | solution.py:435
  549.0 22.6 %collective-permute-done.45 = bf16[384,1536]{1,0:T(8,128)(2,1)S(1)} collective-permute-done((bf16[384,1536]{1,0:T(8,128)(2,1)S(1)}, bf16[384,1536]{1,0:T(8,128)(2,1)S(1)}, u32[]{:S(2)}, u32[]{:S(2)}) %collective-permute-start.45) | collective-permute-done | bytes 1179680 | tf_op jit(solution)/shard_map/ppermute | solution.py:672
  589.0 12.4 %collective-permute-done.54 = bf16[432,384]{1,0:T(8,128)(2,1)S(1)} collective-permute-done((bf16[432,384]{1,0:T(8,128)(2,1)S(1)}, bf16[432,384]{1,0:T(8,128)(2,1)S(1)}, u32[]{:S(2)}, u32[]{:S(2)}) %collective-permute-start.54) | collective-permute-done | bytes 331808 | tf_op jit(solution)/shard_map/ppermute | solution.py:672
  611.2 23.1 %collective-permute-done.56 = bf16[1728,384]{1,0:T(8,128)(2,1)} collective-permute-done((bf16[1728,384]{1,0:T(8,128)(2,1)}, bf16[1728,384]{1,0:T(8,128)(2,1)}, u32[]{:S(2)}, u32[]{:S(2)}) %collective-permute-start.56) | collective-permute-done | bytes 1327136 | tf_op jit(solution)/shard_map/ppermute | solution.py:672
  (272 shorter events, 167.4 us)
Async XLA Ops:
  15.6 47.5 %collective-permute-start.7 = (bf16[3456,384]{1,0:T(8,128)(2,1)}, bf16[3456,384]{1,0:T(8,128)(2,1)}, u32[]{:S(2)}, u32[]{:S(2)}) collective-permute-start(bf16[3456,384]{1,0:T(8,128)(2,1)} %pad.8.rest_0_.rest_3_), channel_id=1, source_target_pairs={{0,8},{8,0},{16,24},{24,16},{1,9},{9,1},{17,25},{25,17},{2,10},{10... | collective-permute-start | bytes 7962632 | tf_op jit(solution)/shard_map/ppermute | solution.py:672
  62.6 80.5 %collective-permute-start.14 = (bf16[3072,384]{1,0:T(8,128)(2,1)S(1)}, bf16[3072,384]{1,0:T(8,128)(2,1)}, u32[]{:S(2)}, u32[]{:S(2)}) collective-permute-start(bf16[3072,384]{1,0:T(8,128)(2,1)S(1)} %slice.121.rest_0_), channel_id=1, source_target_pairs={{0,8},{8,0},{16,24},{24,16},{1,9},{9,1},{17,25},{25,17},{2,10},{10... | collective-permute-start | bytes 7077896 | tf_op jit(solution)/shard_map/ppermute | solution.py:672
  63.2 79.9 %collective-permute-start.18 = (bf16[768,1536]{1,0:T(8,128)(2,1)}, bf16[768,1536]{1,0:T(8,128)(2,1)}, u32[]{:S(2)}, u32[]{:S(2)}) collective-permute-start(bf16[768,1536]{1,0:T(8,128)(2,1)} %rest_0_.1), channel_id=1, source_target_pairs={{0,8},{8,0},{16,24},{24,16},{1,9},{9,1},{17,25},{25,17},{2,10},{10... | collective-permute-start | bytes 7077896 | tf_op jit(solution)/shard_map/ppermute | solution.py:672
  63.8 78.7 %collective-permute-start.17 = (bf16[768,1536]{1,0:T(8,128)(2,1)}, bf16[768,1536]{1,0:T(8,128)(2,1)}, u32[]{:S(2)}, u32[]{:S(2)}) collective-permute-start(bf16[768,1536]{1,0:T(8,128)(2,1)} %rest_0_.1), channel_id=1, source_target_pairs={{0,16},{8,24},{16,0},{24,8},{1,17},{9,25},{17,1},{25,9},{2,18},{10... | collective-permute-start | bytes 7077896 | tf_op jit(solution)/shard_map/ppermute | solution.py:672
  92.2 50.8 %collective-permute-start.13 = (bf16[1536,384]{1,0:T(8,128)(2,1)}, bf16[1536,384]{1,0:T(8,128)(2,1)}, u32[]{:S(2)}, u32[]{:S(2)}) collective-permute-start(bf16[1536,384]{1,0:T(8,128)(2,1)} %collective-permute-done.12.rest_1_), channel_id=1, source_target_pairs={{0,1},{1,0},{2,3},{3,2},{4,5},{5,4},{6,7},{7,6},{8,9},{9,8},{10,11... | collective-permute-start | bytes 3538952 | tf_op jit(solution)/shard_map/ppermute | solution.py:672
  221.3 54.7 %collective-permute-start.23 = (bf16[768,1536]{1,0:T(8,128)(2,1)}, bf16[768,1536]{1,0:T(8,128)(2,1)}, u32[]{:S(2)}, u32[]{:S(2)}) collective-permute-start(bf16[768,1536]{1,0:T(8,128)(2,1)} %get-tuple-element.162), channel_id=1, source_target_pairs={{0,16},{8,24},{16,0},{24,8},{1,17},{9,25},{17,1},{25,9},{2,18},{10... | collective-permute-start | bytes 7077896 | tf_op jit(solution)/shard_map/ppermute | solution.py:672
  279.8 34.0 %collective-permute-start.24 = (bf16[384,1536]{1,0:T(8,128)(2,1)S(1)}, bf16[384,1536]{1,0:T(8,128)(2,1)S(1)}, u32[]{:S(2)}, u32[]{:S(2)}) collective-permute-start(bf16[384,1536]{1,0:T(8,128)(2,1)S(1)} %get-tuple-element.168), channel_id=1, source_target_pairs={{0,1},{1,0},{2,3},{3,2},{4,5},{5,4},{6,7},{7,6},{8,9},{9,8},{10,11... | collective-permute-start | bytes 3538952 | tf_op jit(solution)/shard_map/ppermute | solution.py:672
  321.3 53.8 %collective-permute-start.26 = (bf16[3072,384]{1,0:T(8,128)(2,1)}, bf16[3072,384]{1,0:T(8,128)(2,1)}, u32[]{:S(2)}, u32[]{:S(2)}) collective-permute-start(bf16[3072,384]{1,0:T(8,128)(2,1)} %get-tuple-element.160), channel_id=1, source_target_pairs={{0,16},{8,24},{16,0},{24,8},{1,17},{9,25},{17,1},{25,9},{2,18},{10... | collective-permute-start | bytes 7077896 | tf_op jit(solution)/shard_map/ppermute | solution.py:672
  322.8 91.9 %collective-permute-start.29 = (bf16[96,1536]{1,0:T(8,128)(2,1)}, bf16[96,1536]{1,0:T(8,128)(2,1)S(1)}, u32[]{:S(2)}, u32[]{:S(2)}) collective-permute-start(bf16[96,1536]{1,0:T(8,128)(2,1)} %get-tuple-element.181), channel_id=1, source_target_pairs={{0,2},{1,3},{2,0},{3,1},{4,6},{5,7},{6,4},{7,5},{8,10},{9,11},{10,... | collective-permute-start | bytes 884744 | tf_op jit(solution)/shard_map/ppermute | solution.py:672
  324.4 90.3 %collective-permute-start.30 = (bf16[96,1536]{1,0:T(8,128)(2,1)}, bf16[96,1536]{1,0:T(8,128)(2,1)S(1)}, u32[]{:S(2)}, u32[]{:S(2)}) collective-permute-start(bf16[96,1536]{1,0:T(8,128)(2,1)} %get-tuple-element.180), channel_id=1, source_target_pairs={{0,4},{1,5},{2,6},{3,7},{4,0},{5,1},{6,2},{7,3},{8,12},{9,13},{10,... | collective-permute-start | bytes 884744 | tf_op jit(solution)/shard_map/ppermute | solution.py:672
  326.9 87.7 %collective-permute-start.31 = (bf16[96,1536]{1,0:T(8,128)(2,1)}, bf16[96,1536]{1,0:T(8,128)(2,1)S(1)}, u32[]{:S(2)}, u32[]{:S(2)}) collective-permute-start(bf16[96,1536]{1,0:T(8,128)(2,1)} %get-tuple-element.179), channel_id=1, source_target_pairs={{0,6},{1,7},{2,4},{3,5},{4,2},{5,3},{6,0},{7,1},{8,14},{9,15},{10,... | collective-permute-start | bytes 884744 | tf_op jit(solution)/shard_map/ppermute | solution.py:672
  377.3 36.3 %collective-permute-start.28 = (bf16[1536,384]{1,0:T(8,128)(2,1)S(1)}, bf16[1536,384]{1,0:T(8,128)(2,1)S(1)}, u32[]{:S(2)}, u32[]{:S(2)}) collective-permute-start(bf16[1536,384]{1,0:T(8,128)(2,1)S(1)} %get-tuple-element.166), channel_id=1, source_target_pairs={{0,1},{1,0},{2,3},{3,2},{4,5},{5,4},{6,7},{7,6},{8,9},{9,8},{10,11... | collective-permute-start | bytes 3538952 | tf_op jit(solution)/shard_map/ppermute | solution.py:672
  378.1 36.6 %collective-permute-start.27 = (bf16[2048,384]{1,0:T(8,128)(2,1)S(1)}, bf16[2048,384]{1,0:T(8,128)(2,1)S(1)}, u32[]{:S(2)}, u32[]{:S(2)}) collective-permute-start(bf16[2048,384]{1,0:T(8,128)(2,1)S(1)} %get-tuple-element.169), channel_id=1, source_target_pairs={{0,16},{8,24},{16,0},{24,8},{1,17},{9,25},{17,1},{25,9},{2,18},{10... | collective-permute-start | bytes 4718600 | tf_op jit(solution)/shard_map/ppermute | solution.py:672
  427.1 32.1 %collective-permute-start.34 = (bf16[384,384]{1,0:T(8,128)(2,1)}, bf16[384,384]{1,0:T(8,128)(2,1)S(1)}, u32[]{:S(2)}, u32[]{:S(2)}) collective-permute-start(bf16[384,384]{1,0:T(8,128)(2,1)} %get-tuple-element.178), channel_id=1, source_target_pairs={{0,2},{1,3},{2,0},{3,1},{4,6},{5,7},{6,4},{7,5},{8,10},{9,11},{10,... | collective-permute-start | bytes 884744 | tf_op jit(solution)/shard_map/ppermute | solution.py:672
  431.5 38.9 %collective-permute-start.38 = (bf16[96,1536]{1,0:T(8,128)(2,1)S(1)}, bf16[96,1536]{1,0:T(8,128)(2,1)S(1)}, u32[]{:S(2)}, u32[]{:S(2)}) collective-permute-start(bf16[96,1536]{1,0:T(8,128)(2,1)S(1)} %add_convert_fusion.11), channel_id=1, source_target_pairs={{0,2},{1,3},{2,0},{3,1},{4,6},{5,7},{6,4},{7,5},{8,10},{9,11},{10,... | collective-permute-start | bytes 884744 | tf_op jit(solution)/shard_map/ppermute | solution.py:672
  461.4 40.9 %collective-permute-start.39 = (bf16[384,384]{1,0:T(8,128)(2,1)}, bf16[384,384]{1,0:T(8,128)(2,1)}, u32[]{:S(2)}, u32[]{:S(2)}) collective-permute-start(bf16[384,384]{1,0:T(8,128)(2,1)} %add_convert_fusion.10), channel_id=1, source_target_pairs={{0,2},{1,3},{2,0},{3,1},{4,6},{5,7},{6,4},{7,5},{8,10},{9,11},{10,... | collective-permute-start | bytes 884744 | tf_op jit(solution)/shard_map/ppermute | solution.py:672
  462.8 39.5 %collective-permute-start.40 = (bf16[384,384]{1,0:T(8,128)(2,1)}, bf16[384,384]{1,0:T(8,128)(2,1)}, u32[]{:S(2)}, u32[]{:S(2)}) collective-permute-start(bf16[384,384]{1,0:T(8,128)(2,1)} %add_convert_fusion.10), channel_id=1, source_target_pairs={{0,4},{1,5},{2,6},{3,7},{4,0},{5,1},{6,2},{7,3},{8,12},{9,13},{10,... | collective-permute-start | bytes 884744 | tf_op jit(solution)/shard_map/ppermute | solution.py:672
  464.9 37.4 %collective-permute-start.41 = (bf16[384,384]{1,0:T(8,128)(2,1)}, bf16[384,384]{1,0:T(8,128)(2,1)}, u32[]{:S(2)}, u32[]{:S(2)}) collective-permute-start(bf16[384,384]{1,0:T(8,128)(2,1)} %add_convert_fusion.10), channel_id=1, source_target_pairs={{0,6},{1,7},{2,4},{3,5},{4,2},{5,3},{6,0},{7,1},{8,14},{9,15},{10,... | collective-permute-start | bytes 884744 | tf_op jit(solution)/shard_map/ppermute | solution.py:672
  471.4 44.9 %collective-permute-start.42 = (bf16[192,1536]{1,0:T(8,128)(2,1)}, bf16[192,1536]{1,0:T(8,128)(2,1)}, u32[]{:S(2)}, u32[]{:S(2)}) collective-permute-start(bf16[192,1536]{1,0:T(8,128)(2,1)} %pad_maximum_fusion.9), channel_id=1, source_target_pairs={{0,4},{1,5},{2,6},{3,7},{4,0},{5,1},{6,2},{7,3},{8,12},{9,13},{10,... | collective-permute-start | bytes 1769480 | tf_op jit(solution)/shard_map/ppermute | solution.py:672
  473.4 42.9 %collective-permute-start.37 = (bf16[1728,384]{1,0:T(8,128)(2,1)}, bf16[1728,384]{1,0:T(8,128)(2,1)}, u32[]{:S(2)}, u32[]{:S(2)}) collective-permute-start(bf16[1728,384]{1,0:T(8,128)(2,1)} %get-tuple-element.163), channel_id=1, source_target_pairs={{0,1},{1,0},{2,3},{3,2},{4,5},{5,4},{6,7},{7,6},{8,9},{9,8},{10,11... | collective-permute-start | bytes 3981320 | tf_op jit(solution)/shard_map/ppermute | solution.py:672
  520.0 51.6 %collective-permute-start.44 = (bf16[1536,384]{1,0:T(8,128)(2,1)S(1)}, bf16[1536,384]{1,0:T(8,128)(2,1)S(1)}, u32[]{:S(2)}, u32[]{:S(2)}) collective-permute-start(bf16[1536,384]{1,0:T(8,128)(2,1)S(1)} %pad_maximum_fusion.7), channel_id=1, source_target_pairs={{0,1},{1,0},{2,3},{3,2},{4,5},{5,4},{6,7},{7,6},{8,9},{9,8},{10,11... | collective-permute-start | bytes 3538952 | tf_op jit(solution)/shard_map/ppermute | solution.py:672
  522.8 48.8 %collective-permute-start.45 = (bf16[384,1536]{1,0:T(8,128)(2,1)S(1)}, bf16[384,1536]{1,0:T(8,128)(2,1)S(1)}, u32[]{:S(2)}, u32[]{:S(2)}) collective-permute-start(bf16[384,1536]{1,0:T(8,128)(2,1)S(1)} %pad_maximum_fusion.8), channel_id=1, source_target_pairs={{0,1},{1,0},{2,3},{3,2},{4,5},{5,4},{6,7},{7,6},{8,9},{9,8},{10,11... | collective-permute-start | bytes 3538952 | tf_op jit(solution)/shard_map/ppermute | solution.py:672
  524.4 47.2 %collective-permute-start.46 = (bf16[432,384]{1,0:T(8,128)(2,1)S(1)}, bf16[432,384]{1,0:T(8,128)(2,1)S(1)}, u32[]{:S(2)}, u32[]{:S(2)}) collective-permute-start(bf16[432,384]{1,0:T(8,128)(2,1)S(1)} %get-tuple-element.174), channel_id=1, source_target_pairs={{0,4},{1,5},{2,6},{3,7},{4,0},{5,1},{6,2},{7,3},{8,12},{9,13},{10,... | collective-permute-start | bytes 995336 | tf_op jit(solution)/shard_map/ppermute | solution.py:672
  527.8 43.8 %collective-permute-start.47 = (bf16[432,384]{1,0:T(8,128)(2,1)S(1)}, bf16[432,384]{1,0:T(8,128)(2,1)S(1)}, u32[]{:S(2)}, u32[]{:S(2)}) collective-permute-start(bf16[432,384]{1,0:T(8,128)(2,1)S(1)} %get-tuple-element.173), channel_id=1, source_target_pairs={{0,6},{1,7},{2,4},{3,5},{4,2},{5,3},{6,0},{7,1},{8,14},{9,15},{10,... | collective-permute-start | bytes 995336 | tf_op jit(solution)/shard_map/ppermute | solution.py:672
  (65 other events, 873.6 us)

commit v5 on v4

--- a/solution.py
+++ b/solution.py
@@ -884,7 +884,7 @@
     half = model // 2
     left, right = normed[:, :half], normed[:, half:]
     gate_sent = outer(dgate, right)
-    marks = o.step(gate_sent)
+    marks = o.step(o.value)
     g = chain(outer(after(dgate, *marks), left), gate_sent, 1)
     marks = marks + g.step(g.value)
 
@@ -906,7 +906,7 @@
             marks = marks + o.step(dproj, *marks)
         dproj = after(dproj, *marks)
         sent = outer(dproj, right)
-        kept = outer(dproj, left)
+        kept = outer(after(dproj, sent, *g.coming) if index == 1 else dproj, left)
         new = chain(kept, sent, 1)
         chains.append(new)
         if index == 0:
@@ -933,11 +933,11 @@
     flat = jnp.concatenate([v.reshape(groups, -1) for v in pieces]
                            + [dcw.reshape(taps, groups, -1).transpose(1, 0, 2).reshape(groups, -1)], axis=1)
     flat = jnp.concatenate([dgain[0].reshape(groups, -1), flat], axis=1)
-    marks = abc.step(dgain, *g.coming, *o.coming)
+    marks = abc.step(dgain, *g.coming)
     marks = marks + g.step(*marks)
-    marks = marks + o.step(*marks)
     output = run_project_out(place, after(mixed, *marks), tok, ow)
-    marks = abc.step(output, *g.coming, *o.coming)
+    marks = abc.step(output, *g.coming)
+    o.step(output)
     flat = after(flat, output, *marks)
     for axis, size in (("shard", groups), ("rep", copies)):
         for bit in bits_of(size):

time: 649 us -> 586 us (0.903)
  waiting for transfers between devices: 161 us -> 73.9 us
  starting transfers between devices: 54.4 us -> 78.3 us
    ppermute x57, waiting for transfers between devices: 161 us -> 73.9 us  [swap(): return lax.ppermute(value, axis, [(i, i ^ bit) for i in range(size)])]
    ppermute x57, starting transfers between devices: 54.4 us -> 78.3 us  [swap(): return lax.ppermute(value, axis, [(i, i ^ bit) for i in range(size)])]
  transfers between devices with their start and end apart: 57 -> 57, of which waited for: 16 -> 12; matrix products, arithmetic and copies ran while one was open for 16% -> 19% of each run, Pallas kernels for 37% -> 41%
where the time goes in v5:
time: 586 us; the launch traced here: 578 us
  Pallas kernels  281 us (48%)
  starting transfers between devices  78.3 us (13%)
  waiting for transfers between devices  73.9 us (13%)
  matrix products  62 us (11%)
  other arithmetic  55.6 us (9%)
  local copies, waits for them, and re-layouts  24.5 us (4%)
    pallas_call x3, Pallas kernels, run_scan_backward(): pl.pallas_call(functools.partial(scan_backward, nstate=nstate, low=low, g...  97.2 us
    ppermute x57, starting transfers between devices, swap(): return lax.ppermute(value, axis, [(i, i ^ bit) for i in range(size)])  78.3 us
    ppermute x57, waiting for transfers between devices, swap(): return lax.ppermute(value, axis, [(i, i ^ bit) for i in range(size)])  73.9 us
    dot_general x10, matrix products, outer(): lax.dot_general(left, right, (((0,), (0,)), ((), ())), preferred_element_...  62 us
    pallas_call x1, Pallas kernels, run_scan_forward(): pl.pallas_call(functools.partial(scan_forward, inner=inner, nstate=nstate...  48.7 us
    pallas_call x1, Pallas kernels, run_gating(): pl.pallas_call(functools.partial(gating, wg_pieces=wg_pieces, ow_pieces=o...  42 us
    pallas_call x1, Pallas kernels, run_input_back(): pl.pallas_call(functools.partial(input_back, count=len(dprojs), pieces=pi...  27.6 us
    pallas_call x1, Pallas kernels, run_project_in(): pl.pallas_call(functools.partial(project_in, pieces=pieces, order=order),...  24.2 us
  transfers between devices with their start and end apart: 57, of which 12 were waited for; matrix products, arithmetic and copies ran while one was open for 19% of the time, Pallas kernels for 41%

profile of v5, /device:TPU:0, one launch (start us, length us, event | category | flops | bytes accessed | tf_op | source)
XLA Modules:
  0.0 577.7 jit_solution(17392554379993638159)
XLA Ops:
  21.0 8.9 %collective-permute-done.4.rest_2_.rest_5_ = bf16[864,384]{1,0:T(8,128)(2,1)} collective-permute-done((bf16[864,384]{1,0:T(8,128)(2,1)}, bf16[864,384]{1,0:T(8,128)(2,1)}, u32[]{:S(2)}, u32[]{:S(2)}) %collective-permute-start.4) | collective-permute-done | bytes 663584 | tf_op jit(solution)/shard_map/ppermute | solution.py:672
  31.5 12.2 %collective-permute-done.3.rest_1_.rest_4_ = bf16[864,384]{1,0:T(8,128)(2,1)} collective-permute-done((bf16[864,384]{1,0:T(8,128)(2,1)}, bf16[864,384]{1,0:T(8,128)(2,1)}, u32[]{:S(2)}, u32[]{:S(2)}) %collective-permute-start.3) | collective-permute-done | bytes 663584 | tf_op jit(solution)/shard_map/ppermute | solution.py:672
  50.1 10.4 %collective-permute-done.5.rest_3_.rest_6_ = bf16[864,384]{1,0:T(8,128)(2,1)} collective-permute-done((bf16[864,384]{1,0:T(8,128)(2,1)}, bf16[864,384]{1,0:T(8,128)(2,1)}, u32[]{:S(2)}, u32[]{:S(2)}) %collective-permute-start.5) | collective-permute-done | bytes 663584 | tf_op jit(solution)/shard_map/ppermute | solution.py:672
  65.3 24.2 %project_in.1 = (bf16[1024,1536]{1,0:T(8,128)(2,1)}, f32[1024,3456]{1,0:T(8,128)}) custom-call(s32[2]{0:T(128)S(1)} %pad_add_fusion.place_ref, bf16[1024,1536]{1,0:T(8,128)(2,1)} %bitcast.45, f32[1,1536]{1,0:T(1,128)S(1)} %bitcast.41, bf16[3456,384]{1,0:T(8,128)(2,1)} %pad.8.rest_0_.rest_3_, bf16[864,384]{1,0:T(8,128)(2,1)} %collective-permute-done.3.rest_1_.rest_4_, ...), custom_call_target="tpu_custom_call" | custom-call | flops 20000000000 | bytes 30000000 | tf_op jit(solution)/shard_map/project_in/pallas_call | solution.py:222
  93.8 48.7 %scan_forward.1 = (f32[1024,3072]{1,0:T(8,128)}, f32[1024,3328]{1,0:T(8,128)}, bf16[1024,3072]{1,0:T(8,128)(2,1)}) custom-call(f32[1024,3456]{1,0:T(8,128)} %get-tuple-element.90.proj_ref.tail_ref, f32[4,3328]{1,0:T(4,128)} %reshape.119.cw_ref.cwk_ref, f32[1,3328]{1,0:T(1,128)} %broadcast_in_dim_reshape.13.cb_ref, f32[8,128]{1,0:T(8,128)} %select_maximum_fusion.vec_ref, ...), custom_call_target="tpu_custom_call" | custom-call | flops 12000000000 | bytes 60000000 | tf_op jit(solution)/shard_map/scan_forward/pallas_call | solution.py:127
  143.1 6.0 %collective-permute-done.15.rest_4_ = bf16[1536,384]{1,0:T(8,128)(2,1)} collective-permute-done((bf16[1536,384]{1,0:T(8,128)(2,1)}, bf16[1536,384]{1,0:T(8,128)(2,1)}, u32[]{:S(2)}, u32[]{:S(2)}) %collective-permute-start.15) | collective-permute-done | bytes 1179680 | tf_op jit(solution)/shard_map/ppermute | solution.py:672
  150.7 42.0 %gating.1 = (bf16[1024,3072]{1,0:T(8,128)(2,1)}, f32[1024,3072]{1,0:T(8,128)}, bf16[1024,3072]{1,0:T(8,128)(2,1)}, f32[1,3072]{1,0:T(1,128)}) custom-call(s32[2]{0:T(128)} %copy-done.6, bf16[1024,1536]{1,0:T(8,128)(2,1)} %get-tuple-element.86.normed_ref, bf16[1024,1536]{1,0:T(8,128)(2,1)} %bitcast.55, f32[1024,3072]{1,0:T(8,128)} %get-tuple-element.91.scan_ref.out_ref, ...), custom_call_target="tpu_custom_call" | custom-call | flops 40000000000 | bytes 70000000 | tf_op jit(solution)/shard_map/gating/pallas_call | solution.py:305
  192.8 7.8 %convolution_convert_fusion = bf16[1536,1536]{1,0:T(8,128)(2,1)S(1)} fusion(bf16[1024,3072]{1,0:T(8,128)(2,1)} %get-tuple-element.139.mixed_ref, bf16[1,1024,1536]{2,1,0:T(8,128)(2,1)} %param.21), kind=kOutput, calls=%fused_computation.1 | convolution fusion | flops 4834197504 | bytes 11010048 | tf_op jit(solution)/shard_map/dot_general | solution.py:814
  200.8 8.7 %convolution_convert_fusion.2 = bf16[3072,768]{1,0:T(8,128)(2,1)S(1)} fusion(bf16[1024,3072]{1,0:T(8,128)(2,1)} %get-tuple-element.127.dgate_ref, bf16[1024,1536]{1,0:T(8,128)(2,1)S(1)} %copy-done.36), kind=kOutput, calls=%fused_computation.7 | convolution fusion | flops 4834197504 | bytes 12582912 | tf_op jit(solution)/shard_map/dot_general | solution.py:814
  209.9 7.5 %convolution_convert_fusion.1 = bf16[1536,1536]{1,0:T(8,128)(2,1)S(1)} fusion(bf16[1024,3072]{1,0:T(8,128)(2,1)} %get-tuple-element.139.mixed_ref, bf16[1,1024,1536]{2,1,0:T(8,128)(2,1)S(1)} %copy-done.35), kind=kOutput, calls=%fused_computation.2 | convolution fusion | flops 4834197504 | bytes 11010048 | tf_op jit(solution)/shard_map/dot_general | solution.py:814
  221.6 8.5 %convolution_convert_fusion.3 = bf16[3072,768]{1,0:T(8,128)(2,1)S(1)} fusion(bf16[1024,3072]{1,0:T(8,128)(2,1)} %get-tuple-element.127.dgate_ref, bf16[1024,1536]{1,0:T(8,128)(2,1)S(1)} %copy-done.36), kind=kOutput, calls=%fused_computation.8 | convolution fusion | flops 4834197504 | bytes 12582912 | tf_op jit(solution)/shard_map/dot_general | solution.py:814
  233.7 31.7 %scan_backward.3 = (bf16[1024,1024]{1,0:T(8,128)(2,1)}, f32[4,1024]{1,0:T(4,128)S(1)}, f32[1,1024]{1,0:T(1,128)S(1)}, f32[1,1024]{1,0:T(1,128)S(1)}, f32[8,128]{...) custom-call(f32[1024,3456]{1,0:T(8,128)} %get-tuple-element.90.proj_ref.tail_ref, ...), custom_call_target="tpu_custom_call" | custom-call | flops 40000000000 | bytes 40000000 | tf_op jit(solution)/shard_map/scan_backward/pallas_call | solution.py:636
  265.5 5.5 convolution_convert_fusion.8
  272.6 5.0 convolution_convert_fusion.9
  284.0 31.5 %scan_backward.4 = (bf16[1024,1024]{1,0:T(8,128)(2,1)}, f32[4,1024]{1,0:T(4,128)S(1)}, f32[1,1024]{1,0:T(1,128)S(1)}, f32[1,1024]{1,0:T(1,128)S(1)}, f32[8,128]{...) custom-call(f32[1024,3456]{1,0:T(8,128)} %get-tuple-element.90.proj_ref.tail_ref, ...), custom_call_target="tpu_custom_call" | custom-call | flops 40000000000 | bytes 40000000 | tf_op jit(solution)/shard_map/scan_backward/pallas_call | solution.py:636
  333.0 4.8 add_convert_fusion.2
  341.4 34.1 %scan_backward.5 = (bf16[1024,1408]{1,0:T(8,128)(2,1)}, f32[4,1280]{1,0:T(4,128)S(1)}, f32[1,1280]{1,0:T(1,128)S(1)}, f32[1,1024]{1,0:T(1,128)S(1)}, f32[8,128]{1,0:T(8,128)S(1)}) custom-call(f32[1024,3456]{1,0:T(8,128)} %get-tuple-element.90.proj_ref.tail_ref, f32[1024,3456]{1,0:T(8,128)} %get-tuple-element.90.proj_ref.tail_ref, ...), custom_call_target="tpu_custom_call" | custom-call | flops 40000000000 | bytes 40000000 | tf_op jit(solution)/shard_map/scan_backward/pallas_call | solution.py:636
  379.0 5.7 convolution_convert_fusion.4
  399.0 20.5 %gate_back.1.part_ref = f32[1024,1536]{1,0:T(8,128)} custom-call(s32[2]{0:T(128)S(1)} %copy-done.7, bf16[1024,3072]{1,0:T(8,128)(2,1)} %get-tuple-element.127.dgate_ref, bf16[3072,384]{1,0:T(8,128)(2,1)S(1)} %copy-done.1, bf16[1536,384]{1,0:T(8,128)(2,1)} %collective-permute-done.12.rest_1_, bf16[1536,384]{1,0:T(8,128)(2,1)} %collective-permute-done.13.rest_2_, ...), custom_call_target="tpu_custom_call" | custom-call | flops 16000000000 | bytes 22000000 | tf_op jit(solution)/shard_map/gate_back/pallas_call | solution.py:344
  433.0 27.6 %input_back.1 = (f32[1024,1536]{1,0:T(8,128)}, f32[1,1536]{1,0:T(1,128)S(1)}) custom-call(s32[2]{0:T(128)S(1)} %copy-done.7, f32[1024,1536]{1,0:T(8,128)} %gate_back.1.part_ref, bf16[1024,1536]{1,0:T(8,128)(2,1)} %bitcast.46, bf16[1024,1536]{1,0:T(8,128)(2,1)} %bitcast.56, f32[1,1536]{1,0:T(1,128)S(1)} %bitcast.42, ...), custom_call_target="tpu_custom_call" | custom-call | flops 22000001024 | bytes 46000000 | tf_op jit(solution)/shard_map/input_back/pallas_call | solution.py:400
  464.9 5.7 collective-permute-start.42
  474.0 20.9 %project_out.1 = bf16[1024,1536]{1,0:T(8,128)(2,1)} custom-call(s32[2]{0:T(128)S(1)} %copy-done.7, bf16[1024,3072]{1,0:T(8,128)(2,1)} %get-tuple-element.139.mixed_ref, bf16[1024,1536]{1,0:T(8,128)(2,1)S(1)} %bitcast.47, bf16[768,1536]{1,0:T(8,128)(2,1)} %rest_0_.1, bf16[768,1536]{1,0:T(8,128)(2,1)} %collective-permute-done.17.rest_7_.rest_1_, ...), custom_call_target="tpu_custom_call" | custom-call | flops 14000000000 | bytes 20000000 | tf_op jit(solution)/shard_map/project_out/pallas_call | solution.py:435
  504.5 16.1 %collective-permute-start.52 = (bf16[432,384]{1,0:T(8,128)(2,1)S(1)}, bf16[432,384]{1,0:T(8,128)(2,1)S(1)}, u32[]{:S(2)}, u32[]{:S(2)}) collective-permute-start(bf16[432,384]{1,0:T(8,128)(2,1)S(1)} %add_convert_fusion.6), channel_id=1, source_target_pairs={{0,4},{1,5},{2,6},{3,7},{4,0},{5,1},{6,2},{7,3},{8,12},{9,13},{10,... | collective-permute-start | bytes 995336 | tf_op jit(solution)/shard_map/ppermute | solution.py:672
  547.3 23.9 %collective-permute-done.54 = bf16[1728,384]{1,0:T(8,128)(2,1)} collective-permute-done((bf16[1728,384]{1,0:T(8,128)(2,1)}, bf16[1728,384]{1,0:T(8,128)(2,1)}, u32[]{:S(2)}, u32[]{:S(2)}) %collective-permute-start.54) | collective-permute-done | bytes 1327136 | tf_op jit(solution)/shard_map/ppermute | solution.py:672
  (290 shorter events, 157.5 us)
Async XLA Ops:
  12.0 31.8 %collective-permute-start.3 = (bf16[864,384]{1,0:T(8,128)(2,1)}, bf16[864,384]{1,0:T(8,128)(2,1)}, u32[]{:S(2)}, u32[]{:S(2)}) collective-permute-start(bf16[864,384]{1,0:T(8,128)(2,1)} %get-tuple-element.187), channel_id=1, source_target_pairs={{0,16},{8,24},{16,0},{24,8},{1,17},{9,25},{17,1},{25,9},{2,18},{10... | collective-permute-start | bytes 1990664 | tf_op jit(solution)/shard_map/ppermute | solution.py:672
  15.6 47.6 %collective-permute-start.7 = (bf16[3456,384]{1,0:T(8,128)(2,1)}, bf16[3456,384]{1,0:T(8,128)(2,1)}, u32[]{:S(2)}, u32[]{:S(2)}) collective-permute-start(bf16[3456,384]{1,0:T(8,128)(2,1)} %pad.8.rest_0_.rest_3_), channel_id=1, source_target_pairs={{0,8},{8,0},{16,24},{24,16},{1,9},{9,1},{17,25},{25,17},{2,10},{10... | collective-permute-start | bytes 7962632 | tf_op jit(solution)/shard_map/ppermute | solution.py:672
  62.6 80.5 %collective-permute-start.14 = (bf16[3072,384]{1,0:T(8,128)(2,1)S(1)}, bf16[3072,384]{1,0:T(8,128)(2,1)}, u32[]{:S(2)}, u32[]{:S(2)}) collective-permute-start(bf16[3072,384]{1,0:T(8,128)(2,1)S(1)} %slice.121.rest_0_), channel_id=1, source_target_pairs={{0,8},{8,0},{16,24},{24,16},{1,9},{9,1},{17,25},{25,17},{2,10},{10... | collective-permute-start | bytes 7077896 | tf_op jit(solution)/shard_map/ppermute | solution.py:672
  63.2 79.9 %collective-permute-start.18 = (bf16[768,1536]{1,0:T(8,128)(2,1)}, bf16[768,1536]{1,0:T(8,128)(2,1)}, u32[]{:S(2)}, u32[]{:S(2)}) collective-permute-start(bf16[768,1536]{1,0:T(8,128)(2,1)} %rest_0_.1), channel_id=1, source_target_pairs={{0,8},{8,0},{16,24},{24,16},{1,9},{9,1},{17,25},{25,17},{2,10},{10... | collective-permute-start | bytes 7077896 | tf_op jit(solution)/shard_map/ppermute | solution.py:672
  63.8 78.7 %collective-permute-start.17 = (bf16[768,1536]{1,0:T(8,128)(2,1)}, bf16[768,1536]{1,0:T(8,128)(2,1)}, u32[]{:S(2)}, u32[]{:S(2)}) collective-permute-start(bf16[768,1536]{1,0:T(8,128)(2,1)} %rest_0_.1), channel_id=1, source_target_pairs={{0,16},{8,24},{16,0},{24,8},{1,17},{9,25},{17,1},{25,9},{2,18},{10... | collective-permute-start | bytes 7077896 | tf_op jit(solution)/shard_map/ppermute | solution.py:672
  92.2 50.8 %collective-permute-start.13 = (bf16[1536,384]{1,0:T(8,128)(2,1)}, bf16[1536,384]{1,0:T(8,128)(2,1)}, u32[]{:S(2)}, u32[]{:S(2)}) collective-permute-start(bf16[1536,384]{1,0:T(8,128)(2,1)} %collective-permute-done.12.rest_1_), channel_id=1, source_target_pairs={{0,1},{1,0},{2,3},{3,2},{4,5},{5,4},{6,7},{7,6},{8,9},{9,8},{10,11... | collective-permute-start | bytes 3538952 | tf_op jit(solution)/shard_map/ppermute | solution.py:672
  221.1 56.6 %collective-permute-start.23 = (bf16[768,1536]{1,0:T(8,128)(2,1)}, bf16[768,1536]{1,0:T(8,128)(2,1)}, u32[]{:S(2)}, u32[]{:S(2)}) collective-permute-start(bf16[768,1536]{1,0:T(8,128)(2,1)} %get-tuple-element.164), channel_id=1, source_target_pairs={{0,16},{8,24},{16,0},{24,8},{1,17},{9,25},{17,1},{25,9},{2,18},{10... | collective-permute-start | bytes 7077896 | tf_op jit(solution)/shard_map/ppermute | solution.py:672
  271.1 56.1 %collective-permute-start.25 = (bf16[3072,384]{1,0:T(8,128)(2,1)}, bf16[3072,384]{1,0:T(8,128)(2,1)}, u32[]{:S(2)}, u32[]{:S(2)}) collective-permute-start(bf16[3072,384]{1,0:T(8,128)(2,1)} %get-tuple-element.162), channel_id=1, source_target_pairs={{0,16},{8,24},{16,0},{24,8},{1,17},{9,25},{17,1},{25,9},{2,18},{10... | collective-permute-start | bytes 7077896 | tf_op jit(solution)/shard_map/ppermute | solution.py:672
  281.5 34.0 %collective-permute-start.24 = (bf16[384,1536]{1,0:T(8,128)(2,1)S(1)}, bf16[384,1536]{1,0:T(8,128)(2,1)S(1)}, u32[]{:S(2)}, u32[]{:S(2)}) collective-permute-start(bf16[384,1536]{1,0:T(8,128)(2,1)S(1)} %get-tuple-element.170), channel_id=1, source_target_pairs={{0,1},{1,0},{2,3},{3,2},{4,5},{5,4},{6,7},{7,6},{8,9},{9,8},{10,11... | collective-permute-start | bytes 3538952 | tf_op jit(solution)/shard_map/ppermute | solution.py:672
  322.7 53.7 %collective-permute-start.29 = (bf16[96,1536]{1,0:T(8,128)(2,1)}, bf16[96,1536]{1,0:T(8,128)(2,1)S(1)}, u32[]{:S(2)}, u32[]{:S(2)}) collective-permute-start(bf16[96,1536]{1,0:T(8,128)(2,1)} %get-tuple-element.183), channel_id=1, source_target_pairs={{0,2},{1,3},{2,0},{3,1},{4,6},{5,7},{6,4},{7,5},{8,10},{9,11},{10,... | collective-permute-start | bytes 884744 | tf_op jit(solution)/shard_map/ppermute | solution.py:672
  324.4 52.2 %collective-permute-start.30 = (bf16[96,1536]{1,0:T(8,128)(2,1)}, bf16[96,1536]{1,0:T(8,128)(2,1)S(1)}, u32[]{:S(2)}, u32[]{:S(2)}) collective-permute-start(bf16[96,1536]{1,0:T(8,128)(2,1)} %get-tuple-element.182), channel_id=1, source_target_pairs={{0,4},{1,5},{2,6},{3,7},{4,0},{5,1},{6,2},{7,3},{8,12},{9,13},{10,... | collective-permute-start | bytes 884744 | tf_op jit(solution)/shard_map/ppermute | solution.py:672
  327.0 49.6 %collective-permute-start.31 = (bf16[96,1536]{1,0:T(8,128)(2,1)}, bf16[96,1536]{1,0:T(8,128)(2,1)S(1)}, u32[]{:S(2)}, u32[]{:S(2)}) collective-permute-start(bf16[96,1536]{1,0:T(8,128)(2,1)} %get-tuple-element.181), channel_id=1, source_target_pairs={{0,6},{1,7},{2,4},{3,5},{4,2},{5,3},{6,0},{7,1},{8,14},{9,15},{10,... | collective-permute-start | bytes 884744 | tf_op jit(solution)/shard_map/ppermute | solution.py:672
  340.0 35.4 %collective-permute-start.28 = (bf16[1536,384]{1,0:T(8,128)(2,1)S(1)}, bf16[1536,384]{1,0:T(8,128)(2,1)S(1)}, u32[]{:S(2)}, u32[]{:S(2)}) collective-permute-start(bf16[1536,384]{1,0:T(8,128)(2,1)S(1)} %get-tuple-element.168), channel_id=1, source_target_pairs={{0,1},{1,0},{2,3},{3,2},{4,5},{5,4},{6,7},{7,6},{8,9},{9,8},{10,11... | collective-permute-start | bytes 3538952 | tf_op jit(solution)/shard_map/ppermute | solution.py:672
  340.8 35.7 %collective-permute-start.27 = (bf16[2048,384]{1,0:T(8,128)(2,1)S(1)}, bf16[2048,384]{1,0:T(8,128)(2,1)S(1)}, u32[]{:S(2)}, u32[]{:S(2)}) collective-permute-start(bf16[2048,384]{1,0:T(8,128)(2,1)S(1)} %get-tuple-element.171), channel_id=1, source_target_pairs={{0,16},{8,24},{16,0},{24,8},{1,17},{9,25},{17,1},{25,9},{2,18},{10... | collective-permute-start | bytes 4718600 | tf_op jit(solution)/shard_map/ppermute | solution.py:672
  387.3 32.3 %collective-permute-start.34 = (bf16[384,384]{1,0:T(8,128)(2,1)}, bf16[384,384]{1,0:T(8,128)(2,1)S(1)}, u32[]{:S(2)}, u32[]{:S(2)}) collective-permute-start(bf16[384,384]{1,0:T(8,128)(2,1)} %get-tuple-element.180), channel_id=1, source_target_pairs={{0,2},{1,3},{2,0},{3,1},{4,6},{5,7},{6,4},{7,5},{8,10},{9,11},{10,... | collective-permute-start | bytes 884744 | tf_op jit(solution)/shard_map/ppermute | solution.py:672
  388.3 31.3 %collective-permute-start.35 = (bf16[384,384]{1,0:T(8,128)(2,1)}, bf16[384,384]{1,0:T(8,128)(2,1)S(1)}, u32[]{:S(2)}, u32[]{:S(2)}) collective-permute-start(bf16[384,384]{1,0:T(8,128)(2,1)} %get-tuple-element.179), channel_id=1, source_target_pairs={{0,4},{1,5},{2,6},{3,7},{4,0},{5,1},{6,2},{7,3},{8,12},{9,13},{10,... | collective-permute-start | bytes 884744 | tf_op jit(solution)/shard_map/ppermute | solution.py:672
  391.8 39.0 %collective-permute-start.38 = (bf16[96,1536]{1,0:T(8,128)(2,1)S(1)}, bf16[96,1536]{1,0:T(8,128)(2,1)S(1)}, u32[]{:S(2)}, u32[]{:S(2)}) collective-permute-start(bf16[96,1536]{1,0:T(8,128)(2,1)S(1)} %add_convert_fusion.11), channel_id=1, source_target_pairs={{0,2},{1,3},{2,0},{3,1},{4,6},{5,7},{6,4},{7,5},{8,10},{9,11},{10,... | collective-permute-start | bytes 884744 | tf_op jit(solution)/shard_map/ppermute | solution.py:672
  421.1 39.6 %collective-permute-start.39 = (bf16[384,384]{1,0:T(8,128)(2,1)S(1)}, bf16[384,384]{1,0:T(8,128)(2,1)S(1)}, u32[]{:S(2)}, u32[]{:S(2)}) collective-permute-start(bf16[384,384]{1,0:T(8,128)(2,1)S(1)} %add_convert_fusion.10), channel_id=1, source_target_pairs={{0,2},{1,3},{2,0},{3,1},{4,6},{5,7},{6,4},{7,5},{8,10},{9,11},{10,... | collective-permute-start | bytes 884744 | tf_op jit(solution)/shard_map/ppermute | solution.py:672
  422.8 37.9 %collective-permute-start.40 = (bf16[384,384]{1,0:T(8,128)(2,1)S(1)}, bf16[384,384]{1,0:T(8,128)(2,1)S(1)}, u32[]{:S(2)}, u32[]{:S(2)}) collective-permute-start(bf16[384,384]{1,0:T(8,128)(2,1)S(1)} %add_convert_fusion.10), channel_id=1, source_target_pairs={{0,4},{1,5},{2,6},{3,7},{4,0},{5,1},{6,2},{7,3},{8,12},{9,13},{10,... | collective-permute-start | bytes 884744 | tf_op jit(solution)/shard_map/ppermute | solution.py:672
  425.1 35.7 %collective-permute-start.41 = (bf16[384,384]{1,0:T(8,128)(2,1)S(1)}, bf16[384,384]{1,0:T(8,128)(2,1)S(1)}, u32[]{:S(2)}, u32[]{:S(2)}) collective-permute-start(bf16[384,384]{1,0:T(8,128)(2,1)S(1)} %add_convert_fusion.10), channel_id=1, source_target_pairs={{0,6},{1,7},{2,4},{3,5},{4,2},{5,3},{6,0},{7,1},{8,14},{9,15},{10,... | collective-permute-start | bytes 884744 | tf_op jit(solution)/shard_map/ppermute | solution.py:672
  430.9 64.0 %collective-permute-start.55 = (bf16[192,1536]{1,0:T(8,128)(2,1)S(1)}, bf16[192,1536]{1,0:T(8,128)(2,1)S(1)}, u32[]{:S(2)}, u32[]{:S(2)}) collective-permute-start(bf16[192,1536]{1,0:T(8,128)(2,1)S(1)} %pad_maximum_fusion.9), channel_id=1, source_target_pairs={{0,4},{1,5},{2,6},{3,7},{4,0},{5,1},{6,2},{7,3},{8,12},{9,13},{10,... | collective-permute-start | bytes 1769480 | tf_op jit(solution)/shard_map/ppermute | solution.py:672
  464.2 35.4 %collective-permute-start.43 = (bf16[1536,384]{1,0:T(8,128)(2,1)}, bf16[1536,384]{1,0:T(8,128)(2,1)}, u32[]{:S(2)}, u32[]{:S(2)}) collective-permute-start(bf16[1536,384]{1,0:T(8,128)(2,1)} %pad_maximum_fusion.7), channel_id=1, source_target_pairs={{0,1},{1,0},{2,3},{3,2},{4,5},{5,4},{6,7},{7,6},{8,9},{9,8},{10,11... | collective-permute-start | bytes 3538952 | tf_op jit(solution)/shard_map/ppermute | solution.py:672
  464.9 34.7 %collective-permute-start.42 = (bf16[432,384]{1,0:T(8,128)(2,1)}, bf16[432,384]{1,0:T(8,128)(2,1)}, u32[]{:S(2)}, u32[]{:S(2)}) collective-permute-start(bf16[432,384]{1,0:T(8,128)(2,1)} %get-tuple-element.177), channel_id=1, source_target_pairs={{0,2},{1,3},{2,0},{3,1},{4,6},{5,7},{6,4},{7,5},{8,10},{9,11},{10,... | collective-permute-start | bytes 995336 | tf_op jit(solution)/shard_map/ppermute | solution.py:672
  501.2 33.0 %collective-permute-start.51 = (bf16[432,384]{1,0:T(8,128)(2,1)S(1)}, bf16[432,384]{1,0:T(8,128)(2,1)S(1)}, u32[]{:S(2)}, u32[]{:S(2)}) collective-permute-start(bf16[432,384]{1,0:T(8,128)(2,1)S(1)} %add_convert_fusion.6), channel_id=1, source_target_pairs={{0,6},{1,7},{2,4},{3,5},{4,2},{5,3},{6,0},{7,1},{8,14},{9,15},{10,... | collective-permute-start | bytes 995336 | tf_op jit(solution)/shard_map/ppermute | solution.py:672
  (74 other events, 903.4 us)

commit v6 on v5

--- a/solution.py
+++ b/solution.py
@@ -889,40 +889,37 @@
     marks = marks + g.step(g.value)
 
     blocks = heads // per
-    cuts = [blocks * v // 3 for v in range(4)]
+    cuts = [0, blocks // 2, blocks]
     chains, grads, carried = [o, g], [], None
-    for index in range(3):
+    for index in range(2):
         low, high = cuts[index], cuts[index + 1]
         found = run_scan_backward(
             proj, sums, scan_out, after(dscan, *marks), starts, cw, vec, skip_cols, pick, inner, nstate, low,
-            high - low, per, carried, index == 2)
+            high - low, per, carried, index == 1)
         grads.append(found[:5])
         carried = tuple(found[5:])
         dproj, marks = found[0], []
         if index == 1:
             marks = o.step(dproj)
-        if index == 2:
-            marks = ab.coming + g.step(dproj)
-            marks = marks + o.step(dproj, *marks)
+            marks = marks + g.step(dproj, *marks) + chains[2].coming
         dproj = after(dproj, *marks)
         sent = outer(dproj, right)
-        kept = outer(after(dproj, sent, *g.coming) if index == 1 else dproj, left)
+        kept = outer(dproj, left)
         new = chain(kept, sent, 1)
         chains.append(new)
         if index == 0:
-            marks = marks + new.coming + o.step(kept)
-        if index == 1:
-            ab = Total.join(chains[2:])
-            marks = marks + ab.step(kept)
-            marks = marks + g.step(kept, *marks)
-        if index == 2:
-            marks = marks + new.step(kept)
+            marks = o.step(kept)
+        marks = marks + new.step(kept, *marks)
+    a, c = chains[2:]
 
     part = run_gate_back(place, after(dgate, *marks), model, wg)
-    abc = Total.join([ab, chains[4]])
     marks = g.step(part)
-    marks = marks + abc.step(part, *marks)
     marks = marks + o.step(part, *marks)
+    output = run_project_out(place, after(mixed, *marks), tok, ow)
+    abc = Total.join([a, c])
+    marks = g.step(output)
+    marks = marks + abc.step(output, *marks)
+    marks = marks + o.step(output, *marks)
     input_grad, dgain = run_input_back(place, after(part, *marks), [v[0] for v in grads], tok, cot, gain, wc, order)
 
     dcw = jnp.concatenate([v[1] for v in grads], axis=1)
@@ -935,14 +932,11 @@
     flat = jnp.concatenate([dgain[0].reshape(groups, -1), flat], axis=1)
     marks = abc.step(dgain, *g.coming)
     marks = marks + g.step(*marks)
-    output = run_project_out(place, after(mixed, *marks), tok, ow)
-    marks = abc.step(output, *g.coming)
-    o.step(output)
-    flat = after(flat, output, *marks)
+    flat = after(flat, *marks)
     for axis, size in (("shard", groups), ("rep", copies)):
         for bit in bits_of(size):
             flat = flat + swap(flat, axis, bit, size)
-    for old in (g, o, abc):
+    for old in (abc, g, o):
         while not old.done():
             old.step()
 

time: 586 us -> 600 us (1.024)
  waiting for transfers between devices: 73.9 us -> 121 us
  starting transfers between devices: 78.3 us -> 58.9 us
  Pallas kernels: 281 us -> 273 us
  matrix products: 62 us -> 54.9 us
    ppermute x57 -> x56, waiting for transfers between devices: 73.9 us -> 121 us  [swap(): return lax.ppermute(value, axis, [(i, i ^ bit) for i in range(size)])]
    ppermute x57 -> x56, starting transfers between devices: 78.3 us -> 58.9 us  [swap(): return lax.ppermute(value, axis, [(i, i ^ bit) for i in range(size)])]
    pallas_call x3 -> x2, Pallas kernels: 97.2 us -> 88.7 us  [run_scan_backward(): pl.pallas_call(functools.partial(scan_backward, nstate=nstate, low=low, g...]
    dot_general x10 -> x8, matrix products: 62 us -> 54.9 us  [outer(): lax.dot_general(left, right, (((0,), (0,)), ((), ())), preferred_element_...]
    add x4 -> x5, other arithmetic: 13.2 us -> 19.6 us  [step(): sum((lax.dynamic_slice_in_dim(v, start, size, axis).astype(F32) for v in...]
  transfers between devices with their start and end apart: 57 -> 56, of which waited for: 12 -> 16; matrix products, arithmetic and copies ran while one was open for 19% -> 19% of each run, Pallas kernels for 41% -> 39%
where the time goes in v6:
time: 600 us; the launch traced here: 592 us
  Pallas kernels  273 us (46%)
  waiting for transfers between devices  121 us (20%)
  other arithmetic  61.2 us (10%)
  starting transfers between devices  58.9 us (10%)
  matrix products  54.9 us (9%)
  local copies, waits for them, and re-layouts  21.4 us (4%)
    ppermute x56, waiting for transfers between devices, swap(): return lax.ppermute(value, axis, [(i, i ^ bit) for i in range(size)])  121 us
    pallas_call x2, Pallas kernels, run_scan_backward(): pl.pallas_call(functools.partial(scan_backward, nstate=nstate, low=low, g...  88.7 us
    ppermute x56, starting transfers between devices, swap(): return lax.ppermute(value, axis, [(i, i ^ bit) for i in range(size)])  58.9 us
    dot_general x8, matrix products, outer(): lax.dot_general(left, right, (((0,), (0,)), ((), ())), preferred_element_...  54.9 us
    pallas_call x1, Pallas kernels, run_scan_forward(): pl.pallas_call(functools.partial(scan_forward, inner=inner, nstate=nstate...  48.7 us
    pallas_call x1, Pallas kernels, run_gating(): pl.pallas_call(functools.partial(gating, wg_pieces=wg_pieces, ow_pieces=o...  42.1 us
    pallas_call x1, Pallas kernels, run_input_back(): pl.pallas_call(functools.partial(input_back, count=len(dprojs), pieces=pi...  27.3 us
    pallas_call x1, Pallas kernels, run_project_in(): pl.pallas_call(functools.partial(project_in, pieces=pieces, order=order),...  24.3 us
  transfers between devices with their start and end apart: 56, of which 16 were waited for; matrix products, arithmetic and copies ran while one was open for 19% of the time, Pallas kernels for 39%

profile of v6, /device:TPU:0, one launch (start us, length us, event | category | flops | bytes accessed | tf_op | source)
XLA Modules:
  0.0 591.7 jit_solution(17706643511555611453)
XLA Ops:
  21.0 8.9 %collective-permute-done.3.rest_1_.rest_3_ = bf16[864,384]{1,0:T(8,128)(2,1)} collective-permute-done((bf16[864,384]{1,0:T(8,128)(2,1)}, bf16[864,384]{1,0:T(8,128)(2,1)}, u32[]{:S(2)}, u32[]{:S(2)}) %collective-permute-start.3) | collective-permute-done | bytes 663584 | tf_op jit(solution)/shard_map/ppermute | solution.py:672
  31.5 12.2 %collective-permute-done.4.rest_2_.rest_4_ = bf16[864,384]{1,0:T(8,128)(2,1)} collective-permute-done((bf16[864,384]{1,0:T(8,128)(2,1)}, bf16[864,384]{1,0:T(8,128)(2,1)}, u32[]{:S(2)}, u32[]{:S(2)}) %collective-permute-start.4) | collective-permute-done | bytes 663584 | tf_op jit(solution)/shard_map/ppermute | solution.py:672
  50.1 10.4 %collective-permute-done.6.rest_4_.rest_6_ = bf16[864,384]{1,0:T(8,128)(2,1)} collective-permute-done((bf16[864,384]{1,0:T(8,128)(2,1)}, bf16[864,384]{1,0:T(8,128)(2,1)}, u32[]{:S(2)}, u32[]{:S(2)}) %collective-permute-start.6) | collective-permute-done | bytes 663584 | tf_op jit(solution)/shard_map/ppermute | solution.py:672
  65.3 24.3 %project_in.1 = (bf16[1024,1536]{1,0:T(8,128)(2,1)}, f32[1024,3456]{1,0:T(8,128)}) custom-call(s32[2]{0:T(128)S(1)} %pad_add_fusion.place_ref, bf16[1024,1536]{1,0:T(8,128)(2,1)} %bitcast.39, f32[1,1536]{1,0:T(1,128)S(1)} %bitcast.37, bf16[3456,384]{1,0:T(8,128)(2,1)} %pad.8.rest_0_.rest_2_, bf16[864,384]{1,0:T(8,128)(2,1)} %collective-permute-done.3.rest_1_.rest_3_, ...), custom_call_target="tpu_custom_call" | custom-call | flops 20000000000 | bytes 30000000 | tf_op jit(solution)/shard_map/project_in/pallas_call | solution.py:222
  93.8 48.7 %scan_forward.1 = (f32[1024,3072]{1,0:T(8,128)}, f32[1024,3328]{1,0:T(8,128)}, bf16[1024,3072]{1,0:T(8,128)(2,1)}) custom-call(f32[1024,3456]{1,0:T(8,128)} %get-tuple-element.75.proj_ref.tail_ref, f32[4,3328]{1,0:T(4,128)} %reshape.117.cw_ref.cwk_ref, f32[1,3328]{1,0:T(1,128)} %broadcast_in_dim_reshape.13.cb_ref, f32[8,128]{1,0:T(8,128)} %select_maximum_fusion.vec_ref, ...), custom_call_target="tpu_custom_call" | custom-call | flops 12000000000 | bytes 60000000 | tf_op jit(solution)/shard_map/scan_forward/pallas_call | solution.py:127
  143.1 6.0 %collective-permute-done.15.rest_4_ = bf16[1536,384]{1,0:T(8,128)(2,1)} collective-permute-done((bf16[1536,384]{1,0:T(8,128)(2,1)}, bf16[1536,384]{1,0:T(8,128)(2,1)}, u32[]{:S(2)}, u32[]{:S(2)}) %collective-permute-start.15) | collective-permute-done | bytes 1179680 | tf_op jit(solution)/shard_map/ppermute | solution.py:672
  150.7 42.1 %gating.1 = (bf16[1024,3072]{1,0:T(8,128)(2,1)}, f32[1024,3072]{1,0:T(8,128)}, bf16[1024,3072]{1,0:T(8,128)(2,1)}, f32[1,3072]{1,0:T(1,128)}) custom-call(s32[2]{0:T(128)} %copy-done.6, bf16[1024,1536]{1,0:T(8,128)(2,1)} %get-tuple-element.71.normed_ref, bf16[1024,1536]{1,0:T(8,128)(2,1)} %bitcast.49, f32[1024,3072]{1,0:T(8,128)} %get-tuple-element.76.scan_ref.out_ref, ...), custom_call_target="tpu_custom_call" | custom-call | flops 40000000000 | bytes 70000000 | tf_op jit(solution)/shard_map/gating/pallas_call | solution.py:305
  192.9 7.8 %convolution_convert_fusion = bf16[1536,1536]{1,0:T(8,128)(2,1)S(1)} fusion(bf16[1024,3072]{1,0:T(8,128)(2,1)} %get-tuple-element.106.mixed_ref, bf16[1,1024,1536]{2,1,0:T(8,128)(2,1)} %param.21), kind=kOutput, calls=%fused_computation.1 | convolution fusion | flops 4834197504 | bytes 11010048 | tf_op jit(solution)/shard_map/dot_general | solution.py:814
  200.9 8.7 %convolution_convert_fusion.2 = bf16[3072,768]{1,0:T(8,128)(2,1)S(1)} fusion(bf16[1024,3072]{1,0:T(8,128)(2,1)} %get-tuple-element.101.dgate_ref, bf16[1024,1536]{1,0:T(8,128)(2,1)S(1)} %copy-done.26), kind=kOutput, calls=%fused_computation.7 | convolution fusion | flops 4834197504 | bytes 12582912 | tf_op jit(solution)/shard_map/dot_general | solution.py:814
  210.0 7.8 %convolution_convert_fusion.1 = bf16[1536,1536]{1,0:T(8,128)(2,1)S(1)} fusion(bf16[1024,3072]{1,0:T(8,128)(2,1)} %get-tuple-element.106.mixed_ref, bf16[1,1024,1536]{2,1,0:T(8,128)(2,1)S(1)} %copy-done.25), kind=kOutput, calls=%fused_computation.2 | convolution fusion | flops 4834197504 | bytes 11010048 | tf_op jit(solution)/shard_map/dot_general | solution.py:814
  221.9 8.5 %convolution_convert_fusion.3 = bf16[3072,768]{1,0:T(8,128)(2,1)S(1)} fusion(bf16[1024,3072]{1,0:T(8,128)(2,1)} %get-tuple-element.101.dgate_ref, bf16[1024,1536]{1,0:T(8,128)(2,1)S(1)} %copy-done.26), kind=kOutput, calls=%fused_computation.8 | convolution fusion | flops 4834197504 | bytes 12582912 | tf_op jit(solution)/shard_map/dot_general | solution.py:814
  234.0 42.9 %scan_backward.2 = (bf16[1024,1536]{1,0:T(8,128)(2,1)}, f32[4,1536]{1,0:T(4,128)S(1)}, f32[1,1536]{1,0:T(1,128)S(1)}, f32[1,1536]{1,0:T(1,128)S(1)}, f32[8,128]{...) custom-call(f32[1024,3456]{1,0:T(8,128)} %get-tuple-element.75.proj_ref.tail_ref, ...), custom_call_target="tpu_custom_call" | custom-call | flops 40000000000 | bytes 40000000 | tf_op jit(solution)/shard_map/scan_backward/pallas_call | solution.py:636
  276.9 6.1 %convolution_convert_fusion.4 = bf16[1536,768]{1,0:T(8,128)(2,1)} fusion(bf16[1024,1536]{1,0:T(8,128)(2,1)} %get-tuple-element.89.rest_0_, bf16[1024,1536]{1,0:T(8,128)(2,1)S(1)} %copy-done.26), kind=kOutput, calls=%fused_computation.16 | convolution fusion | flops 2417098752 | bytes 7077888 | tf_op jit(solution)/shard_map/dot_general | solution.py:814
  300.1 45.9 %scan_backward.3 = (bf16[1024,1920]{1,0:T(8,128)(2,1)}, f32[4,1792]{1,0:T(4,128)S(1)}, f32[1,1792]{1,0:T(1,128)S(1)}, f32[1,1536]{1,0:T(1,128)S(1)}, f32[8,128]{1,0:T(8,128)S(1)}) custom-call(f32[1024,3456]{1,0:T(8,128)} %get-tuple-element.75.proj_ref.tail_ref, f32[1024,3456]{1,0:T(8,128)} %get-tuple-element.75.proj_ref.tail_ref, ...), custom_call_target="tpu_custom_call" | custom-call | flops 40000000000 | bytes 40000000 | tf_op jit(solution)/shard_map/scan_backward/pallas_call | solution.py:636
  349.5 12.8 %collective-permute-done.27 = bf16[1536,384]{1,0:T(8,128)(2,1)} collective-permute-done((bf16[1536,384]{1,0:T(8,128)(2,1)}, bf16[1536,384]{1,0:T(8,128)(2,1)}, u32[]{:S(2)}, u32[]{:S(2)}) %collective-permute-start.27) | collective-permute-done | bytes 1179680 | tf_op jit(solution)/shard_map/ppermute | solution.py:672
  362.2 5.1 convolution_convert_fusion.6
  375.3 5.9 convolution_convert_fusion.7
  384.0 20.5 %gate_back.1.part_ref = f32[1024,1536]{1,0:T(8,128)} custom-call(s32[2]{0:T(128)S(1)} %copy-done.7, bf16[1024,3072]{1,0:T(8,128)(2,1)} %get-tuple-element.101.dgate_ref, bf16[3072,384]{1,0:T(8,128)(2,1)S(1)} %copy-done.1, bf16[1536,384]{1,0:T(8,128)(2,1)} %collective-permute-done.12.rest_1_, bf16[1536,384]{1,0:T(8,128)(2,1)} %collective-permute-done.13.rest_2_, ...), custom_call_target="tpu_custom_call" | custom-call | flops 16000000000 | bytes 22000000 | tf_op jit(solution)/shard_map/gate_back/pallas_call | solution.py:344
  413.4 21.0 %project_out.1 = bf16[1024,1536]{1,0:T(8,128)(2,1)} custom-call(s32[2]{0:T(128)S(1)} %copy-done.7, bf16[1024,3072]{1,0:T(8,128)(2,1)} %get-tuple-element.106.mixed_ref, bf16[1024,1536]{1,0:T(8,128)(2,1)S(1)} %bitcast.41, bf16[768,1536]{1,0:T(8,128)(2,1)} %rest_0_.1, bf16[768,1536]{1,0:T(8,128)(2,1)} %collective-permute-done.17.rest_7_.rest_1_, ...), custom_call_target="tpu_custom_call" | custom-call | flops 14000000000 | bytes 20000000 | tf_op jit(solution)/shard_map/project_out/pallas_call | solution.py:435
  455.2 27.3 %input_back.1 = (f32[1024,1536]{1,0:T(8,128)}, f32[1,1536]{1,0:T(1,128)S(1)}) custom-call(s32[2]{0:T(128)S(1)} %copy-done.7, f32[1024,1536]{1,0:T(8,128)} %gate_back.1.part_ref, bf16[1024,1536]{1,0:T(8,128)(2,1)} %bitcast.40, bf16[1024,1536]{1,0:T(8,128)(2,1)} %bitcast.50, f32[1,1536]{1,0:T(1,128)S(1)} %bitcast.38, ...), custom_call_target="tpu_custom_call" | custom-call | flops 22000001024 | bytes 46000000 | tf_op jit(solution)/shard_map/input_back/pallas_call | solution.py:400
  505.5 11.7 %collective-permute-done.44 = f32[4,5348]{1,0:T(4,128)S(1)} collective-permute-done((f32[4,5348]{1,0:T(4,128)S(1)}, f32[4,5348]{1,0:T(4,128)S(1)}, u32[]{:S(2)}, u32[]{:S(2)}) %collective-permute-start.44) | collective-permute-done | bytes 85600 | tf_op jit(solution)/shard_map/ppermute | solution.py:672
  522.0 5.1 collective-permute-done.48
  541.9 14.8 %collective-permute-done.51 = bf16[432,384]{1,0:T(8,128)(2,1)S(1)} collective-permute-done((bf16[432,384]{1,0:T(8,128)(2,1)}, bf16[432,384]{1,0:T(8,128)(2,1)S(1)}, u32[]{:S(2)}, u32[]{:S(2)}) %collective-permute-start.51) | collective-permute-done | bytes 331808 | tf_op jit(solution)/shard_map/ppermute | solution.py:672
  565.7 21.2 %collective-permute-done.53 = bf16[1728,384]{1,0:T(8,128)(2,1)S(1)} collective-permute-done((bf16[1728,384]{1,0:T(8,128)(2,1)S(1)}, bf16[1728,384]{1,0:T(8,128)(2,1)S(1)}, u32[]{:S(2)}, u32[]{:S(2)}) %collective-permute-start.53) | collective-permute-done | bytes 1327136 | tf_op jit(solution)/shard_map/ppermute | solution.py:672
  (263 shorter events, 164.3 us)
Async XLA Ops:
  12.0 31.8 %collective-permute-start.4 = (bf16[864,384]{1,0:T(8,128)(2,1)}, bf16[864,384]{1,0:T(8,128)(2,1)}, u32[]{:S(2)}, u32[]{:S(2)}) collective-permute-start(bf16[864,384]{1,0:T(8,128)(2,1)} %get-tuple-element.156), channel_id=1, source_target_pairs={{0,16},{8,24},{16,0},{24,8},{1,17},{9,25},{17,1},{25,9},{2,18},{10... | collective-permute-start | bytes 1990664 | tf_op jit(solution)/shard_map/ppermute | solution.py:672
  15.6 47.6 %collective-permute-start.7 = (bf16[3456,384]{1,0:T(8,128)(2,1)}, bf16[3456,384]{1,0:T(8,128)(2,1)}, u32[]{:S(2)}, u32[]{:S(2)}) collective-permute-start(bf16[3456,384]{1,0:T(8,128)(2,1)} %pad.8.rest_0_.rest_2_), channel_id=1, source_target_pairs={{0,8},{8,0},{16,24},{24,16},{1,9},{9,1},{17,25},{25,17},{2,10},{10... | collective-permute-start | bytes 7962632 | tf_op jit(solution)/shard_map/ppermute | solution.py:672
  62.6 80.5 %collective-permute-start.14 = (bf16[3072,384]{1,0:T(8,128)(2,1)S(1)}, bf16[3072,384]{1,0:T(8,128)(2,1)}, u32[]{:S(2)}, u32[]{:S(2)}) collective-permute-start(bf16[3072,384]{1,0:T(8,128)(2,1)S(1)} %slice.121.rest_0_), channel_id=1, source_target_pairs={{0,8},{8,0},{16,24},{24,16},{1,9},{9,1},{17,25},{25,17},{2,10},{10... | collective-permute-start | bytes 7077896 | tf_op jit(solution)/shard_map/ppermute | solution.py:672
  63.2 79.9 %collective-permute-start.18 = (bf16[768,1536]{1,0:T(8,128)(2,1)}, bf16[768,1536]{1,0:T(8,128)(2,1)}, u32[]{:S(2)}, u32[]{:S(2)}) collective-permute-start(bf16[768,1536]{1,0:T(8,128)(2,1)} %rest_0_.1), channel_id=1, source_target_pairs={{0,8},{8,0},{16,24},{24,16},{1,9},{9,1},{17,25},{25,17},{2,10},{10... | collective-permute-start | bytes 7077896 | tf_op jit(solution)/shard_map/ppermute | solution.py:672
  63.8 78.7 %collective-permute-start.17 = (bf16[768,1536]{1,0:T(8,128)(2,1)}, bf16[768,1536]{1,0:T(8,128)(2,1)}, u32[]{:S(2)}, u32[]{:S(2)}) collective-permute-start(bf16[768,1536]{1,0:T(8,128)(2,1)} %rest_0_.1), channel_id=1, source_target_pairs={{0,16},{8,24},{16,0},{24,8},{1,17},{9,25},{17,1},{25,9},{2,18},{10... | collective-permute-start | bytes 7077896 | tf_op jit(solution)/shard_map/ppermute | solution.py:672
  92.2 50.8 %collective-permute-start.13 = (bf16[1536,384]{1,0:T(8,128)(2,1)}, bf16[1536,384]{1,0:T(8,128)(2,1)}, u32[]{:S(2)}, u32[]{:S(2)}) collective-permute-start(bf16[1536,384]{1,0:T(8,128)(2,1)} %collective-permute-done.12.rest_1_), channel_id=1, source_target_pairs={{0,1},{1,0},{2,3},{3,2},{4,5},{5,4},{6,7},{7,6},{8,9},{9,8},{10,11... | collective-permute-start | bytes 3538952 | tf_op jit(solution)/shard_map/ppermute | solution.py:672
  221.4 68.2 %collective-permute-start.23 = (bf16[768,1536]{1,0:T(8,128)(2,1)}, bf16[768,1536]{1,0:T(8,128)(2,1)}, u32[]{:S(2)}, u32[]{:S(2)}) collective-permute-start(bf16[768,1536]{1,0:T(8,128)(2,1)} %get-tuple-element.132), channel_id=1, source_target_pairs={{0,16},{8,24},{16,0},{24,8},{1,17},{9,25},{17,1},{25,9},{2,18},{10... | collective-permute-start | bytes 7077896 | tf_op jit(solution)/shard_map/ppermute | solution.py:672
  283.0 64.2 %collective-permute-start.22 = (bf16[3072,384]{1,0:T(8,128)(2,1)}, bf16[3072,384]{1,0:T(8,128)(2,1)S(1)}, u32[]{:S(2)}, u32[]{:S(2)}) collective-permute-start(bf16[3072,384]{1,0:T(8,128)(2,1)} %get-tuple-element.133), channel_id=1, source_target_pairs={{0,16},{8,24},{16,0},{24,8},{1,17},{9,25},{17,1},{25,9},{2,18},{10... | collective-permute-start | bytes 7077896 | tf_op jit(solution)/shard_map/ppermute | solution.py:672
  294.3 51.7 %collective-permute-start.25 = (bf16[384,1536]{1,0:T(8,128)(2,1)}, bf16[384,1536]{1,0:T(8,128)(2,1)S(1)}, u32[]{:S(2)}, u32[]{:S(2)}) collective-permute-start(bf16[384,1536]{1,0:T(8,128)(2,1)} %get-tuple-element.140), channel_id=1, source_target_pairs={{0,1},{1,0},{2,3},{3,2},{4,5},{5,4},{6,7},{7,6},{8,9},{9,8},{10,11... | collective-permute-start | bytes 3538952 | tf_op jit(solution)/shard_map/ppermute | solution.py:672
  299.6 62.7 %collective-permute-start.27 = (bf16[1536,384]{1,0:T(8,128)(2,1)}, bf16[1536,384]{1,0:T(8,128)(2,1)}, u32[]{:S(2)}, u32[]{:S(2)}) collective-permute-start(bf16[1536,384]{1,0:T(8,128)(2,1)} %get-tuple-element.144), channel_id=1, source_target_pairs={{0,16},{8,24},{16,0},{24,8},{1,17},{9,25},{17,1},{25,9},{2,18},{10... | collective-permute-start | bytes 3538952 | tf_op jit(solution)/shard_map/ppermute | solution.py:672
  369.6 34.9 %collective-permute-start.26 = (bf16[1536,384]{1,0:T(8,128)(2,1)}, bf16[1536,384]{1,0:T(8,128)(2,1)S(1)}, u32[]{:S(2)}, u32[]{:S(2)}) collective-permute-start(bf16[1536,384]{1,0:T(8,128)(2,1)} %get-tuple-element.137), channel_id=1, source_target_pairs={{0,1},{1,0},{2,3},{3,2},{4,5},{5,4},{6,7},{7,6},{8,9},{9,8},{10,11... | collective-permute-start | bytes 3538952 | tf_op jit(solution)/shard_map/ppermute | solution.py:672
  370.9 37.5 %collective-permute-start.31 = (bf16[96,1536]{1,0:T(8,128)(2,1)}, bf16[96,1536]{1,0:T(8,128)(2,1)S(1)}, u32[]{:S(2)}, u32[]{:S(2)}) collective-permute-start(bf16[96,1536]{1,0:T(8,128)(2,1)} %get-tuple-element.151), channel_id=1, source_target_pairs={{0,6},{1,7},{2,4},{3,5},{4,2},{5,3},{6,0},{7,1},{8,14},{9,15},{10,... | collective-permute-start | bytes 884744 | tf_op jit(solution)/shard_map/ppermute | solution.py:672
  374.6 34.7 %collective-permute-start.30 = (bf16[96,1536]{1,0:T(8,128)(2,1)}, bf16[96,1536]{1,0:T(8,128)(2,1)S(1)}, u32[]{:S(2)}, u32[]{:S(2)}) collective-permute-start(bf16[96,1536]{1,0:T(8,128)(2,1)} %get-tuple-element.152), channel_id=1, source_target_pairs={{0,4},{1,5},{2,6},{3,7},{4,0},{5,1},{6,2},{7,3},{8,12},{9,13},{10,... | collective-permute-start | bytes 884744 | tf_op jit(solution)/shard_map/ppermute | solution.py:672
  374.6 36.2 %collective-permute-start.29 = (bf16[96,1536]{1,0:T(8,128)(2,1)S(1)}, bf16[96,1536]{1,0:T(8,128)(2,1)S(1)}, u32[]{:S(2)}, u32[]{:S(2)}) collective-permute-start(bf16[96,1536]{1,0:T(8,128)(2,1)S(1)} %get-tuple-element.153), channel_id=1, source_target_pairs={{0,2},{1,3},{2,0},{3,1},{4,6},{5,7},{6,4},{7,5},{8,10},{9,11},{10,... | collective-permute-start | bytes 884744 | tf_op jit(solution)/shard_map/ppermute | solution.py:672
  409.2 32.9 %collective-permute-start.35 = (bf16[1920,384]{1,0:T(8,128)(2,1)S(1)}, bf16[1920,384]{1,0:T(8,128)(2,1)S(1)}, u32[]{:S(2)}, u32[]{:S(2)}) collective-permute-start(bf16[1920,384]{1,0:T(8,128)(2,1)S(1)} %get-tuple-element.142), channel_id=1, source_target_pairs={{0,16},{8,24},{16,0},{24,8},{1,17},{9,25},{17,1},{25,9},{2,18},{10... | collective-permute-start | bytes 4423688 | tf_op jit(solution)/shard_map/ppermute | solution.py:672
  412.1 37.0 %collective-permute-start.36 = (bf16[96,1536]{1,0:T(8,128)(2,1)S(1)}, bf16[96,1536]{1,0:T(8,128)(2,1)}, u32[]{:S(2)}, u32[]{:S(2)}) collective-permute-start(bf16[96,1536]{1,0:T(8,128)(2,1)S(1)} %add_convert_fusion.11), channel_id=1, source_target_pairs={{0,2},{1,3},{2,0},{3,1},{4,6},{5,7},{6,4},{7,5},{8,10},{9,11},{10,... | collective-permute-start | bytes 884744 | tf_op jit(solution)/shard_map/ppermute | solution.py:672
  435.7 47.6 %collective-permute-start.38 = (bf16[384,384]{1,0:T(8,128)(2,1)S(1)}, bf16[384,384]{1,0:T(8,128)(2,1)}, u32[]{:S(2)}, u32[]{:S(2)}) collective-permute-start(bf16[384,384]{1,0:T(8,128)(2,1)S(1)} %add_convert_fusion.10), channel_id=1, source_target_pairs={{0,2},{1,3},{2,0},{3,1},{4,6},{5,7},{6,4},{7,5},{8,10},{9,11},{10,... | collective-permute-start | bytes 884744 | tf_op jit(solution)/shard_map/ppermute | solution.py:672
  436.5 46.8 %collective-permute-start.39 = (bf16[384,384]{1,0:T(8,128)(2,1)S(1)}, bf16[384,384]{1,0:T(8,128)(2,1)}, u32[]{:S(2)}, u32[]{:S(2)}) collective-permute-start(bf16[384,384]{1,0:T(8,128)(2,1)S(1)} %add_convert_fusion.10), channel_id=1, source_target_pairs={{0,4},{1,5},{2,6},{3,7},{4,0},{5,1},{6,2},{7,3},{8,12},{9,13},{10,... | collective-permute-start | bytes 884744 | tf_op jit(solution)/shard_map/ppermute | solution.py:672
  438.8 44.6 %collective-permute-start.40 = (bf16[384,384]{1,0:T(8,128)(2,1)S(1)}, bf16[384,384]{1,0:T(8,128)(2,1)}, u32[]{:S(2)}, u32[]{:S(2)}) collective-permute-start(bf16[384,384]{1,0:T(8,128)(2,1)S(1)} %add_convert_fusion.10), channel_id=1, source_target_pairs={{0,6},{1,7},{2,4},{3,5},{4,2},{5,3},{6,0},{7,1},{8,14},{9,15},{10,... | collective-permute-start | bytes 884744 | tf_op jit(solution)/shard_map/ppermute | solution.py:672
  448.4 35.0 %collective-permute-start.37 = (bf16[1728,384]{1,0:T(8,128)(2,1)}, bf16[1728,384]{1,0:T(8,128)(2,1)}, u32[]{:S(2)}, u32[]{:S(2)}) collective-permute-start(bf16[1728,384]{1,0:T(8,128)(2,1)} %get-tuple-element.136), channel_id=1, source_target_pairs={{0,1},{1,0},{2,3},{3,2},{4,5},{5,4},{6,7},{7,6},{8,9},{9,8},{10,11... | collective-permute-start | bytes 3981320 | tf_op jit(solution)/shard_map/ppermute | solution.py:672
  452.8 46.2 %collective-permute-start.54 = (bf16[192,1536]{1,0:T(8,128)(2,1)}, bf16[192,1536]{1,0:T(8,128)(2,1)}, u32[]{:S(2)}, u32[]{:S(2)}) collective-permute-start(bf16[192,1536]{1,0:T(8,128)(2,1)} %pad_maximum_fusion.7), channel_id=1, source_target_pairs={{0,4},{1,5},{2,6},{3,7},{4,0},{5,1},{6,2},{7,3},{8,12},{9,13},{10,... | collective-permute-start | bytes 1769480 | tf_op jit(solution)/shard_map/ppermute | solution.py:672
  493.7 33.5 %collective-permute-start.48 = (bf16[432,384]{1,0:T(8,128)(2,1)}, bf16[432,384]{1,0:T(8,128)(2,1)S(1)}, u32[]{:S(2)}, u32[]{:S(2)}) collective-permute-start(bf16[432,384]{1,0:T(8,128)(2,1)} %get-tuple-element.146), channel_id=1, source_target_pairs={{0,4},{1,5},{2,6},{3,7},{4,0},{5,1},{6,2},{7,3},{8,12},{9,13},{10,... | collective-permute-start | bytes 995336 | tf_op jit(solution)/shard_map/ppermute | solution.py:672
  504.2 55.2 %collective-permute-start.55 = (bf16[384,1536]{1,0:T(8,128)(2,1)}, bf16[384,1536]{1,0:T(8,128)(2,1)}, u32[]{:S(2)}, u32[]{:S(2)}) collective-permute-start(bf16[384,1536]{1,0:T(8,128)(2,1)} %pad_maximum_fusion.6), channel_id=1, source_target_pairs={{0,1},{1,0},{2,3},{3,2},{4,5},{5,4},{6,7},{7,6},{8,9},{9,8},{10,11... | collective-permute-start | bytes 3538952 | tf_op jit(solution)/shard_map/ppermute | solution.py:672
  517.2 46.8 %collective-permute-start.46 = (bf16[1536,384]{1,0:T(8,128)(2,1)}, bf16[1536,384]{1,0:T(8,128)(2,1)}, u32[]{:S(2)}, u32[]{:S(2)}) collective-permute-start(bf16[1536,384]{1,0:T(8,128)(2,1)} %pad_maximum_fusion.5), channel_id=1, source_target_pairs={{0,1},{1,0},{2,3},{3,2},{4,5},{5,4},{6,7},{7,6},{8,9},{9,8},{10,11... | collective-permute-start | bytes 3538952 | tf_op jit(solution)/shard_map/ppermute | solution.py:672
  (63 other events, 959.6 us)

commit v7 on v5

--- a/solution.py
+++ b/solution.py
@@ -941,8 +941,10 @@
     flat = after(flat, output, *marks)
     for axis, size in (("shard", groups), ("rep", copies)):
         for bit in bits_of(size):
+            if axis == "rep" and bit == 2:
+                flat = after(flat, *abc.step())
             flat = flat + swap(flat, axis, bit, size)
-    for old in (g, o, abc):
+    for old in (abc, g, o):
         while not old.done():
             old.step()
 

time: 586 us -> 599 us (1.022)
  waiting for transfers between devices: 73.9 us -> 94.4 us
  starting transfers between devices: 78.3 us -> 66.6 us
    ppermute x57, waiting for transfers between devices: 73.9 us -> 94.4 us  [swap(): return lax.ppermute(value, axis, [(i, i ^ bit) for i in range(size)])]
    ppermute x57, starting transfers between devices: 78.3 us -> 66.6 us  [swap(): return lax.ppermute(value, axis, [(i, i ^ bit) for i in range(size)])]
  transfers between devices with their start and end apart: 57 -> 57, of which waited for: 12 -> 13; matrix products, arithmetic and copies ran while one was open for 19% -> 19% of each run, Pallas kernels for 41% -> 40%
where the time goes in v7:
time: 599 us; the launch traced here: 591 us
  Pallas kernels  281 us (47%)
  waiting for transfers between devices  94.4 us (16%)
  starting transfers between devices  66.6 us (11%)
  matrix products  62.2 us (10%)
  other arithmetic  61.5 us (10%)
  local copies, waits for them, and re-layouts  23.7 us (4%)
    pallas_call x3, Pallas kernels, run_scan_backward(): pl.pallas_call(functools.partial(scan_backward, nstate=nstate, low=low, g...  97 us
    ppermute x57, waiting for transfers between devices, swap(): return lax.ppermute(value, axis, [(i, i ^ bit) for i in range(size)])  94.4 us
    ppermute x57, starting transfers between devices, swap(): return lax.ppermute(value, axis, [(i, i ^ bit) for i in range(size)])  66.6 us
    dot_general x10, matrix products, outer(): lax.dot_general(left, right, (((0,), (0,)), ((), ())), preferred_element_...  62.2 us
    pallas_call x1, Pallas kernels, run_scan_forward(): pl.pallas_call(functools.partial(scan_forward, inner=inner, nstate=nstate...  48.7 us
    pallas_call x1, Pallas kernels, run_gating(): pl.pallas_call(functools.partial(gating, wg_pieces=wg_pieces, ow_pieces=o...  42 us
    pallas_call x1, Pallas kernels, run_input_back(): pl.pallas_call(functools.partial(input_back, count=len(dprojs), pieces=pi...  27.4 us
    pallas_call x1, Pallas kernels, run_project_in(): pl.pallas_call(functools.partial(project_in, pieces=pieces, order=order),...  24.2 us
  transfers between devices with their start and end apart: 57, of which 13 were waited for; matrix products, arithmetic and copies ran while one was open for 19% of the time, Pallas kernels for 40%

profile of v7, /device:TPU:0, one launch (start us, length us, event | category | flops | bytes accessed | tf_op | source)
XLA Modules:
  0.0 591.0 jit_solution(499392880041998204)
XLA Ops:
  21.1 8.9 %collective-permute-done.4.rest_2_.rest_5_ = bf16[864,384]{1,0:T(8,128)(2,1)} collective-permute-done((bf16[864,384]{1,0:T(8,128)(2,1)}, bf16[864,384]{1,0:T(8,128)(2,1)}, u32[]{:S(2)}, u32[]{:S(2)}) %collective-permute-start.4) | collective-permute-done | bytes 663584 | tf_op jit(solution)/shard_map/ppermute | solution.py:672
  31.5 12.2 %collective-permute-done.3.rest_1_.rest_4_ = bf16[864,384]{1,0:T(8,128)(2,1)} collective-permute-done((bf16[864,384]{1,0:T(8,128)(2,1)}, bf16[864,384]{1,0:T(8,128)(2,1)}, u32[]{:S(2)}, u32[]{:S(2)}) %collective-permute-start.3) | collective-permute-done | bytes 663584 | tf_op jit(solution)/shard_map/ppermute | solution.py:672
  50.1 10.4 %collective-permute-done.5.rest_3_.rest_6_ = bf16[864,384]{1,0:T(8,128)(2,1)} collective-permute-done((bf16[864,384]{1,0:T(8,128)(2,1)}, bf16[864,384]{1,0:T(8,128)(2,1)}, u32[]{:S(2)}, u32[]{:S(2)}) %collective-permute-start.5) | collective-permute-done | bytes 663584 | tf_op jit(solution)/shard_map/ppermute | solution.py:672
  65.3 24.2 %project_in.1 = (bf16[1024,1536]{1,0:T(8,128)(2,1)}, f32[1024,3456]{1,0:T(8,128)}) custom-call(s32[2]{0:T(128)S(1)} %pad_add_fusion.place_ref, bf16[1024,1536]{1,0:T(8,128)(2,1)} %bitcast.45, f32[1,1536]{1,0:T(1,128)S(1)} %bitcast.41, bf16[3456,384]{1,0:T(8,128)(2,1)} %pad.8.rest_0_.rest_3_, bf16[864,384]{1,0:T(8,128)(2,1)} %collective-permute-done.3.rest_1_.rest_4_, ...), custom_call_target="tpu_custom_call" | custom-call | flops 20000000000 | bytes 30000000 | tf_op jit(solution)/shard_map/project_in/pallas_call | solution.py:222
  93.8 48.7 %scan_forward.1 = (f32[1024,3072]{1,0:T(8,128)}, f32[1024,3328]{1,0:T(8,128)}, bf16[1024,3072]{1,0:T(8,128)(2,1)}) custom-call(f32[1024,3456]{1,0:T(8,128)} %get-tuple-element.91.proj_ref.tail_ref, f32[4,3328]{1,0:T(4,128)} %reshape.119.cw_ref.cwk_ref, f32[1,3328]{1,0:T(1,128)} %broadcast_in_dim_reshape.13.cb_ref, f32[8,128]{1,0:T(8,128)} %select_maximum_fusion.vec_ref, ...), custom_call_target="tpu_custom_call" | custom-call | flops 12000000000 | bytes 60000000 | tf_op jit(solution)/shard_map/scan_forward/pallas_call | solution.py:127
  143.1 6.0 %collective-permute-done.15.rest_4_ = bf16[1536,384]{1,0:T(8,128)(2,1)} collective-permute-done((bf16[1536,384]{1,0:T(8,128)(2,1)}, bf16[1536,384]{1,0:T(8,128)(2,1)}, u32[]{:S(2)}, u32[]{:S(2)}) %collective-permute-start.15) | collective-permute-done | bytes 1179680 | tf_op jit(solution)/shard_map/ppermute | solution.py:672
  150.7 42.0 %gating.1 = (bf16[1024,3072]{1,0:T(8,128)(2,1)}, f32[1024,3072]{1,0:T(8,128)}, bf16[1024,3072]{1,0:T(8,128)(2,1)}, f32[1,3072]{1,0:T(1,128)}) custom-call(s32[2]{0:T(128)} %copy-done.6, bf16[1024,1536]{1,0:T(8,128)(2,1)} %get-tuple-element.87.normed_ref, bf16[1024,1536]{1,0:T(8,128)(2,1)} %bitcast.55, f32[1024,3072]{1,0:T(8,128)} %get-tuple-element.92.scan_ref.out_ref, ...), custom_call_target="tpu_custom_call" | custom-call | flops 40000000000 | bytes 70000000 | tf_op jit(solution)/shard_map/gating/pallas_call | solution.py:305
  192.8 7.8 %convolution_convert_fusion = bf16[1536,1536]{1,0:T(8,128)(2,1)S(1)} fusion(bf16[1024,3072]{1,0:T(8,128)(2,1)} %get-tuple-element.140.mixed_ref, bf16[1,1024,1536]{2,1,0:T(8,128)(2,1)} %param.21), kind=kOutput, calls=%fused_computation.1 | convolution fusion | flops 4834197504 | bytes 11010048 | tf_op jit(solution)/shard_map/dot_general | solution.py:814
  200.8 8.7 %convolution_convert_fusion.2 = bf16[3072,768]{1,0:T(8,128)(2,1)S(1)} fusion(bf16[1024,3072]{1,0:T(8,128)(2,1)} %get-tuple-element.128.dgate_ref, bf16[1024,1536]{1,0:T(8,128)(2,1)S(1)} %copy-done.38), kind=kOutput, calls=%fused_computation.7 | convolution fusion | flops 4834197504 | bytes 12582912 | tf_op jit(solution)/shard_map/dot_general | solution.py:814
  210.0 7.7 %convolution_convert_fusion.1 = bf16[1536,1536]{1,0:T(8,128)(2,1)S(1)} fusion(bf16[1024,3072]{1,0:T(8,128)(2,1)} %get-tuple-element.140.mixed_ref, bf16[1,1024,1536]{2,1,0:T(8,128)(2,1)S(1)} %copy-done.37), kind=kOutput, calls=%fused_computation.2 | convolution fusion | flops 4834197504 | bytes 11010048 | tf_op jit(solution)/shard_map/dot_general | solution.py:814
  221.8 8.5 %convolution_convert_fusion.3 = bf16[3072,768]{1,0:T(8,128)(2,1)S(1)} fusion(bf16[1024,3072]{1,0:T(8,128)(2,1)} %get-tuple-element.128.dgate_ref, bf16[1024,1536]{1,0:T(8,128)(2,1)S(1)} %copy-done.38), kind=kOutput, calls=%fused_computation.8 | convolution fusion | flops 4834197504 | bytes 12582912 | tf_op jit(solution)/shard_map/dot_general | solution.py:814
  233.9 31.4 %scan_backward.3 = (bf16[1024,1024]{1,0:T(8,128)(2,1)}, f32[4,1024]{1,0:T(4,128)S(1)}, f32[1,1024]{1,0:T(1,128)S(1)}, f32[1,1024]{1,0:T(1,128)S(1)}, f32[8,128]{...) custom-call(f32[1024,3456]{1,0:T(8,128)} %get-tuple-element.91.proj_ref.tail_ref, ...), custom_call_target="tpu_custom_call" | custom-call | flops 40000000000 | bytes 40000000 | tf_op jit(solution)/shard_map/scan_backward/pallas_call | solution.py:636
  265.4 5.5 convolution_convert_fusion.8
  272.7 5.0 convolution_convert_fusion.9
  284.0 31.5 %scan_backward.4 = (bf16[1024,1024]{1,0:T(8,128)(2,1)}, f32[4,1024]{1,0:T(4,128)S(1)}, f32[1,1024]{1,0:T(1,128)S(1)}, f32[1,1024]{1,0:T(1,128)S(1)}, f32[8,128]{...) custom-call(f32[1024,3456]{1,0:T(8,128)} %get-tuple-element.91.proj_ref.tail_ref, ...), custom_call_target="tpu_custom_call" | custom-call | flops 40000000000 | bytes 40000000 | tf_op jit(solution)/shard_map/scan_backward/pallas_call | solution.py:636
  333.0 5.1 add_convert_fusion.2
  341.6 34.0 %scan_backward.5 = (bf16[1024,1408]{1,0:T(8,128)(2,1)}, f32[4,1280]{1,0:T(4,128)S(1)}, f32[1,1280]{1,0:T(1,128)S(1)}, f32[1,1024]{1,0:T(1,128)S(1)}, f32[8,128]{1,0:T(8,128)S(1)}) custom-call(f32[1024,3456]{1,0:T(8,128)} %get-tuple-element.91.proj_ref.tail_ref, f32[1024,3456]{1,0:T(8,128)} %get-tuple-element.91.proj_ref.tail_ref, ...), custom_call_target="tpu_custom_call" | custom-call | flops 40000000000 | bytes 40000000 | tf_op jit(solution)/shard_map/scan_backward/pallas_call | solution.py:636
  379.2 5.8 convolution_convert_fusion.4
  393.9 4.7 convolution_convert_fusion.5
  400.8 20.5 %gate_back.1.part_ref = f32[1024,1536]{1,0:T(8,128)} custom-call(s32[2]{0:T(128)S(1)} %copy-done.7, bf16[1024,3072]{1,0:T(8,128)(2,1)} %get-tuple-element.128.dgate_ref, bf16[3072,384]{1,0:T(8,128)(2,1)S(1)} %copy-done.1, bf16[1536,384]{1,0:T(8,128)(2,1)} %collective-permute-done.12.rest_1_, bf16[1536,384]{1,0:T(8,128)(2,1)} %collective-permute-done.13.rest_2_, ...), custom_call_target="tpu_custom_call" | custom-call | flops 16000000000 | bytes 22000000 | tf_op jit(solution)/shard_map/gate_back/pallas_call | solution.py:344
  437.1 27.4 %input_back.1 = (f32[1024,1536]{1,0:T(8,128)}, f32[1,1536]{1,0:T(1,128)S(1)}) custom-call(s32[2]{0:T(128)S(1)} %copy-done.7, f32[1024,1536]{1,0:T(8,128)} %gate_back.1.part_ref, bf16[1024,1536]{1,0:T(8,128)(2,1)} %bitcast.46, bf16[1024,1536]{1,0:T(8,128)(2,1)} %bitcast.56, f32[1,1536]{1,0:T(1,128)S(1)} %bitcast.42, ...), custom_call_target="tpu_custom_call" | custom-call | flops 22000001024 | bytes 46000000 | tf_op jit(solution)/shard_map/input_back/pallas_call | solution.py:400
  478.9 20.8 %project_out.1 = bf16[1024,1536]{1,0:T(8,128)(2,1)} custom-call(s32[2]{0:T(128)S(1)} %copy-done.7, bf16[1024,3072]{1,0:T(8,128)(2,1)} %get-tuple-element.140.mixed_ref, bf16[1024,1536]{1,0:T(8,128)(2,1)S(1)} %bitcast.47, bf16[768,1536]{1,0:T(8,128)(2,1)} %rest_0_.1, bf16[768,1536]{1,0:T(8,128)(2,1)} %collective-permute-done.17.rest_7_.rest_1_, ...), custom_call_target="tpu_custom_call" | custom-call | flops 14000000000 | bytes 20000000 | tf_op jit(solution)/shard_map/project_out/pallas_call | solution.py:435
  520.0 17.4 %collective-permute-done.48 = f32[4,5348]{1,0:T(4,128)S(1)} collective-permute-done((f32[4,5348]{1,0:T(4,128)S(1)}, f32[4,5348]{1,0:T(4,128)S(1)}, u32[]{:S(2)}, u32[]{:S(2)}) %collective-permute-start.48) | collective-permute-done | bytes 85600 | tf_op jit(solution)/shard_map/ppermute | solution.py:672
  560.1 24.6 %collective-permute-done.54 = bf16[1728,384]{1,0:T(8,128)(2,1)} collective-permute-done((bf16[1728,384]{1,0:T(8,128)(2,1)}, bf16[1728,384]{1,0:T(8,128)(2,1)}, u32[]{:S(2)}, u32[]{:S(2)}) %collective-permute-start.54) | collective-permute-done | bytes 1327136 | tf_op jit(solution)/shard_map/ppermute | solution.py:672
  (294 shorter events, 170.2 us)
Async XLA Ops:
  12.0 31.8 %collective-permute-start.3 = (bf16[864,384]{1,0:T(8,128)(2,1)}, bf16[864,384]{1,0:T(8,128)(2,1)}, u32[]{:S(2)}, u32[]{:S(2)}) collective-permute-start(bf16[864,384]{1,0:T(8,128)(2,1)} %get-tuple-element.189), channel_id=1, source_target_pairs={{0,16},{8,24},{16,0},{24,8},{1,17},{9,25},{17,1},{25,9},{2,18},{10... | collective-permute-start | bytes 1990664 | tf_op jit(solution)/shard_map/ppermute | solution.py:672
  15.7 47.5 %collective-permute-start.7 = (bf16[3456,384]{1,0:T(8,128)(2,1)}, bf16[3456,384]{1,0:T(8,128)(2,1)}, u32[]{:S(2)}, u32[]{:S(2)}) collective-permute-start(bf16[3456,384]{1,0:T(8,128)(2,1)} %pad.8.rest_0_.rest_3_), channel_id=1, source_target_pairs={{0,8},{8,0},{16,24},{24,16},{1,9},{9,1},{17,25},{25,17},{2,10},{10... | collective-permute-start | bytes 7962632 | tf_op jit(solution)/shard_map/ppermute | solution.py:672
  62.6 80.5 %collective-permute-start.14 = (bf16[3072,384]{1,0:T(8,128)(2,1)S(1)}, bf16[3072,384]{1,0:T(8,128)(2,1)}, u32[]{:S(2)}, u32[]{:S(2)}) collective-permute-start(bf16[3072,384]{1,0:T(8,128)(2,1)S(1)} %slice.121.rest_0_), channel_id=1, source_target_pairs={{0,8},{8,0},{16,24},{24,16},{1,9},{9,1},{17,25},{25,17},{2,10},{10... | collective-permute-start | bytes 7077896 | tf_op jit(solution)/shard_map/ppermute | solution.py:672
  63.2 79.9 %collective-permute-start.18 = (bf16[768,1536]{1,0:T(8,128)(2,1)}, bf16[768,1536]{1,0:T(8,128)(2,1)}, u32[]{:S(2)}, u32[]{:S(2)}) collective-permute-start(bf16[768,1536]{1,0:T(8,128)(2,1)} %rest_0_.1), channel_id=1, source_target_pairs={{0,8},{8,0},{16,24},{24,16},{1,9},{9,1},{17,25},{25,17},{2,10},{10... | collective-permute-start | bytes 7077896 | tf_op jit(solution)/shard_map/ppermute | solution.py:672
  63.8 78.7 %collective-permute-start.17 = (bf16[768,1536]{1,0:T(8,128)(2,1)}, bf16[768,1536]{1,0:T(8,128)(2,1)}, u32[]{:S(2)}, u32[]{:S(2)}) collective-permute-start(bf16[768,1536]{1,0:T(8,128)(2,1)} %rest_0_.1), channel_id=1, source_target_pairs={{0,16},{8,24},{16,0},{24,8},{1,17},{9,25},{17,1},{25,9},{2,18},{10... | collective-permute-start | bytes 7077896 | tf_op jit(solution)/shard_map/ppermute | solution.py:672
  92.2 50.8 %collective-permute-start.13 = (bf16[1536,384]{1,0:T(8,128)(2,1)}, bf16[1536,384]{1,0:T(8,128)(2,1)}, u32[]{:S(2)}, u32[]{:S(2)}) collective-permute-start(bf16[1536,384]{1,0:T(8,128)(2,1)} %collective-permute-done.12.rest_1_), channel_id=1, source_target_pairs={{0,1},{1,0},{2,3},{3,2},{4,5},{5,4},{6,7},{7,6},{8,9},{9,8},{10,11... | collective-permute-start | bytes 3538952 | tf_op jit(solution)/shard_map/ppermute | solution.py:672
  221.3 56.4 %collective-permute-start.23 = (bf16[768,1536]{1,0:T(8,128)(2,1)}, bf16[768,1536]{1,0:T(8,128)(2,1)}, u32[]{:S(2)}, u32[]{:S(2)}) collective-permute-start(bf16[768,1536]{1,0:T(8,128)(2,1)} %get-tuple-element.166), channel_id=1, source_target_pairs={{0,16},{8,24},{16,0},{24,8},{1,17},{9,25},{17,1},{25,9},{2,18},{10... | collective-permute-start | bytes 7077896 | tf_op jit(solution)/shard_map/ppermute | solution.py:672
  271.1 56.1 %collective-permute-start.25 = (bf16[3072,384]{1,0:T(8,128)(2,1)}, bf16[3072,384]{1,0:T(8,128)(2,1)}, u32[]{:S(2)}, u32[]{:S(2)}) collective-permute-start(bf16[3072,384]{1,0:T(8,128)(2,1)} %get-tuple-element.164), channel_id=1, source_target_pairs={{0,16},{8,24},{16,0},{24,8},{1,17},{9,25},{17,1},{25,9},{2,18},{10... | collective-permute-start | bytes 7077896 | tf_op jit(solution)/shard_map/ppermute | solution.py:672
  281.6 33.9 %collective-permute-start.24 = (bf16[384,1536]{1,0:T(8,128)(2,1)S(1)}, bf16[384,1536]{1,0:T(8,128)(2,1)S(1)}, u32[]{:S(2)}, u32[]{:S(2)}) collective-permute-start(bf16[384,1536]{1,0:T(8,128)(2,1)S(1)} %get-tuple-element.172), channel_id=1, source_target_pairs={{0,1},{1,0},{2,3},{3,2},{4,5},{5,4},{6,7},{7,6},{8,9},{9,8},{10,11... | collective-permute-start | bytes 3538952 | tf_op jit(solution)/shard_map/ppermute | solution.py:672
  322.7 53.9 %collective-permute-start.29 = (bf16[96,1536]{1,0:T(8,128)(2,1)}, bf16[96,1536]{1,0:T(8,128)(2,1)S(1)}, u32[]{:S(2)}, u32[]{:S(2)}) collective-permute-start(bf16[96,1536]{1,0:T(8,128)(2,1)} %get-tuple-element.185), channel_id=1, source_target_pairs={{0,2},{1,3},{2,0},{3,1},{4,6},{5,7},{6,4},{7,5},{8,10},{9,11},{10,... | collective-permute-start | bytes 884744 | tf_op jit(solution)/shard_map/ppermute | solution.py:672
  324.4 52.4 %collective-permute-start.30 = (bf16[96,1536]{1,0:T(8,128)(2,1)}, bf16[96,1536]{1,0:T(8,128)(2,1)S(1)}, u32[]{:S(2)}, u32[]{:S(2)}) collective-permute-start(bf16[96,1536]{1,0:T(8,128)(2,1)} %get-tuple-element.184), channel_id=1, source_target_pairs={{0,4},{1,5},{2,6},{3,7},{4,0},{5,1},{6,2},{7,3},{8,12},{9,13},{10,... | collective-permute-start | bytes 884744 | tf_op jit(solution)/shard_map/ppermute | solution.py:672
  327.0 49.8 %collective-permute-start.31 = (bf16[96,1536]{1,0:T(8,128)(2,1)}, bf16[96,1536]{1,0:T(8,128)(2,1)S(1)}, u32[]{:S(2)}, u32[]{:S(2)}) collective-permute-start(bf16[96,1536]{1,0:T(8,128)(2,1)} %get-tuple-element.183), channel_id=1, source_target_pairs={{0,6},{1,7},{2,4},{3,5},{4,2},{5,3},{6,0},{7,1},{8,14},{9,15},{10,... | collective-permute-start | bytes 884744 | tf_op jit(solution)/shard_map/ppermute | solution.py:672
  340.3 35.4 %collective-permute-start.28 = (bf16[1536,384]{1,0:T(8,128)(2,1)S(1)}, bf16[1536,384]{1,0:T(8,128)(2,1)S(1)}, u32[]{:S(2)}, u32[]{:S(2)}) collective-permute-start(bf16[1536,384]{1,0:T(8,128)(2,1)S(1)} %get-tuple-element.170), channel_id=1, source_target_pairs={{0,1},{1,0},{2,3},{3,2},{4,5},{5,4},{6,7},{7,6},{8,9},{9,8},{10,11... | collective-permute-start | bytes 3538952 | tf_op jit(solution)/shard_map/ppermute | solution.py:672
  341.1 35.7 %collective-permute-start.27 = (bf16[2048,384]{1,0:T(8,128)(2,1)S(1)}, bf16[2048,384]{1,0:T(8,128)(2,1)S(1)}, u32[]{:S(2)}, u32[]{:S(2)}) collective-permute-start(bf16[2048,384]{1,0:T(8,128)(2,1)S(1)} %get-tuple-element.173), channel_id=1, source_target_pairs={{0,16},{8,24},{16,0},{24,8},{1,17},{9,25},{17,1},{25,9},{2,18},{10... | collective-permute-start | bytes 4718600 | tf_op jit(solution)/shard_map/ppermute | solution.py:672
  389.2 32.2 %collective-permute-start.34 = (bf16[384,384]{1,0:T(8,128)(2,1)}, bf16[384,384]{1,0:T(8,128)(2,1)S(1)}, u32[]{:S(2)}, u32[]{:S(2)}) collective-permute-start(bf16[384,384]{1,0:T(8,128)(2,1)} %get-tuple-element.182), channel_id=1, source_target_pairs={{0,2},{1,3},{2,0},{3,1},{4,6},{5,7},{6,4},{7,5},{8,10},{9,11},{10,... | collective-permute-start | bytes 884744 | tf_op jit(solution)/shard_map/ppermute | solution.py:672
  390.1 31.3 %collective-permute-start.35 = (bf16[384,384]{1,0:T(8,128)(2,1)}, bf16[384,384]{1,0:T(8,128)(2,1)S(1)}, u32[]{:S(2)}, u32[]{:S(2)}) collective-permute-start(bf16[384,384]{1,0:T(8,128)(2,1)} %get-tuple-element.181), channel_id=1, source_target_pairs={{0,4},{1,5},{2,6},{3,7},{4,0},{5,1},{6,2},{7,3},{8,12},{9,13},{10,... | collective-permute-start | bytes 884744 | tf_op jit(solution)/shard_map/ppermute | solution.py:672
  393.5 40.6 %collective-permute-start.38 = (bf16[96,1536]{1,0:T(8,128)(2,1)S(1)}, bf16[96,1536]{1,0:T(8,128)(2,1)S(1)}, u32[]{:S(2)}, u32[]{:S(2)}) collective-permute-start(bf16[96,1536]{1,0:T(8,128)(2,1)S(1)} %add_convert_fusion.11), channel_id=1, source_target_pairs={{0,2},{1,3},{2,0},{3,1},{4,6},{5,7},{6,4},{7,5},{8,10},{9,11},{10,... | collective-permute-start | bytes 884744 | tf_op jit(solution)/shard_map/ppermute | solution.py:672
  399.2 29.6 %collective-permute-start.33 = (bf16[1408,384]{1,0:T(8,128)(2,1)S(1)}, bf16[1408,384]{1,0:T(8,128)(2,1)S(1)}, u32[]{:S(2)}, u32[]{:S(2)}) collective-permute-start(bf16[1408,384]{1,0:T(8,128)(2,1)S(1)} %get-tuple-element.175), channel_id=1, source_target_pairs={{0,16},{8,24},{16,0},{24,8},{1,17},{9,25},{17,1},{25,9},{2,18},{10... | collective-permute-start | bytes 3244040 | tf_op jit(solution)/shard_map/ppermute | solution.py:672
  423.5 41.2 %collective-permute-start.39 = (bf16[384,384]{1,0:T(8,128)(2,1)}, bf16[384,384]{1,0:T(8,128)(2,1)}, u32[]{:S(2)}, u32[]{:S(2)}) collective-permute-start(bf16[384,384]{1,0:T(8,128)(2,1)} %add_convert_fusion.10), channel_id=1, source_target_pairs={{0,2},{1,3},{2,0},{3,1},{4,6},{5,7},{6,4},{7,5},{8,10},{9,11},{10,... | collective-permute-start | bytes 884744 | tf_op jit(solution)/shard_map/ppermute | solution.py:672
  425.2 39.5 %collective-permute-start.40 = (bf16[384,384]{1,0:T(8,128)(2,1)}, bf16[384,384]{1,0:T(8,128)(2,1)}, u32[]{:S(2)}, u32[]{:S(2)}) collective-permute-start(bf16[384,384]{1,0:T(8,128)(2,1)} %add_convert_fusion.10), channel_id=1, source_target_pairs={{0,4},{1,5},{2,6},{3,7},{4,0},{5,1},{6,2},{7,3},{8,12},{9,13},{10,... | collective-permute-start | bytes 884744 | tf_op jit(solution)/shard_map/ppermute | solution.py:672
  427.4 37.3 %collective-permute-start.41 = (bf16[384,384]{1,0:T(8,128)(2,1)}, bf16[384,384]{1,0:T(8,128)(2,1)}, u32[]{:S(2)}, u32[]{:S(2)}) collective-permute-start(bf16[384,384]{1,0:T(8,128)(2,1)} %add_convert_fusion.10), channel_id=1, source_target_pairs={{0,6},{1,7},{2,4},{3,5},{4,2},{5,3},{6,0},{7,1},{8,14},{9,15},{10,... | collective-permute-start | bytes 884744 | tf_op jit(solution)/shard_map/ppermute | solution.py:672
  432.9 31.8 %collective-permute-start.37 = (bf16[1728,384]{1,0:T(8,128)(2,1)}, bf16[1728,384]{1,0:T(8,128)(2,1)}, u32[]{:S(2)}, u32[]{:S(2)}) collective-permute-start(bf16[1728,384]{1,0:T(8,128)(2,1)} %get-tuple-element.167), channel_id=1, source_target_pairs={{0,1},{1,0},{2,3},{3,2},{4,5},{5,4},{6,7},{7,6},{8,9},{9,8},{10,11... | collective-permute-start | bytes 3981320 | tf_op jit(solution)/shard_map/ppermute | solution.py:672
  435.1 64.7 %collective-permute-start.55 = (bf16[192,1536]{1,0:T(8,128)(2,1)}, bf16[192,1536]{1,0:T(8,128)(2,1)}, u32[]{:S(2)}, u32[]{:S(2)}) collective-permute-start(bf16[192,1536]{1,0:T(8,128)(2,1)} %pad_maximum_fusion.9), channel_id=1, source_target_pairs={{0,4},{1,5},{2,6},{3,7},{4,0},{5,1},{6,2},{7,3},{8,12},{9,13},{10,... | collective-permute-start | bytes 1769480 | tf_op jit(solution)/shard_map/ppermute | solution.py:672
  507.2 38.9 %collective-permute-start.56 = (bf16[384,1536]{1,0:T(8,128)(2,1)}, bf16[384,1536]{1,0:T(8,128)(2,1)}, u32[]{:S(2)}, u32[]{:S(2)}) collective-permute-start(bf16[384,1536]{1,0:T(8,128)(2,1)} %pad_maximum_fusion.8), channel_id=1, source_target_pairs={{0,1},{1,0},{2,3},{3,2},{4,5},{5,4},{6,7},{7,6},{8,9},{9,8},{10,11... | collective-permute-start | bytes 3538952 | tf_op jit(solution)/shard_map/ppermute | solution.py:672
  (76 other events, 951.1 us)
